TPU v7x, 256 devices: a whole 4x4x8 slice. The times are simulated.
256 devices in a mesh: dp: 4 (over y), cp: 64 (over x, z, core).
Axes of the slice: x: 4, y: 4, z: 8, core: 2. Of those that a mesh axis runs over, the one named last changes fastest.
Arguments:
- query_rows: bfloat16 [32768, 4096], P(('dp', 'cp')), parts along dimension 0, may hold values from -90 to 90
- key_rows: bfloat16 [32768, 512], P(('dp', 'cp')), parts along dimension 0, may hold values from -5 to 5
- value_rows: bfloat16 [32768, 512], P(('dp', 'cp')), parts along dimension 0, may hold values from -6 to 6
- gate_rows: bfloat16 [32768, 4096], P(('dp', 'cp')), parts along dimension 0, may hold values from -6 to 6
- doc_ids: int32 [32768], P(('dp', 'cp')), parts along dimension 0, may hold values from 0 to 15, never falling along the last dimension, each value on 1 to 4096 neighbouring positions
- block_lists: int32 [256, 64], P(('dp', 'cp')), parts along dimension 0, may hold values from 0 to 1, as said below
Outputs:
- gated_attention: bfloat16 [32768, 4096], P(('dp', 'cp')), parts along dimension 0
There are 4 independent parts, one for each index of `dp`. A program takes and returns all parts, laid end to end along the dimension named above; each array names one. Nothing has to cross between parts.
Inputs may be any that keep to these rules, and one draw needn't show every extreme that they name: `block_lists`: row q has a 1 at column q and only zeros at columns above q.
All inputs are finite; a program needn't handle non-finite values.
Results may differ from a plain program's by a relative error of at most 0.0038.
Values may be sent and summed in bfloat16 or wider, within the bound.
No kernel may reach another device: no remote copies, remote signals or barrier semaphores. Data moves between devices by JAX's collectives and lax.ppermute only.
A program may use at most 128 MiB of HBM per device.

v0:
```python
import math

import jax
import jax.numpy as jnp
from jax import lax
from jax.sharding import PartitionSpec as P

H = 16
KVH = 2
HD = 256
BLK = 128


def pick_size(length):
    for candidate in (2048, 1024, 512, 256, 128):
        return candidate
    return length


def make_fold(query_rows, positions, query_docs, all_docs, all_lists):
    total_rows = query_rows.shape[0]
    num_blocks = all_lists.shape[0]
    seq_rows = all_docs.shape[0]
    groups = H // KVH
    scale_factor = 1.0 / math.sqrt(HD)
    grouped = query_rows.reshape(total_rows, KVH, groups, HD)
    block_range = jnp.arange(num_blocks, dtype=jnp.int32)
    selector = ((positions // BLK)[:, None] == block_range[None, :]).astype(jnp.bfloat16)
    row_lists = jnp.dot(
        selector, all_lists.astype(jnp.bfloat16), preferred_element_type=jnp.float32
    ).astype(jnp.bfloat16)
    padded_lists = jnp.concatenate(
        [jnp.zeros((total_rows, num_blocks), jnp.bfloat16), row_lists], axis=1
    )
    padded_docs = jnp.concatenate([jnp.full((seq_rows,), -1, jnp.int32), all_docs], axis=0)

    def update(state, key_block, value_block, block_start):
        width = key_block.shape[0]
        key_pos = block_start + jnp.arange(width, dtype=jnp.int32)
        key_docs = lax.dynamic_slice_in_dim(padded_docs, block_start + seq_rows, width)
        block_count = width // BLK
        listed_blocks = lax.dynamic_slice_in_dim(
            padded_lists, block_start // BLK + num_blocks, block_count, 1
        )
        listed = jnp.repeat(listed_blocks, BLK, axis=1)
        visible = (
            (key_pos[None, :] >= 0)
            & (key_pos[None, :] <= positions[:, None])
            & (key_docs[None, :] == query_docs[:, None])
            & (listed > 0.5)
        )

        def compute(inner):
            running_max, running_sum, weighted = inner
            scores = (
                jnp.einsum(
                    "rkgd,nkd->kgrn",
                    grouped,
                    key_block.reshape(width, KVH, HD),
                    preferred_element_type=jnp.float32,
                )
                * scale_factor
            )
            scores = jnp.where(visible[None, None], scores, -1e30)
            new_max = jnp.maximum(running_max, jnp.max(scores, axis=-1))
            weights = jnp.where(visible[None, None], jnp.exp(scores - new_max[..., None]), 0.0)
            decay = jnp.exp(running_max - new_max)
            new_sum = decay * running_sum + jnp.sum(weights, axis=-1)
            product = jnp.einsum(
                "kgrn,nkd->kgrd",
                weights.astype(jnp.bfloat16),
                value_block.reshape(width, KVH, HD),
                preferred_element_type=jnp.float32,
            )
            return (new_max, new_sum, decay[..., None] * weighted + product)

        return lax.cond(jnp.any(visible), compute, lambda inner: inner, state)

    def fold(state, piece, start):
        key_piece, value_piece = piece
        length = key_piece.shape[0]
        step_size = pick_size(length)
        count = length // step_size
        key_steps = key_piece.reshape(count, step_size, key_piece.shape[1])
        value_steps = value_piece.reshape(count, step_size, value_piece.shape[1])
        starts = step_size * jnp.arange(count, dtype=jnp.int32)

        def advance(inner, inputs):
            return (update(inner, inputs[0], inputs[1], inputs[2]), None)

        state, _ = lax.scan(advance, state, (key_steps, value_steps, starts))
        return state

    initial = (
        jnp.full((KVH, groups, total_rows), -1e30, jnp.float32),
        jnp.zeros((KVH, groups, total_rows), jnp.float32),
        jnp.zeros((KVH, groups, total_rows, HD), jnp.float32),
    )
    return (fold, initial)


def finish(state, total_rows):
    running_max, running_sum, weighted = state
    result = weighted / running_sum[..., None]
    return jnp.transpose(result, (2, 0, 1, 3)).reshape(total_rows, H * HD)


def fold_all(fold, initial, key_rows, value_rows):
    return fold(
        initial,
        (
            lax.all_gather(key_rows, "cp", axis=0, tiled=True),
            lax.all_gather(value_rows, "cp", axis=0, tiled=True),
        ),
        jnp.int32(0),
    )


def on_device(query_rows, key_rows, value_rows, gate_rows, doc_ids, block_lists):
    rows_here = query_rows.shape[0]
    position = lax.axis_index("cp")
    all_docs, all_lists = (
        lax.all_gather(doc_ids, "cp", axis=0, tiled=True),
        lax.all_gather(block_lists, "cp", axis=0, tiled=True),
    )
    first_row = position * rows_here
    positions = first_row + jnp.arange(rows_here, dtype=jnp.int32)
    fold, initial = make_fold(query_rows, positions, doc_ids, all_docs, all_lists)
    state = fold_all(fold, initial, key_rows, value_rows)
    attended = finish(state, rows_here)
    gated = (attended * jax.nn.sigmoid(gate_rows.astype(jnp.float32))).astype(jnp.bfloat16)
    return gated


def solution(mesh):
    return jax.shard_map(
        on_device,
        mesh=mesh,
        in_specs=(
            P(("dp", "cp"), None),
            P(("dp", "cp"), None),
            P(("dp", "cp"), None),
            P(("dp", "cp"), None),
            P(("dp", "cp")),
            P(("dp", "cp"), None),
        ),
        out_specs=P(("dp", "cp"), None),
        check_vma=False,
    )
```

profile of v0, /device:TPU:15, one launch (start us, length us, event | category | flops | bytes accessed | tf_op | source)
XLA Modules:
  0.0 298.1 jit_solution(7128368392556407107)
XLA Ops:
  6.5 0.7 all-gather.5.cloned.1.call-update
  7.3 0.7 all-gather.7.cloned.1.call-update
  8.0 1.6 copy.41
  9.6 1.3 copy.43
  11.0 41.3 %all-gather.1 = s32[64,1,64]{2,1,0:T(1,128)S(1)} all-gather(s32[1,1,64]{2,1,0:T(1,128)S(1)} %bitcast.63), channel_id=1, replica_groups=mesh['dp'=4,'cp'=64] {'cp'}, dimensions={0}, use_global_device_ids=true | all-gather | bytes 16640 | tf_op jit(solution)/shard_map/all_gather | solution.py:124
  52.6 37.3 %all-gather = s32[64,1,128]{2,1,0:T(1,128)S(1)} all-gather(s32[1,1,128]{2,1,0:T(1,128)S(1)} %bitcast.61), channel_id=1, replica_groups=mesh['dp'=4,'cp'=64] {'cp'}, dimensions={0}, use_global_device_ids=true | all-gather | bytes 33280 | tf_op jit(solution)/shard_map/all_gather | solution.py:123
  89.9 4.7 %all-gather.5.cloned.1.call-done = bf16[8192,512]{1,0:T(8,128)(2,1)} async-done(((bf16[128,512]{1,0:T(8,128)(2,1)}), bf16[8192,512]{1,0:T(8,128)(2,1)}) %all-gather.5.cloned.1.call-update) | async-done | bytes 8388624 | tf_op jit(solution)/shard_map/all_gather | solution.py:112
  94.6 11.5 %copy.42 = bf16[4,2048,512]{1,2,0:T(8,128)(2,1)} copy(bf16[4,2048,512]{2,1,0:T(8,128)(2,1)} %bitcast.54) | data formatting | bytes 16777216
  106.1 71.6 %all-gather.7.cloned.1.call-done = bf16[8192,512]{1,0:T(8,128)(2,1)} async-done(((bf16[128,512]{1,0:T(8,128)(2,1)}), bf16[8192,512]{1,0:T(8,128)(2,1)}) %all-gather.7.cloned.1.call-update) | async-done | bytes 8388624 | tf_op jit(solution)/shard_map/all_gather | solution.py:113
  177.8 11.4 %copy.44 = bf16[4,2048,512]{1,2,0:T(8,128)(2,1)} copy(bf16[4,2048,512]{2,1,0:T(8,128)(2,1)} %bitcast.55) | data formatting | bytes 16777216
  189.2 1.6 broadcast_in_dim.58
  190.8 96.7 %while.17 = (s32[]{:T(128)}, f32[2,8,128]{2,1,0:T(8,128)S(1)}, f32[2,8,128]{2,1,0:T(8,128)S(1)}, f32[2,8,128,256]{3,2,1,0:T(8,128)}, s32[4]{0:T(128)S(1)}, /*ind...) while((s32[]{:T(128)}, f32[2,8,128]{2,1,0:T(8,128)S(1)}, ...), condition=%wide.region_6.7_spmd.clone, body=%wide.region_0.6_spmd.clone.sunk | while | flops 4353456128 | bytes 73665688 | solution.py:91
  195.8 0.7 add_add_fusion.2
  196.5 0.7 broadcast_compare_fusion.6
  197.2 1.4 and_reduce_fusion.2
  199.3 0.7 dynamic_slice.50
  204.3 0.7 add_add_fusion.2
  205.0 0.7 broadcast_compare_fusion.6
  205.7 1.4 and_reduce_fusion.2
  207.8 20.9 %conditional.3 = ((f32[2,8,128]{2,1,0:T(8,128)S(1)}, f32[2,8,128]{2,1,0:T(8,128)S(1)}, f32[2,8,128,256]{3,2,1,0:T(8,128)})) conditional(s32[]{:T(128)} %convert_element_type.42, (f32[2,8,128]{2,1,0:T(8,128)S(1)}, f32[2,8,128]{2,1,0:T(8,128)S(1)}, f32[2,8,128,256]{3,2,1,0:T(8,128)}) %tuple.57, (s32[]{:T(128)}, s32[1,2048]{1,0:T(1,128)S(1)}, ...), branch_computations={%region_2.2_spmd, %region_3.5_spmd} | conditional | flops 4351862784 | bytes 73577536 | solution.py:77
  207.8 0.7 compare_reduce_fusion
  208.5 1.8 bitcast_and_fusion
  210.3 2.7 constant_dynamic-slice_fusion
  213.1 4.0 %fusion.2 = (f32[2,8,128]{2,1,0:T(8,128)S(1)}, f32[2,2048,128,8]{2,1,3,0:T(8,128)S(1)}) fusion(pred[128,2048]{0,1:T(8,128)(4,1)S(1)} %bitcast_and_fusion, bf16[2048,2,256,1]{0,2,3,1:T(8,128)(2,1)S(1)} %bitcast.53, bf16[128,2,8,256]{3,0,2,1:T(8,128)(2,1)S(1)} %copy-done), kind=kOutput, calls=%fused_computation.3 | convolution fusion | flops 2160064512 | bytes 20193280 | tf_op jit(solution)/shard_map/while/body/eval_jaxpr/cond/branch_1_fun/rkgd,nkd->kgrn/dot_general | solution.py:56
  217.0 4.0 %fusion.4 = f32[2,8,128]{2,1,0:T(8,128)S(1)} fusion(f32[2,2048,128,8]{2,1,3,0:T(8,128)S(1)} %get-tuple-element.413, f32[2,8,128]{2,1,0:T(8,128)S(1)} %max.4, pred[128,2048]{0,1:T(8,128)(4,1)S(1)} %bitcast_and_fusion), kind=kLoop, calls=%fused_computation.5 | loop fusion | flops 20969472 | bytes 17055744 | tf_op jit(solution)/shard_map/while/body/eval_jaxpr/cond/branch_1_fun/reduce_sum | solution.py:68
  221.0 7.6 %multiply_add_fusion = f32[2,8,128,256]{3,2,1,0:T(8,128)} fusion(f32[2,8,128,256]{3,2,1,0:T(8,128)} %get-tuple-element.282, bf16[2048,2,256,1]{0,2,3,1:T(8,128)(2,1)S(1)} %bitcast.52, f32[2,2048,128,8]{2,1,3,0:T(8,128)S(1)} %get-tuple-element.413, f32[2,8,128]{2,1,0:T(8,128)S(1)} %max.4, pred[128,2048]{0,1:T(8,128)(4,1)S(1)} %bitcast_and_fusion, ...), kind=kOutput, calls=%fused_computation.8 | convolution fusion | flops 2169503744 | bytes 23347200 | tf_op jit(solution)/shard_map/while/body/eval_jaxpr/cond/branch_1_fun/kgrn,nkd->kgrd/dot_general | solution.py:69
  233.7 0.7 add_add_fusion.2
  234.4 0.7 broadcast_compare_fusion.6
  235.1 1.4 and_reduce_fusion.2
  237.2 20.9 %conditional.3 = ((f32[2,8,128]{2,1,0:T(8,128)S(1)}, f32[2,8,128]{2,1,0:T(8,128)S(1)}, f32[2,8,128,256]{3,2,1,0:T(8,128)})) conditional(s32[]{:T(128)} %convert_element_type.42, (f32[2,8,128]{2,1,0:T(8,128)S(1)}, f32[2,8,128]{2,1,0:T(8,128)S(1)}, f32[2,8,128,256]{3,2,1,0:T(8,128)}) %tuple.57, (s32[]{:T(128)}, s32[1,2048]{1,0:T(1,128)S(1)}, ...), branch_computations={%region_2.2_spmd, %region_3.5_spmd} | conditional | flops 4351862784 | bytes 73577536 | solution.py:77
  237.2 0.7 compare_reduce_fusion
  237.9 1.8 bitcast_and_fusion
  239.7 2.7 constant_dynamic-slice_fusion
  242.5 4.0 %fusion.2 = (f32[2,8,128]{2,1,0:T(8,128)S(1)}, f32[2,2048,128,8]{2,1,3,0:T(8,128)S(1)}) fusion(pred[128,2048]{0,1:T(8,128)(4,1)S(1)} %bitcast_and_fusion, bf16[2048,2,256,1]{0,2,3,1:T(8,128)(2,1)S(1)} %bitcast.53, bf16[128,2,8,256]{3,0,2,1:T(8,128)(2,1)S(1)} %copy-done), kind=kOutput, calls=%fused_computation.3 | convolution fusion | flops 2160064512 | bytes 20193280 | tf_op jit(solution)/shard_map/while/body/eval_jaxpr/cond/branch_1_fun/rkgd,nkd->kgrn/dot_general | solution.py:56
  246.4 4.0 %fusion.4 = f32[2,8,128]{2,1,0:T(8,128)S(1)} fusion(f32[2,2048,128,8]{2,1,3,0:T(8,128)S(1)} %get-tuple-element.413, f32[2,8,128]{2,1,0:T(8,128)S(1)} %max.4, pred[128,2048]{0,1:T(8,128)(4,1)S(1)} %bitcast_and_fusion), kind=kLoop, calls=%fused_computation.5 | loop fusion | flops 20969472 | bytes 17055744 | tf_op jit(solution)/shard_map/while/body/eval_jaxpr/cond/branch_1_fun/reduce_sum | solution.py:68
  250.4 7.6 %multiply_add_fusion = f32[2,8,128,256]{3,2,1,0:T(8,128)} fusion(f32[2,8,128,256]{3,2,1,0:T(8,128)} %get-tuple-element.282, bf16[2048,2,256,1]{0,2,3,1:T(8,128)(2,1)S(1)} %bitcast.52, f32[2,2048,128,8]{2,1,3,0:T(8,128)S(1)} %get-tuple-element.413, f32[2,8,128]{2,1,0:T(8,128)S(1)} %max.4, pred[128,2048]{0,1:T(8,128)(4,1)S(1)} %bitcast_and_fusion, ...), kind=kOutput, calls=%fused_computation.8 | convolution fusion | flops 2169503744 | bytes 23347200 | tf_op jit(solution)/shard_map/while/body/eval_jaxpr/cond/branch_1_fun/kgrn,nkd->kgrd/dot_general | solution.py:69
  263.1 0.7 add_add_fusion.2
  263.8 0.7 broadcast_compare_fusion.6
  264.5 1.4 and_reduce_fusion.2
  266.6 20.9 %conditional.3 = ((f32[2,8,128]{2,1,0:T(8,128)S(1)}, f32[2,8,128]{2,1,0:T(8,128)S(1)}, f32[2,8,128,256]{3,2,1,0:T(8,128)})) conditional(s32[]{:T(128)} %convert_element_type.42, (f32[2,8,128]{2,1,0:T(8,128)S(1)}, f32[2,8,128]{2,1,0:T(8,128)S(1)}, f32[2,8,128,256]{3,2,1,0:T(8,128)}) %tuple.57, (s32[]{:T(128)}, s32[1,2048]{1,0:T(1,128)S(1)}, ...), branch_computations={%region_2.2_spmd, %region_3.5_spmd} | conditional | flops 4351862784 | bytes 73577536 | solution.py:77
  266.6 0.7 compare_reduce_fusion
  267.3 1.8 bitcast_and_fusion
  269.1 2.7 constant_dynamic-slice_fusion
  271.9 4.0 %fusion.2 = (f32[2,8,128]{2,1,0:T(8,128)S(1)}, f32[2,2048,128,8]{2,1,3,0:T(8,128)S(1)}) fusion(pred[128,2048]{0,1:T(8,128)(4,1)S(1)} %bitcast_and_fusion, bf16[2048,2,256,1]{0,2,3,1:T(8,128)(2,1)S(1)} %bitcast.53, bf16[128,2,8,256]{3,0,2,1:T(8,128)(2,1)S(1)} %copy-done), kind=kOutput, calls=%fused_computation.3 | convolution fusion | flops 2160064512 | bytes 20193280 | tf_op jit(solution)/shard_map/while/body/eval_jaxpr/cond/branch_1_fun/rkgd,nkd->kgrn/dot_general | solution.py:56
  275.8 4.0 %fusion.4 = f32[2,8,128]{2,1,0:T(8,128)S(1)} fusion(f32[2,2048,128,8]{2,1,3,0:T(8,128)S(1)} %get-tuple-element.413, f32[2,8,128]{2,1,0:T(8,128)S(1)} %max.4, pred[128,2048]{0,1:T(8,128)(4,1)S(1)} %bitcast_and_fusion), kind=kLoop, calls=%fused_computation.5 | loop fusion | flops 20969472 | bytes 17055744 | tf_op jit(solution)/shard_map/while/body/eval_jaxpr/cond/branch_1_fun/reduce_sum | solution.py:68
  279.8 7.6 %multiply_add_fusion = f32[2,8,128,256]{3,2,1,0:T(8,128)} fusion(f32[2,8,128,256]{3,2,1,0:T(8,128)} %get-tuple-element.282, bf16[2048,2,256,1]{0,2,3,1:T(8,128)(2,1)S(1)} %bitcast.52, f32[2,2048,128,8]{2,1,3,0:T(8,128)S(1)} %get-tuple-element.413, f32[2,8,128]{2,1,0:T(8,128)S(1)} %max.4, pred[128,2048]{0,1:T(8,128)(4,1)S(1)} %bitcast_and_fusion, ...), kind=kOutput, calls=%fused_computation.8 | convolution fusion | flops 2169503744 | bytes 23347200 | tf_op jit(solution)/shard_map/while/body/eval_jaxpr/cond/branch_1_fun/kgrn,nkd->kgrd/dot_general | solution.py:69
  287.5 2.0 divide_bitcast_fusion
  289.8 1.5 multiply_convert_fusion
  (62 shorter events, 3.8 us)
Async XLA Ops:
  6.5 4.4 %copy-start.3 = (s32[1,64]{1,0:T(1,128)S(1)}, s32[1,64]{1,0:T(1,128)}, u32[]{:S(2)}) copy-start(s32[1,64]{1,0:T(1,128)} %param.15) | copy-start | bytes 772
  6.5 46.0 %copy-start.2 = (s32[128]{0:T(128)S(1)}, s32[128]{0:T(128)}, u32[]{:S(2)}) copy-start(s32[128]{0:T(128)} %param.14) | copy-start | bytes 1540
  6.5 88.1 %all-gather.5.cloned.1.call-start = ((), (), s32[]{:S(2)}) async-start(), calls=%async_computation | async-start | bytes 8519680 | tf_op jit(solution)/shard_map/all_gather | solution.py:112
  7.3 170.5 %all-gather.7.cloned.1.call-start = ((), (), s32[]{:S(2)}) async-start(), calls=%async_computation.1 | async-start | bytes 8519680 | tf_op jit(solution)/shard_map/all_gather | solution.py:113
  210.3 2.8 copy-start
  239.7 2.8 copy-start
  269.1 2.8 copy-start
  287.5 2.3 copy-start.1
Sparse Core Ops, SparseCore 0:
  10.1 84.4 all-gather.4
  97.4 80.3 all-gather.6
where the time goes:
time: 299 us; the launch traced here: 298 us
  blocking collectives  78.7 us (26%)
  waiting for transfers between devices  77.8 us (26%)
  local copies, waits for them, and re-layouts  39.7 us (13%)
  matrix products  35 us (12%)
  other arithmetic  34.1 us (11%)
  loops' own time  19.3 us (6%)
  between operations  13.5 us (5%)
    all_gather x1, waiting for transfers between devices, fold_all(): lax.all_gather(value_rows, 'cp', axis=0, tiled=True)  71.6 us
    all_gather x1, blocking collectives, on_device(): lax.all_gather(block_lists, 'cp', axis=0, tiled=True)  41.3 us
    all_gather x1, blocking collectives, on_device(): lax.all_gather(doc_ids, 'cp', axis=0, tiled=True)  37.3 us
    unnamed x11, local copies, waits for them, and re-layouts  26.1 us
    dot_general x3, matrix products, compute(): jnp.einsum('kgrn,nkd->kgrd', weights.astype(jnp.bfloat16), value_block.re...  22.9 us
    another operation x1, loops' own time, fold(): state, _ = lax.scan(advance, state, (key_steps, value_steps, starts))  19.1 us
    reduce_sum x3, other arithmetic, compute(): new_sum = decay * running_sum + jnp.sum(weights, axis=-1)  11.9 us
    dot_general x3, matrix products, compute(): jnp.einsum('rkgd,nkd->kgrn', grouped, key_block.reshape(width, KVH, HD),...  11.9 us
  transfers between devices with their start and end apart: 2, of which 2 were waited for; matrix products, arithmetic and copies ran while one was open for 5% of the time, Pallas kernels for 0%

commit v1 on v0

v1 whole, which is shorter than its diff:
```python
import functools
import math

import jax
import jax.numpy as jnp
from jax import lax
from jax.experimental import pallas as pl
from jax.experimental.pallas import tpu as pltpu
from jax.sharding import PartitionSpec as P

H = 16
KVH = 2
HD = 256
BLK = 128
GROUPS = H // KVH
NX, NZ = 4, 8
UNIT = 2 * BLK
META = 16
ROWS = GROUPS * UNIT
HALF = GROUPS * HD
LOG2E = 1.4426950408889634
NEG = -1e30


def permutation(target):
    pairs = []
    for x in range(NX):
        for z in range(NZ):
            for core in range(2):
                goal = target(x, z, core)
                if goal is not None:
                    gx, gz, gc = goal
                    pairs.append(((x * NZ + z) * 2 + core, (gx * NZ + gz) * 2 + gc))
    return pairs


SWAP = permutation(lambda x, z, c: (x, z, 1 - c))
ONE_X = permutation(lambda x, z, c: (x + 1, z, c) if x < 3 else None)
TWO_X = permutation(lambda x, z, c: ((x + 2) % NX, z, c))
NEAR_UP = permutation(
    lambda x, z, c: (x, z + 1, c) if z < 7 else ((x + 2, 0, c) if x < 2 else None)
)
NEAR_DOWN = permutation(
    lambda x, z, c: (x, z - 1, c) if z > 0 else ((x + 2) % NX, 7, c)
)
MID_UP = permutation(lambda x, z, c: (x, (z + 1) % NZ, c) if x > 0 else None)
MID_DOWN = permutation(lambda x, z, c: (x, (z - 1) % NZ, c) if x > 0 else None)


def attend(own_at, last, count, *refs):
    flags, core, q, qdocs = refs[:4]
    units = refs[4 : 4 + count]
    rest = list(refs[4 + count :])
    first = own_at is not None
    if not first:
        m_in, l_in, acc_in = rest[:3]
        rest = rest[3:]
    if last:
        gate_mine, gate_other = rest[:2]
        rest = rest[2:]
        out_mine, out_other = rest[:2]
    else:
        m_out, l_out, acc_out = rest[:3]
        rest = rest[3:]
    me = core[0]
    lane = lax.broadcasted_iota(jnp.int32, (1, UNIT), 1)
    biases = []
    for j in range(count):
        kd = units[j][UNIT : UNIT + META, :].astype(jnp.float32)[0:1, :]
        halves = []
        for r in range(2):
            listed = jnp.where(lane < BLK, flags[j, 2 * r], flags[j, 2 * r + 1])
            kd_r = jnp.where(listed == 1, kd, -1.0)
            qd = qdocs[r * BLK : (r + 1) * BLK, :]
            qd = jnp.concatenate([qd, qd], axis=1)
            seen = qd == kd_r
            if own_at == j:
                col = lax.broadcasted_iota(jnp.int32, (BLK, UNIT), 1)
                row = lax.broadcasted_iota(jnp.int32, (BLK, UNIT), 0)
                low = jnp.where(me == 0, col, lax.rem(col + BLK, UNIT))
                place = row + jnp.where(me == r, 0, BLK)
                seen = seen & (low <= place)
            halves.append(jnp.where(seen, 0.0, NEG))
        biases.append(jnp.concatenate(halves, axis=0))
    scale = LOG2E / math.sqrt(HD)
    for h in range(GROUPS):
        qh = q[h * UNIT : (h + 1) * UNIT, :]
        scores = []
        for j in range(count):
            s = lax.dot_general(
                qh,
                units[j][0:UNIT, :],
                (((1,), (1,)), ((), ())),
                preferred_element_type=jnp.float32,
            )
            scores.append(s * scale + biases[j])
        top = scores[0]
        for s in scores[1:]:
            top = jnp.maximum(top, s)
        top = jnp.max(top, axis=1, keepdims=True)
        if first:
            m_new = jnp.broadcast_to(top, (UNIT, BLK))
        else:
            m_old = m_in[h]
            m_new = jnp.maximum(m_old, top)
            alpha = jnp.exp2(m_old - m_new)
        m_wide = jnp.concatenate([m_new, m_new], axis=1)
        total = None
        product = None
        for j in range(count):
            p = jnp.exp2(scores[j] - m_wide)
            part = p[:, :BLK] + p[:, BLK:]
            total = part if total is None else total + part
            pv = jnp.dot(
                p.astype(jnp.bfloat16),
                units[j][UNIT + META :, :],
                preferred_element_type=jnp.float32,
            )
            product = pv if product is None else product + pv
        if not first:
            total = total + alpha * l_in[h]
            wide = jnp.concatenate([alpha, alpha], axis=1)
            product = product + wide * acc_in[h]
        if last:
            inv = 1.0 / jnp.sum(total, axis=1, keepdims=True)
            att = product * inv
            base = pl.multiple_of(me * HALF + h * HD, HD)
            g = gate_mine[:, pl.ds(base, HD)].astype(jnp.float32)
            out_mine[:, h * HD : (h + 1) * HD] = (
                att[:BLK] * jax.nn.sigmoid(g)
            ).astype(jnp.bfloat16)
            g = gate_other[:, h * HD : (h + 1) * HD].astype(jnp.float32)
            out_other[:, h * HD : (h + 1) * HD] = (
                att[BLK:] * jax.nn.sigmoid(g)
            ).astype(jnp.bfloat16)
        else:
            m_out[h] = m_new
            l_out[h] = total
            acc_out[h] = product


def attend_call(core, flags, q, qdocs, units, state=None, gates=None, own_at=None):
    count = len(units)
    last = gates is not None
    smem = pl.BlockSpec(memory_space=pltpu.SMEM)
    vmem = pl.BlockSpec(memory_space=pltpu.VMEM)
    args = [flags, core, q, qdocs, *units]
    aliases = {}
    if state is not None:
        if not last:
            aliases = {len(args) + i: i for i in range(3)}
        args += list(state)
    if last:
        args += list(gates)
        shapes = [jax.ShapeDtypeStruct((BLK, HALF), jnp.bfloat16)] * 2
    else:
        shapes = [
            jax.ShapeDtypeStruct((GROUPS, UNIT, BLK), jnp.float32),
            jax.ShapeDtypeStruct((GROUPS, UNIT, BLK), jnp.float32),
            jax.ShapeDtypeStruct((GROUPS, UNIT, HD), jnp.float32),
        ]
    specs = [smem, smem] + [vmem] * (len(args) - 2)
    return pl.pallas_call(
        functools.partial(attend, own_at, last, count),
        out_shape=shapes,
        in_specs=specs,
        out_specs=[vmem] * len(shapes),
        input_output_aliases=aliases,
        compiler_params=pltpu.CompilerParams(vmem_limit_bytes=32 << 20),
        cost_estimate=pl.CostEstimate(
            flops=4 * ROWS * UNIT * HD * count,
            bytes_accessed=count * 270000 + 9000000,
            transcendentals=ROWS * UNIT * count,
        ),
    )(*args)


def on_device(query_rows, key_rows, value_rows, gate_rows, doc_ids, block_lists):
    place = lax.axis_index("cp")
    core = lax.rem(place, 2)
    chip = place // 2
    x, z = chip // NZ, lax.rem(chip, NZ)

    def send(value, pairs):
        return lax.ppermute(value, "cp", pairs)

    def take(rows, which, width):
        return lax.dynamic_slice_in_dim(rows, which * width, width, 1)

    docs_row = doc_ids.astype(jnp.bfloat16).reshape(1, BLK)
    lists_row = jnp.pad(
        block_lists.astype(jnp.bfloat16), ((0, 0), (0, BLK - block_lists.shape[1]))
    )
    notes = jnp.concatenate(
        [docs_row, lists_row, jnp.zeros((META - 2, BLK), jnp.bfloat16)], axis=0
    )
    notes_wide = jnp.concatenate([notes, jnp.zeros_like(notes)], axis=1)
    parcel = jnp.concatenate(
        [take(key_rows, 1 - core, HD), take(value_rows, 1 - core, HD), notes_wide], axis=0
    )
    got = send(parcel, SWAP)
    unit = jnp.concatenate(
        [
            take(key_rows, core, HD),
            got[:BLK],
            jnp.concatenate([notes, got[2 * BLK :, :BLK]], axis=1),
            take(value_rows, core, HD),
            got[BLK : 2 * BLK],
        ],
        axis=0,
    )
    up = [unit]
    mid0 = send(unit, ONE_X)
    low0 = send(unit, TWO_X)
    down = [low0]
    mup, mdown = [mid0], [mid0]
    for s in range(4):
        up.append(send(up[-1], NEAR_UP))
        mup.append(send(mup[-1], MID_UP))
        if s < 3:
            down.append(send(down[-1], NEAR_DOWN))
            mdown.append(send(mdown[-1], MID_DOWN))

    q_other = send(take(query_rows, 1 - core, HALF), SWAP)
    gate_other = send(take(gate_rows, 1 - core, HALF), SWAP)
    q = jnp.concatenate([take(query_rows, core, HALF), q_other], axis=0)
    q = q.reshape(UNIT, GROUPS, HD).transpose(1, 0, 2).reshape(ROWS, HD)
    meta = unit[UNIT : UNIT + 2].astype(jnp.float32)
    qdocs = jnp.broadcast_to(meta[0][:, None], (UNIT, BLK))
    lists = jnp.stack([meta[1, :64], meta[1, BLK : BLK + 64]])

    def up_id(s):
        return jnp.where(z >= s, chip - s, jnp.where(x >= 2, chip - s - NZ, -1))

    def down_id(s):
        return jnp.where(
            z + s < NZ, jnp.where(x >= 2, chip - 2 * NZ + s, -1), chip + s - NZ
        )

    def mid_id(s):
        return jnp.where(x >= 1, (x - 1) * NZ + lax.rem(z + s + NZ, NZ), -1)

    groups = [
        [(up[0], chip)],
        [(up[1], up_id(1)), (down[0], down_id(0)), (mup[0], mid_id(0))],
        [(up[2], up_id(2)), (down[1], down_id(1)), (mup[1], mid_id(-1)), (mdown[1], mid_id(1))],
        [(up[3], up_id(3)), (down[2], down_id(2)), (mup[2], mid_id(-2)), (mdown[2], mid_id(2))],
        [
            (up[4], up_id(4)),
            (down[3], down_id(3)),
            (mup[3], mid_id(-3)),
            (mdown[3], mid_id(3)),
            (mup[4], mid_id(-4)),
        ],
    ]
    ids = jnp.stack([i for group in groups for _, i in group])
    cols = 2 * ids[:, None] + jnp.stack([core, 1 - core])[None, :]
    cols = jnp.where(ids[:, None] >= 0, cols, -1)
    hot = cols[:, None, :, None] == jnp.arange(64, dtype=jnp.int32)[None, None, None, :]
    table = jnp.sum(jnp.where(hot, lists[None, :, None, :], 0.0), axis=-1)
    table = table.astype(jnp.int32).reshape(ids.shape[0], 4)

    core1 = core.reshape(1)
    state = None
    at = 0
    for n, group in enumerate(groups):
        flags = table[at : at + len(group)]
        at += len(group)
        gates = (gate_rows, gate_other) if n == len(groups) - 1 else None
        state = attend_call(
            core1, flags, q, qdocs, [u for u, _ in group], state, gates, 0 if n == 0 else None
        )
    mine, other = state
    back = send(other, SWAP)
    return jnp.where(
        core == 0,
        jnp.concatenate([mine, back], axis=1),
        jnp.concatenate([back, mine], axis=1),
    )


def solution(mesh):
    return jax.shard_map(
        on_device,
        mesh=mesh,
        in_specs=(
            P(("dp", "cp"), None),
            P(("dp", "cp"), None),
            P(("dp", "cp"), None),
            P(("dp", "cp"), None),
            P(("dp", "cp")),
            P(("dp", "cp"), None),
        ),
        out_specs=P(("dp", "cp"), None),
        check_vma=False,
    )
```

time: 299 us -> 92.1 us (0.31)
  blocking collectives: 78.7 us -> 0 us
  waiting for transfers between devices: 77.8 us -> 3.37 us
  starting transfers between devices: 0.04 us -> 59.5 us
  local copies, waits for them, and re-layouts: 39.7 us -> 4.46 us
  matrix products: 35 us -> 0 us
  other arithmetic: 34.1 us -> 2.95 us
  Pallas kernels: 0 us -> 20.7 us
  loops' own time: 19.3 us -> 0 us
  between operations: 13.5 us -> 0.61 us
    all_gather x2 -> x0, blocking collectives: 78.7 us -> none  [the longest x1 41.3 us: on_device(): lax.all_gather(block_lists, 'cp', axis=0, tiled=True)]
    all_gather x2 -> x0, waiting for transfers between devices: 76.4 us -> none  [the longest x1 71.6 us: fold_all(): lax.all_gather(value_rows, 'cp', axis=0, tiled=True)]
    ppermute x0 -> x20, starting transfers between devices: none -> 59.5 us  [send(): return lax.ppermute(value, 'cp', pairs)]
    dot_general x7 -> x0, matrix products: 35 us -> none  [the longest x3 22.9 us: compute(): jnp.einsum('kgrn,nkd->kgrd', weights.astype(jnp.bfloat16), value_block.re...]
    unnamed x11 -> x13, local copies, waits for them, and re-layouts: 26.1 us -> 0.06 us
    pallas_call x0 -> x5, Pallas kernels: none -> 20.7 us  [attend_call(): pl.pallas_call(functools.partial(attend, own_at, last, count), out_shape=...]
    another operation x5 -> x0, loops' own time: 19.3 us -> none  [the longest x1 19.1 us: fold(): state, _ = lax.scan(advance, state, (key_steps, value_steps, starts))]
    reduce_sum x3 -> x1, other arithmetic: 11.9 us -> 0.13 us  [on_device(): table = jnp.sum(jnp.where(hot, lists[None, :, None, :], 0.0), axis=-1)]
  transfers between devices with their start and end apart: 2 -> 20, of which waited for: 2 -> 3; matrix products, arithmetic and copies ran while one was open for 5% -> 4% of each run, Pallas kernels for 0% -> 16%
where the time goes in v1:
time: 92.1 us; the launch traced here: 91.6 us
  starting transfers between devices  59.5 us (65%)
  Pallas kernels  20.7 us (22%)
  local copies, waits for them, and re-layouts  4.46 us (5%)
  waiting for transfers between devices  3.37 us (4%)
  other arithmetic  2.95 us (3%)
    ppermute x20, starting transfers between devices, send(): return lax.ppermute(value, 'cp', pairs)  59.5 us
    pallas_call x5, Pallas kernels, attend_call(): pl.pallas_call(functools.partial(attend, own_at, last, count), out_shape=...  20.7 us
    ppermute x20, waiting for transfers between devices, send(): return lax.ppermute(value, 'cp', pairs)  3.37 us
    dynamic_slice x2, local copies, waits for them, and re-layouts, take(): return lax.dynamic_slice_in_dim(rows, which * width, width, 1)  3.25 us
  transfers between devices with their start and end apart: 20, of which 3 were waited for; matrix products, arithmetic and copies ran while one was open for 4% of the time, Pallas kernels for 16%

profile of v1, /device:TPU:15, one launch (start us, length us, event | category | flops | bytes accessed | tf_op | source)
XLA Modules:
  0.0 91.6 jit_solution(15967385104628011391)
XLA Ops:
  0.0 2.4 %constant_dynamic-slice_fusion.2 = (bf16[128,2048]{1,0:T(8,128)(2,1)}, bf16[128,2048]{1,0:T(8,128)(2,1)}) fusion(bf16[128,4096]{1,0:T(8,128)(2,1)} %param.6, s32[]{:T(128)S(6)} %select_n.146, s32[]{:T(128)S(6)} %select_n.147), kind=kLoop, calls=%fused_computation.23 | loop fusion | bytes 2097160 | tf_op jit(solution)/shard_map/dynamic_slice | solution.py:188
  2.4 0.7 collective-permute-start.1
  3.3 0.1 collective-permute-start
  3.5 0.1 stack.83
  3.6 0.9 constant_dynamic-slice_fusion
  4.5 0.1 pad_add_fusion
  4.6 0.1 add_select_fusion
  4.6 0.2 collective-permute-done
  4.9 1.3 %collective-permute-start.10 = (bf16[528,256]{1,0:T(8,128)(2,1)S(1)}, bf16[528,256]{1,0:T(8,128)(2,1)S(1)}, u32[]{:S(2)}, u32[]{:S(2)}) collective-permute-start(bf16[528,256]{1,0:T(8,128)(2,1)S(1)} %slice_dynamic-update-slice_fusion.refs_4_), channel_id=1, source_target_pairs={{0,16},{1,17},{2,18},{3,19},{4,20},{5,21},{6,22},{7,23},{8,24},{9,... | collective-permute-start | bytes 811016 | tf_op jit(solution)/shard_map/ppermute | solution.py:185
  6.2 0.1 iota_compare_fusion
  6.3 3.5 %collective-permute-start.2 = (bf16[528,256]{1,0:T(8,128)(2,1)S(1)}, bf16[528,256]{1,0:T(8,128)(2,1)S(1)}, u32[]{:S(2)}, u32[]{:S(2)}) collective-permute-start(bf16[528,256]{1,0:T(8,128)(2,1)S(1)} %slice_dynamic-update-slice_fusion.refs_4_), channel_id=1, source_target_pairs={{0,2},{1,3},{2,4},{3,5},{4,6},{5,7},{6,8},{7,9},{8,10},{9,11},{10,... | collective-permute-start | bytes 811016 | tf_op jit(solution)/shard_map/ppermute | solution.py:185
  9.9 3.1 %collective-permute-start.6 = (bf16[528,256]{1,0:T(8,128)(2,1)S(1)}, bf16[528,256]{1,0:T(8,128)(2,1)S(1)}, u32[]{:S(2)}, u32[]{:S(2)}) collective-permute-start(bf16[528,256]{1,0:T(8,128)(2,1)S(1)} %slice_dynamic-update-slice_fusion.refs_4_), channel_id=1, source_target_pairs={{0,32},{1,33},{2,34},{3,35},{4,36},{5,37},{6,38},{7,39},{8,40},{9,... | collective-permute-start | bytes 811016 | tf_op jit(solution)/shard_map/ppermute | solution.py:185
  12.9 1.6 %collective-permute-done.10.refs_6_ = bf16[528,256]{1,0:T(8,128)(2,1)S(1)} collective-permute-done((bf16[528,256]{1,0:T(8,128)(2,1)S(1)}, bf16[528,256]{1,0:T(8,128)(2,1)S(1)}, u32[]{:S(2)}, u32[]{:S(2)}) %collective-permute-start.10) | collective-permute-done | bytes 270368 | tf_op jit(solution)/shard_map/ppermute | solution.py:185
  14.5 3.5 %collective-permute-start.11 = (bf16[528,256]{1,0:T(8,128)(2,1)S(1)}, bf16[528,256]{1,0:T(8,128)(2,1)S(1)}, u32[]{:S(2)}, u32[]{:S(2)}) collective-permute-start(bf16[528,256]{1,0:T(8,128)(2,1)S(1)} %collective-permute-done.10.refs_6_), channel_id=1, source_target_pairs={{16,18},{17,19},{18,20},{19,21},{20,22},{21,23},{22,24},{23,25},{2... | collective-permute-start | bytes 811016 | tf_op jit(solution)/shard_map/ppermute | solution.py:185
  18.1 5.9 %collective-permute-start.14 = (bf16[528,256]{1,0:T(8,128)(2,1)S(1)}, bf16[528,256]{1,0:T(8,128)(2,1)S(1)}, u32[]{:S(2)}, u32[]{:S(2)}) collective-permute-start(bf16[528,256]{1,0:T(8,128)(2,1)S(1)} %collective-permute-done.10.refs_6_), channel_id=1, source_target_pairs={{16,30},{17,31},{18,16},{19,17},{20,18},{21,19},{22,20},{23,21},{2... | collective-permute-start | bytes 811016 | tf_op jit(solution)/shard_map/ppermute | solution.py:185
  23.9 1.9 %collective-permute-start.3 = (bf16[528,256]{1,0:T(8,128)(2,1)S(1)}, bf16[528,256]{1,0:T(8,128)(2,1)S(1)}, u32[]{:S(2)}, u32[]{:S(2)}) collective-permute-start(bf16[528,256]{1,0:T(8,128)(2,1)S(1)} %collective-permute-done.2.refs_4_), channel_id=1, source_target_pairs={{0,2},{1,3},{2,4},{3,5},{4,6},{5,7},{6,8},{7,9},{8,10},{9,11},{10,... | collective-permute-start | bytes 811016 | tf_op jit(solution)/shard_map/ppermute | solution.py:185
  25.9 5.1 %collective-permute-start.7 = (bf16[528,256]{1,0:T(8,128)(2,1)S(1)}, bf16[528,256]{1,0:T(8,128)(2,1)S(1)}, u32[]{:S(2)}, u32[]{:S(2)}) collective-permute-start(bf16[528,256]{1,0:T(8,128)(2,1)S(1)} %collective-permute-done.6.refs_5_), channel_id=1, source_target_pairs={{0,46},{1,47},{2,0},{3,1},{4,2},{5,3},{6,4},{7,5},{8,6},{9,7},{10,... | collective-permute-start | bytes 811016 | tf_op jit(solution)/shard_map/ppermute | solution.py:185
  31.0 1.9 %collective-permute-start.12 = (bf16[528,256]{1,0:T(8,128)(2,1)S(1)}, bf16[528,256]{1,0:T(8,128)(2,1)S(1)}, u32[]{:S(2)}, u32[]{:S(2)}) collective-permute-start(bf16[528,256]{1,0:T(8,128)(2,1)S(1)} %collective-permute-done.11.refs_6_), channel_id=1, source_target_pairs={{16,18},{17,19},{18,20},{19,21},{20,22},{21,23},{22,24},{23,25},{2... | collective-permute-start | bytes 811016 | tf_op jit(solution)/shard_map/ppermute | solution.py:185
  32.9 0.1 select_reduce_fusion
  33.1 0.1 slice.67.refs_0_
  33.2 0.1 copy.29
  33.3 0.1 copy.30.refs_0_
  33.4 0.1 copy.28
  33.5 0.1 copy.31.refs_0_
  33.6 0.1 copy.27
  33.7 0.1 copy.32.refs_0_
  33.8 0.1 copy.25
  33.9 0.1 copy.33.refs_0_
  34.0 2.9 %collective-permute-start.18 = (bf16[128,2048]{1,0:T(8,128)(2,1)}, bf16[128,2048]{1,0:T(8,128)(2,1)S(1)}, u32[]{:S(2)}, u32[]{:S(2)}) collective-permute-start(bf16[128,2048]{1,0:T(8,128)(2,1)} %constant_dynamic-slice_fusion), channel_id=1, source_target_pairs={{0,1},{1,0},{2,3},{3,2},{4,5},{5,4},{6,7},{7,6},{8,9},{9,8},{10,11... | collective-permute-start | bytes 1572872 | tf_op jit(solution)/shard_map/ppermute | solution.py:185
  36.9 4.8 %collective-permute-start.15 = (bf16[528,256]{1,0:T(8,128)(2,1)S(1)}, bf16[528,256]{1,0:T(8,128)(2,1)S(1)}, u32[]{:S(2)}, u32[]{:S(2)}) collective-permute-start(bf16[528,256]{1,0:T(8,128)(2,1)S(1)} %collective-permute-done.14.refs_7_), channel_id=1, source_target_pairs={{16,30},{17,31},{18,16},{19,17},{20,18},{21,19},{22,20},{23,21},{2... | collective-permute-start | bytes 811016 | tf_op jit(solution)/shard_map/ppermute | solution.py:185
  41.7 1.9 %collective-permute-start.4 = (bf16[528,256]{1,0:T(8,128)(2,1)S(1)}, bf16[528,256]{1,0:T(8,128)(2,1)S(1)}, u32[]{:S(2)}, u32[]{:S(2)}) collective-permute-start(bf16[528,256]{1,0:T(8,128)(2,1)S(1)} %collective-permute-done.3.refs_4_), channel_id=1, source_target_pairs={{0,2},{1,3},{2,4},{3,5},{4,6},{5,7},{6,8},{7,9},{8,10},{9,11},{10,... | collective-permute-start | bytes 811016 | tf_op jit(solution)/shard_map/ppermute | solution.py:185
  43.7 5.1 %collective-permute-start.8 = (bf16[528,256]{1,0:T(8,128)(2,1)S(1)}, bf16[528,256]{1,0:T(8,128)(2,1)S(1)}, u32[]{:S(2)}, u32[]{:S(2)}) collective-permute-start(bf16[528,256]{1,0:T(8,128)(2,1)S(1)} %collective-permute-done.7.refs_5_), channel_id=1, source_target_pairs={{0,46},{1,47},{2,0},{3,1},{4,2},{5,3},{6,4},{7,5},{8,6},{9,7},{10,... | collective-permute-start | bytes 811016 | tf_op jit(solution)/shard_map/ppermute | solution.py:185
  48.8 1.9 %collective-permute-start.13 = (bf16[528,256]{1,0:T(8,128)(2,1)S(1)}, bf16[528,256]{1,0:T(8,128)(2,1)S(1)}, u32[]{:S(2)}, u32[]{:S(2)}) collective-permute-start(bf16[528,256]{1,0:T(8,128)(2,1)S(1)} %collective-permute-done.12.refs_6_), channel_id=1, source_target_pairs={{16,18},{17,19},{18,20},{19,21},{20,22},{21,23},{22,24},{23,25},{2... | collective-permute-start | bytes 811016 | tf_op jit(solution)/shard_map/ppermute | solution.py:185
  50.7 1.3 %pad_maximum_fusion = bf16[256,2048]{1,0:T(8,128)(2,1)S(1)} fusion(bf16[128,2048]{1,0:T(8,128)(2,1)} %collective-permute-done.1, bf16[128,2048]{1,0:T(8,128)(2,1)} %get-tuple-element.33), kind=kLoop, calls=%fused_computation.1 | loop fusion | flops 2097152 | bytes 2097152 | tf_op jit(solution)/shard_map/concatenate | solution.py:226
  52.0 0.1 copy.36
  52.1 0.1 broadcast_in_dim.56.refs_3_
  52.2 1.7 %shard_map.64 = (f32[8,256,128]{2,1,0:T(8,128)S(1)}, f32[8,256,128]{2,1,0:T(8,128)S(1)}, f32[8,256,256]{2,1,0:T(8,128)S(1)}) custom-call(s32[1,4]{1,0:T(1,128)S(1)} %slice.67.refs_0_, s32[1]{0:T(128)} %bitcast.17.refs_1_, bf16[2048,256]{1,0:T(8,128)(2,1)S(1)} %bitcast.33, f32[256,128]{1,0:T(8,128)S(1)} %broadcast_in_dim.56.refs_3_, ...), custom_call_target="tpu_custom_call" | custom-call | flops 536870912 | bytes 9270000 | tf_op jit(solution)/shard_map/pallas_call | solution.py:163
  54.0 3.6 %shard_map.65 = (f32[8,256,128]{2,1,0:T(8,128)S(1)}, f32[8,256,128]{2,1,0:T(8,128)S(1)}, f32[8,256,256]{2,1,0:T(8,128)S(1)}) custom-call(s32[3,4]{1,0:T(4,128)S(1)} %copy.30.refs_0_, s32[1]{0:T(128)} %bitcast.17.refs_1_, bf16[2048,256]{1,0:T(8,128)(2,1)S(1)} %bitcast.34, ...), custom_call_target="tpu_custom_call", output_to_operand_aliasing={{0}: (7, {}), {1}: (8, {}), {2}: (9, {})} | custom-call | flops 1610612736 | bytes 9810000 | tf_op jit(solution)/shard_map/pallas_call | solution.py:163
  57.6 4.6 %collective-permute-start.16 = (bf16[528,256]{1,0:T(8,128)(2,1)S(1)}, bf16[528,256]{1,0:T(8,128)(2,1)S(1)}, u32[]{:S(2)}, u32[]{:S(2)}) collective-permute-start(bf16[528,256]{1,0:T(8,128)(2,1)S(1)} %collective-permute-done.15.refs_7_), channel_id=1, source_target_pairs={{16,30},{17,31},{18,16},{19,17},{20,18},{21,19},{22,20},{23,21},{2... | collective-permute-start | bytes 811016 | tf_op jit(solution)/shard_map/ppermute | solution.py:185
  62.2 1.9 %collective-permute-start.5 = (bf16[528,256]{1,0:T(8,128)(2,1)S(1)}, bf16[528,256]{1,0:T(8,128)(2,1)S(1)}, u32[]{:S(2)}, u32[]{:S(2)}) collective-permute-start(bf16[528,256]{1,0:T(8,128)(2,1)S(1)} %collective-permute-done.4.refs_4_), channel_id=1, source_target_pairs={{0,2},{1,3},{2,4},{3,5},{4,6},{5,7},{6,8},{7,9},{8,10},{9,11},{10,... | collective-permute-start | bytes 811016 | tf_op jit(solution)/shard_map/ppermute | solution.py:185
  64.2 5.1 %collective-permute-start.9 = (bf16[528,256]{1,0:T(8,128)(2,1)S(1)}, bf16[528,256]{1,0:T(8,128)(2,1)S(1)}, u32[]{:S(2)}, u32[]{:S(2)}) collective-permute-start(bf16[528,256]{1,0:T(8,128)(2,1)S(1)} %collective-permute-done.8.refs_5_), channel_id=1, source_target_pairs={{0,46},{1,47},{2,0},{3,1},{4,2},{5,3},{6,4},{7,5},{8,6},{9,7},{10,... | collective-permute-start | bytes 811016 | tf_op jit(solution)/shard_map/ppermute | solution.py:185
  69.3 2.1 %collective-permute-start.17 = (bf16[528,256]{1,0:T(8,128)(2,1)S(1)}, bf16[528,256]{1,0:T(8,128)(2,1)S(1)}, u32[]{:S(2)}, u32[]{:S(2)}) collective-permute-start(bf16[528,256]{1,0:T(8,128)(2,1)S(1)} %collective-permute-done.13.refs_6_), channel_id=1, source_target_pairs={{16,18},{17,19},{18,20},{19,21},{20,22},{21,23},{22,24},{23,25},{2... | collective-permute-start | bytes 811016 | tf_op jit(solution)/shard_map/ppermute | solution.py:185
  71.4 4.6 %shard_map.66 = (f32[8,256,128]{2,1,0:T(8,128)S(1)}, f32[8,256,128]{2,1,0:T(8,128)S(1)}, f32[8,256,256]{2,1,0:T(8,128)S(1)}) custom-call(s32[4,4]{1,0:T(4,128)S(1)} %copy.31.refs_0_, s32[1]{0:T(128)} %bitcast.17.refs_1_, bf16[2048,256]{1,0:T(8,128)(2,1)S(1)} %bitcast.35, ...), custom_call_target="tpu_custom_call", output_to_operand_aliasing={{0}: (8, {}), {1}: (9, {}), {2}: (10, {})} | custom-call | flops 2147483648 | bytes 10080000 | tf_op jit(solution)/shard_map/pallas_call | solution.py:163
  76.0 4.9 %shard_map.67 = (f32[8,256,128]{2,1,0:T(8,128)S(1)}, f32[8,256,128]{2,1,0:T(8,128)S(1)}, f32[8,256,256]{2,1,0:T(8,128)S(1)}) custom-call(s32[4,4]{1,0:T(4,128)S(1)} %copy.32.refs_0_, s32[1]{0:T(128)} %bitcast.17.refs_1_, bf16[2048,256]{1,0:T(8,128)(2,1)S(1)} %bitcast.36, ...), custom_call_target="tpu_custom_call", output_to_operand_aliasing={{0}: (8, {}), {1}: (9, {}), {2}: (10, {})} | custom-call | flops 2147483648 | bytes 10080000 | tf_op jit(solution)/shard_map/pallas_call | solution.py:163
  81.0 5.8 %shard_map.68 = (bf16[128,2048]{1,0:T(8,128)(2,1)S(1)}, bf16[128,2048]{1,0:T(8,128)(2,1)S(1)}) custom-call(s32[5,4]{1,0:T(8,128)S(1)} %copy.33.refs_0_, s32[1]{0:T(128)} %bitcast.17.refs_1_, bf16[2048,256]{1,0:T(8,128)(2,1)S(1)} %bitcast.37, f32[256,128]{1,0:T(8,128)S(1)} %broadcast_in_dim.56.refs_3_, bf16[528,256]{1,0:T(8,128)(2,1)S(1)} %collective-permute-done.5.refs_4_, ...), custom_call_target="tpu_custom_call" | custom-call | flops 2684354560 | bytes 10350000 | tf_op jit(solution)/shard_map/pallas_call | solution.py:163
  86.8 2.1 %collective-permute-start.19 = (bf16[128,2048]{1,0:T(8,128)(2,1)S(1)}, bf16[128,2048]{1,0:T(8,128)(2,1)S(1)}, u32[]{:S(2)}, u32[]{:S(2)}) collective-permute-start(bf16[128,2048]{1,0:T(8,128)(2,1)S(1)} %get-tuple-element.32), channel_id=1, source_target_pairs={{0,1},{1,0},{2,3},{3,2},{4,5},{5,4},{6,7},{7,6},{8,9},{9,8},{10,11... | collective-permute-start | bytes 1572872 | tf_op jit(solution)/shard_map/ppermute | solution.py:185
  88.9 1.5 %collective-permute-done.19 = bf16[128,2048]{1,0:T(8,128)(2,1)S(1)} collective-permute-done((bf16[128,2048]{1,0:T(8,128)(2,1)S(1)}, bf16[128,2048]{1,0:T(8,128)(2,1)S(1)}, u32[]{:S(2)}, u32[]{:S(2)}) %collective-permute-start.19) | collective-permute-done | bytes 524320 | tf_op jit(solution)/shard_map/ppermute | solution.py:185
  90.4 1.2 %maximum_select_fusion = bf16[128,4096]{1,0:T(8,128)(2,1)} fusion(bf16[128,2048]{1,0:T(8,128)(2,1)S(1)} %collective-permute-done.19, bf16[128,2048]{1,0:T(8,128)(2,1)S(1)} %get-tuple-element.31, pred[]{:T(512)S(6)} %eq.21), kind=kLoop, calls=%fused_computation.2 | loop fusion | flops 4718592 | bytes 2097153 | tf_op jit(solution)/shard_map/jit(_where)/select_n | solution.py:275
  (50 shorter events, 0.2 us)
Async XLA Ops:
  0.0 3.1 %copy-start.3 = (s32[1,64]{1,0:T(1,128)S(1)}, s32[1,64]{1,0:T(1,128)}, u32[]{:S(2)}) copy-start(s32[1,64]{1,0:T(1,128)} %param.11) | copy-start | bytes 772
  0.0 3.1 %copy-start.4 = (s32[128]{0:T(128)S(1)}, s32[128]{0:T(128)}, u32[]{:S(2)}) copy-start(s32[128]{0:T(128)} %param.10) | copy-start | bytes 1540
  0.0 3.2 %copy-start.1 = (bf16[128,512]{1,0:T(8,128)(2,1)S(1)}, bf16[128,512]{1,0:T(8,128)(2,1)}, u32[]{:S(2)}) copy-start(bf16[128,512]{1,0:T(8,128)(2,1)} %param.7) | copy-start | bytes 393220
  0.0 3.2 %copy-start.2 = (bf16[128,512]{1,0:T(8,128)(2,1)S(1)}, bf16[128,512]{1,0:T(8,128)(2,1)}, u32[]{:S(2)}) copy-start(bf16[128,512]{1,0:T(8,128)(2,1)} %param.8) | copy-start | bytes 393220
  0.0 3.6 %copy-start = (bf16[128,4096]{1,0:T(8,128)(2,1)S(1)}, bf16[128,4096]{1,0:T(8,128)(2,1)}, u32[]{:S(2)}) copy-start(bf16[128,4096]{1,0:T(8,128)(2,1)} %refs_12_.1) | copy-start | bytes 3145732
  2.4 31.6 %collective-permute-start.1 = (bf16[128,2048]{1,0:T(8,128)(2,1)}, bf16[128,2048]{1,0:T(8,128)(2,1)}, u32[]{:S(2)}, u32[]{:S(2)}) collective-permute-start(bf16[128,2048]{1,0:T(8,128)(2,1)} %get-tuple-element.34), channel_id=1, source_target_pairs={{0,1},{1,0},{2,3},{3,2},{4,5},{5,4},{6,7},{7,6},{8,9},{9,8},{10,11... | collective-permute-start | bytes 1572872 | tf_op jit(solution)/shard_map/ppermute | solution.py:185
  3.3 1.6 %collective-permute-start = (bf16[272,256]{1,0:T(8,128)(2,1)S(1)}, bf16[272,256]{1,0:T(8,128)(2,1)S(1)}, u32[]{:S(2)}, u32[]{:S(2)}) collective-permute-start(bf16[272,256]{1,0:T(8,128)(2,1)S(1)} %pad_maximum_fusion.1), channel_id=1, source_target_pairs={{0,1},{1,0},{2,3},{3,2},{4,5},{5,4},{6,7},{7,6},{8,9},{9,8},{10,11... | collective-permute-start | bytes 417800 | tf_op jit(solution)/shard_map/ppermute | solution.py:185
  4.9 9.6 %collective-permute-start.10 = (bf16[528,256]{1,0:T(8,128)(2,1)S(1)}, bf16[528,256]{1,0:T(8,128)(2,1)S(1)}, u32[]{:S(2)}, u32[]{:S(2)}) collective-permute-start(bf16[528,256]{1,0:T(8,128)(2,1)S(1)} %slice_dynamic-update-slice_fusion.refs_4_), channel_id=1, source_target_pairs={{0,16},{1,17},{2,18},{3,19},{4,20},{5,21},{6,22},{7,23},{8,24},{9,... | collective-permute-start | bytes 811016 | tf_op jit(solution)/shard_map/ppermute | solution.py:185
  6.3 17.6 %collective-permute-start.2 = (bf16[528,256]{1,0:T(8,128)(2,1)S(1)}, bf16[528,256]{1,0:T(8,128)(2,1)S(1)}, u32[]{:S(2)}, u32[]{:S(2)}) collective-permute-start(bf16[528,256]{1,0:T(8,128)(2,1)S(1)} %slice_dynamic-update-slice_fusion.refs_4_), channel_id=1, source_target_pairs={{0,2},{1,3},{2,4},{3,5},{4,6},{5,7},{6,8},{7,9},{8,10},{9,11},{10,... | collective-permute-start | bytes 811016 | tf_op jit(solution)/shard_map/ppermute | solution.py:185
  9.9 16.0 %collective-permute-start.6 = (bf16[528,256]{1,0:T(8,128)(2,1)S(1)}, bf16[528,256]{1,0:T(8,128)(2,1)S(1)}, u32[]{:S(2)}, u32[]{:S(2)}) collective-permute-start(bf16[528,256]{1,0:T(8,128)(2,1)S(1)} %slice_dynamic-update-slice_fusion.refs_4_), channel_id=1, source_target_pairs={{0,32},{1,33},{2,34},{3,35},{4,36},{5,37},{6,38},{7,39},{8,40},{9,... | collective-permute-start | bytes 811016 | tf_op jit(solution)/shard_map/ppermute | solution.py:185
  14.5 16.5 %collective-permute-start.11 = (bf16[528,256]{1,0:T(8,128)(2,1)S(1)}, bf16[528,256]{1,0:T(8,128)(2,1)S(1)}, u32[]{:S(2)}, u32[]{:S(2)}) collective-permute-start(bf16[528,256]{1,0:T(8,128)(2,1)S(1)} %collective-permute-done.10.refs_6_), channel_id=1, source_target_pairs={{16,18},{17,19},{18,20},{19,21},{20,22},{21,23},{22,24},{23,25},{2... | collective-permute-start | bytes 811016 | tf_op jit(solution)/shard_map/ppermute | solution.py:185
  18.1 18.8 %collective-permute-start.14 = (bf16[528,256]{1,0:T(8,128)(2,1)S(1)}, bf16[528,256]{1,0:T(8,128)(2,1)S(1)}, u32[]{:S(2)}, u32[]{:S(2)}) collective-permute-start(bf16[528,256]{1,0:T(8,128)(2,1)S(1)} %collective-permute-done.10.refs_6_), channel_id=1, source_target_pairs={{16,30},{17,31},{18,16},{19,17},{20,18},{21,19},{22,20},{23,21},{2... | collective-permute-start | bytes 811016 | tf_op jit(solution)/shard_map/ppermute | solution.py:185
  23.9 17.8 %collective-permute-start.3 = (bf16[528,256]{1,0:T(8,128)(2,1)S(1)}, bf16[528,256]{1,0:T(8,128)(2,1)S(1)}, u32[]{:S(2)}, u32[]{:S(2)}) collective-permute-start(bf16[528,256]{1,0:T(8,128)(2,1)S(1)} %collective-permute-done.2.refs_4_), channel_id=1, source_target_pairs={{0,2},{1,3},{2,4},{3,5},{4,6},{5,7},{6,8},{7,9},{8,10},{9,11},{10,... | collective-permute-start | bytes 811016 | tf_op jit(solution)/shard_map/ppermute | solution.py:185
  25.9 17.8 %collective-permute-start.7 = (bf16[528,256]{1,0:T(8,128)(2,1)S(1)}, bf16[528,256]{1,0:T(8,128)(2,1)S(1)}, u32[]{:S(2)}, u32[]{:S(2)}) collective-permute-start(bf16[528,256]{1,0:T(8,128)(2,1)S(1)} %collective-permute-done.6.refs_5_), channel_id=1, source_target_pairs={{0,46},{1,47},{2,0},{3,1},{4,2},{5,3},{6,4},{7,5},{8,6},{9,7},{10,... | collective-permute-start | bytes 811016 | tf_op jit(solution)/shard_map/ppermute | solution.py:185
  31.0 17.8 %collective-permute-start.12 = (bf16[528,256]{1,0:T(8,128)(2,1)S(1)}, bf16[528,256]{1,0:T(8,128)(2,1)S(1)}, u32[]{:S(2)}, u32[]{:S(2)}) collective-permute-start(bf16[528,256]{1,0:T(8,128)(2,1)S(1)} %collective-permute-done.11.refs_6_), channel_id=1, source_target_pairs={{16,18},{17,19},{18,20},{19,21},{20,22},{21,23},{22,24},{23,25},{2... | collective-permute-start | bytes 811016 | tf_op jit(solution)/shard_map/ppermute | solution.py:185
  34.0 46.9 %collective-permute-start.18 = (bf16[128,2048]{1,0:T(8,128)(2,1)}, bf16[128,2048]{1,0:T(8,128)(2,1)S(1)}, u32[]{:S(2)}, u32[]{:S(2)}) collective-permute-start(bf16[128,2048]{1,0:T(8,128)(2,1)} %constant_dynamic-slice_fusion), channel_id=1, source_target_pairs={{0,1},{1,0},{2,3},{3,2},{4,5},{5,4},{6,7},{7,6},{8,9},{9,8},{10,11... | collective-permute-start | bytes 1572872 | tf_op jit(solution)/shard_map/ppermute | solution.py:185
  36.9 20.7 %collective-permute-start.15 = (bf16[528,256]{1,0:T(8,128)(2,1)S(1)}, bf16[528,256]{1,0:T(8,128)(2,1)S(1)}, u32[]{:S(2)}, u32[]{:S(2)}) collective-permute-start(bf16[528,256]{1,0:T(8,128)(2,1)S(1)} %collective-permute-done.14.refs_7_), channel_id=1, source_target_pairs={{16,30},{17,31},{18,16},{19,17},{20,18},{21,19},{22,20},{23,21},{2... | collective-permute-start | bytes 811016 | tf_op jit(solution)/shard_map/ppermute | solution.py:185
  41.7 20.5 %collective-permute-start.4 = (bf16[528,256]{1,0:T(8,128)(2,1)S(1)}, bf16[528,256]{1,0:T(8,128)(2,1)S(1)}, u32[]{:S(2)}, u32[]{:S(2)}) collective-permute-start(bf16[528,256]{1,0:T(8,128)(2,1)S(1)} %collective-permute-done.3.refs_4_), channel_id=1, source_target_pairs={{0,2},{1,3},{2,4},{3,5},{4,6},{5,7},{6,8},{7,9},{8,10},{9,11},{10,... | collective-permute-start | bytes 811016 | tf_op jit(solution)/shard_map/ppermute | solution.py:185
  43.7 20.5 %collective-permute-start.8 = (bf16[528,256]{1,0:T(8,128)(2,1)S(1)}, bf16[528,256]{1,0:T(8,128)(2,1)S(1)}, u32[]{:S(2)}, u32[]{:S(2)}) collective-permute-start(bf16[528,256]{1,0:T(8,128)(2,1)S(1)} %collective-permute-done.7.refs_5_), channel_id=1, source_target_pairs={{0,46},{1,47},{2,0},{3,1},{4,2},{5,3},{6,4},{7,5},{8,6},{9,7},{10,... | collective-permute-start | bytes 811016 | tf_op jit(solution)/shard_map/ppermute | solution.py:185
  48.8 20.5 %collective-permute-start.13 = (bf16[528,256]{1,0:T(8,128)(2,1)S(1)}, bf16[528,256]{1,0:T(8,128)(2,1)S(1)}, u32[]{:S(2)}, u32[]{:S(2)}) collective-permute-start(bf16[528,256]{1,0:T(8,128)(2,1)S(1)} %collective-permute-done.12.refs_6_), channel_id=1, source_target_pairs={{16,18},{17,19},{18,20},{19,21},{20,22},{21,23},{22,24},{23,25},{2... | collective-permute-start | bytes 811016 | tf_op jit(solution)/shard_map/ppermute | solution.py:185
  57.6 23.3 %collective-permute-start.16 = (bf16[528,256]{1,0:T(8,128)(2,1)S(1)}, bf16[528,256]{1,0:T(8,128)(2,1)S(1)}, u32[]{:S(2)}, u32[]{:S(2)}) collective-permute-start(bf16[528,256]{1,0:T(8,128)(2,1)S(1)} %collective-permute-done.15.refs_7_), channel_id=1, source_target_pairs={{16,30},{17,31},{18,16},{19,17},{20,18},{21,19},{22,20},{23,21},{2... | collective-permute-start | bytes 811016 | tf_op jit(solution)/shard_map/ppermute | solution.py:185
  62.2 18.7 %collective-permute-start.5 = (bf16[528,256]{1,0:T(8,128)(2,1)S(1)}, bf16[528,256]{1,0:T(8,128)(2,1)S(1)}, u32[]{:S(2)}, u32[]{:S(2)}) collective-permute-start(bf16[528,256]{1,0:T(8,128)(2,1)S(1)} %collective-permute-done.4.refs_4_), channel_id=1, source_target_pairs={{0,2},{1,3},{2,4},{3,5},{4,6},{5,7},{6,8},{7,9},{8,10},{9,11},{10,... | collective-permute-start | bytes 811016 | tf_op jit(solution)/shard_map/ppermute | solution.py:185
  64.2 16.8 %collective-permute-start.9 = (bf16[528,256]{1,0:T(8,128)(2,1)S(1)}, bf16[528,256]{1,0:T(8,128)(2,1)S(1)}, u32[]{:S(2)}, u32[]{:S(2)}) collective-permute-start(bf16[528,256]{1,0:T(8,128)(2,1)S(1)} %collective-permute-done.8.refs_5_), channel_id=1, source_target_pairs={{0,46},{1,47},{2,0},{3,1},{4,2},{5,3},{6,4},{7,5},{8,6},{9,7},{10,... | collective-permute-start | bytes 811016 | tf_op jit(solution)/shard_map/ppermute | solution.py:185
  69.3 11.7 %collective-permute-start.17 = (bf16[528,256]{1,0:T(8,128)(2,1)S(1)}, bf16[528,256]{1,0:T(8,128)(2,1)S(1)}, u32[]{:S(2)}, u32[]{:S(2)}) collective-permute-start(bf16[528,256]{1,0:T(8,128)(2,1)S(1)} %collective-permute-done.13.refs_6_), channel_id=1, source_target_pairs={{16,18},{17,19},{18,20},{19,21},{20,22},{21,23},{22,24},{23,25},{2... | collective-permute-start | bytes 811016 | tf_op jit(solution)/shard_map/ppermute | solution.py:185
  86.8 3.6 %collective-permute-start.19 = (bf16[128,2048]{1,0:T(8,128)(2,1)S(1)}, bf16[128,2048]{1,0:T(8,128)(2,1)S(1)}, u32[]{:S(2)}, u32[]{:S(2)}) collective-permute-start(bf16[128,2048]{1,0:T(8,128)(2,1)S(1)} %get-tuple-element.32), channel_id=1, source_target_pairs={{0,1},{1,0},{2,3},{3,2},{4,5},{5,4},{6,7},{7,6},{8,9},{9,8},{10,11... | collective-permute-start | bytes 1572872 | tf_op jit(solution)/shard_map/ppermute | solution.py:185

commit v2 on v1

--- a/solution.py
+++ b/solution.py
@@ -22,29 +22,37 @@
 NEG = -1e30
 
 
-def permutation(target):
-    pairs = []
-    for x in range(NX):
-        for z in range(NZ):
-            for core in range(2):
-                goal = target(x, z, core)
-                if goal is not None:
-                    gx, gz, gc = goal
-                    pairs.append(((x * NZ + z) * 2 + core, (gx * NZ + gz) * 2 + gc))
-    return pairs
-
-
-SWAP = permutation(lambda x, z, c: (x, z, 1 - c))
-ONE_X = permutation(lambda x, z, c: (x + 1, z, c) if x < 3 else None)
-TWO_X = permutation(lambda x, z, c: ((x + 2) % NX, z, c))
-NEAR_UP = permutation(
-    lambda x, z, c: (x, z + 1, c) if z < 7 else ((x + 2, 0, c) if x < 2 else None)
-)
-NEAR_DOWN = permutation(
-    lambda x, z, c: (x, z - 1, c) if z > 0 else ((x + 2) % NX, 7, c)
-)
-MID_UP = permutation(lambda x, z, c: (x, (z + 1) % NZ, c) if x > 0 else None)
-MID_DOWN = permutation(lambda x, z, c: (x, (z - 1) % NZ, c) if x > 0 else None)
+def pairs_of(links):
+    return [(2 * a + c, 2 * b + c) for a, b in sorted(links) for c in range(2)]
+
+
+def chain_plan(offset, step, length):
+    count = NX * NZ
+
+    def seen_by(chip, s):
+        unit = chip + offset - step * s
+        return 0 <= unit <= chip
+
+    wanted = [set() for _ in range(length + 1)]
+    for s in range(length, -1, -1):
+        wanted[s] |= {u for u in range(count) if seen_by(u, s)}
+        if s:
+            wanted[s - 1] |= {(u - step) % count for u in wanted[s]}
+    hops = [pairs_of({((u + offset) % count, u) for u in wanted[0]})]
+    for s in range(1, length + 1):
+        hops.append(pairs_of({((u - step) % count, u) for u in wanted[s]}))
+    return hops
+
+
+def joined(*hops):
+    return sorted(set().union(*[set(h) for h in hops]))
+
+
+SWAP = [(i, i ^ 1) for i in range(2 * NX * NZ)]
+NEAR_UP = chain_plan(0, 1, 4)
+MID_UP = chain_plan(-NZ, 1, 4)
+MID_DOWN = chain_plan(-NZ, -1, 3)
+FAR_DOWN = chain_plan(-2 * NZ, -1, 3)
 
 
 def attend(own_at, last, count, *refs):
@@ -209,17 +217,16 @@
         ],
         axis=0,
     )
-    up = [unit]
-    mid0 = send(unit, ONE_X)
-    low0 = send(unit, TWO_X)
-    down = [low0]
-    mup, mdown = [mid0], [mid0]
-    for s in range(4):
-        up.append(send(up[-1], NEAR_UP))
-        mup.append(send(mup[-1], MID_UP))
-        if s < 3:
-            down.append(send(down[-1], NEAR_DOWN))
-            mdown.append(send(mdown[-1], MID_DOWN))
+    near = [unit, send(unit, NEAR_UP[1])]
+    mid = [send(unit, joined(MID_UP[0], MID_DOWN[0]))]
+    far = [send(unit, FAR_DOWN[0])]
+    back_mid = [mid[0]]
+    rings = (near, NEAR_UP), (mid, MID_UP), (back_mid, MID_DOWN), (far, FAR_DOWN)
+
+    def advance(s):
+        for chain, hops in rings:
+            if len(chain) == s and s < len(hops):
+                chain.append(send(chain[-1], hops[s]))
 
     q_other = send(take(query_rows, 1 - core, HALF), SWAP)
     gate_other = send(take(gate_rows, 1 - core, HALF), SWAP)
@@ -229,31 +236,21 @@
     qdocs = jnp.broadcast_to(meta[0][:, None], (UNIT, BLK))
     lists = jnp.stack([meta[1, :64], meta[1, BLK : BLK + 64]])
 
-    def up_id(s):
-        return jnp.where(z >= s, chip - s, jnp.where(x >= 2, chip - s - NZ, -1))
-
-    def down_id(s):
-        return jnp.where(
-            z + s < NZ, jnp.where(x >= 2, chip - 2 * NZ + s, -1), chip + s - NZ
+    steps = [
+        [(near, 0, chip)],
+        [(near, 1, chip - 1), (mid, 0, chip - 8), (far, 0, chip - 16)],
+    ]
+    for s in range(1, 4):
+        steps.append(
+            [
+                (near, s + 1, chip - s - 1),
+                (mid, s, chip - 8 - s),
+                (back_mid, s, chip - 8 + s),
+                (far, s, chip - 16 + s),
+            ]
         )
-
-    def mid_id(s):
-        return jnp.where(x >= 1, (x - 1) * NZ + lax.rem(z + s + NZ, NZ), -1)
-
-    groups = [
-        [(up[0], chip)],
-        [(up[1], up_id(1)), (down[0], down_id(0)), (mup[0], mid_id(0))],
-        [(up[2], up_id(2)), (down[1], down_id(1)), (mup[1], mid_id(-1)), (mdown[1], mid_id(1))],
-        [(up[3], up_id(3)), (down[2], down_id(2)), (mup[2], mid_id(-2)), (mdown[2], mid_id(2))],
-        [
-            (up[4], up_id(4)),
-            (down[3], down_id(3)),
-            (mup[3], mid_id(-3)),
-            (mdown[3], mid_id(3)),
-            (mup[4], mid_id(-4)),
-        ],
-    ]
-    ids = jnp.stack([i for group in groups for _, i in group])
+    steps.append([(mid, 4, chip - 12)])
+    ids = jnp.stack([i for step in steps for _, _, i in step])
     cols = 2 * ids[:, None] + jnp.stack([core, 1 - core])[None, :]
     cols = jnp.where(ids[:, None] >= 0, cols, -1)
     hot = cols[:, None, :, None] == jnp.arange(64, dtype=jnp.int32)[None, None, None, :]
@@ -263,13 +260,20 @@
     core1 = core.reshape(1)
     state = None
     at = 0
-    for n, group in enumerate(groups):
-        flags = table[at : at + len(group)]
-        at += len(group)
-        gates = (gate_rows, gate_other) if n == len(groups) - 1 else None
+    for n, step in enumerate(steps):
+        flags = table[at : at + len(step)]
+        at += len(step)
+        gates = (gate_rows, gate_other) if n == len(steps) - 1 else None
+        units = [chain[k] for chain, k, _ in step]
+        if n >= 1 and n < len(steps) - 1:
+            if len(near) == n + 1 and n + 1 < len(NEAR_UP):
+                near.append(send(near[-1], NEAR_UP[n + 1]))
+            advance(n)
         state = attend_call(
-            core1, flags, q, qdocs, [u for u, _ in group], state, gates, 0 if n == 0 else None
+            core1, flags, q, qdocs, units, state, gates, 0 if n == 0 else None
         )
+        if 1 <= n < len(steps) - 2:
+            far[-1], state = lax.optimization_barrier((far[-1], state))
     mine, other = state
     back = send(other, SWAP)
     return jnp.where(

time: 92.1 us -> 115 us (1.25)
  local copies, waits for them, and re-layouts: 4.46 us -> 14.7 us
  waiting for transfers between devices: 3.37 us -> 11.2 us
  Pallas kernels: 20.7 us -> 25.2 us
    unnamed x13 -> x43, local copies, waits for them, and re-layouts: 0.06 us -> 10.7 us
    ppermute x20, waiting for transfers between devices: 3.37 us -> 11.2 us  [send(): return lax.ppermute(value, 'cp', pairs)]
    pallas_call x5 -> x6, Pallas kernels: 20.7 us -> 25.2 us  [attend_call(): pl.pallas_call(functools.partial(attend, own_at, last, count), out_shape=...]
    select_n x1, other arithmetic: 1.21 us -> 2.47 us  [on_device(): jnp.where(core == 0, jnp.concatenate([mine, back], axis=1), jnp.concatena...]
  transfers between devices with their start and end apart: 20 -> 20, of which waited for: 3 -> 2; matrix products, arithmetic and copies ran while one was open for 4% -> 4% of each run, Pallas kernels for 16% -> 19%
where the time goes in v2:
time: 115 us; the launch traced here: 114 us
  starting transfers between devices  58.7 us (51%)
  Pallas kernels  25.2 us (22%)
  local copies, waits for them, and re-layouts  14.7 us (13%)
  waiting for transfers between devices  11.2 us (10%)
  other arithmetic  4.04 us (4%)
    ppermute x20, starting transfers between devices, send(): return lax.ppermute(value, 'cp', pairs)  58.7 us
    pallas_call x6, Pallas kernels, attend_call(): pl.pallas_call(functools.partial(attend, own_at, last, count), out_shape=...  25.2 us
    ppermute x20, waiting for transfers between devices, send(): return lax.ppermute(value, 'cp', pairs)  11.2 us
    unnamed x43, local copies, waits for them, and re-layouts  10.7 us
    select_n x1, other arithmetic, on_device(): jnp.where(core == 0, jnp.concatenate([mine, back], axis=1), jnp.concatena...  2.47 us
  transfers between devices with their start and end apart: 20, of which 2 were waited for; matrix products, arithmetic and copies ran while one was open for 4% of the time, Pallas kernels for 19%

profile of v2, /device:TPU:15, one launch (start us, length us, event | category | flops | bytes accessed | tf_op | source)
XLA Modules:
  0.0 114.4 jit_solution(2587839863045559591)
XLA Ops:
  0.0 1.4 %constant_dynamic-slice_fusion.2 = (bf16[128,2048]{1,0:T(8,128)(2,1)S(1)}, bf16[128,2048]{1,0:T(8,128)(2,1)S(1)}) fusion(bf16[128,4096]{1,0:T(8,128)(2,1)} %param.6, s32[]{:T(128)S(6)} %select_n.45, s32[]{:T(128)S(6)} %select_n.46), kind=kLoop, calls=%fused_computation.23 | loop fusion | bytes 2097160 | tf_op jit(solution)/shard_map/dynamic_slice | solution.py:196
  1.4 0.8 collective-permute-start.1
  2.3 0.1 collective-permute-start
  2.5 0.9 constant_dynamic-slice_fusion
  3.3 0.5 collective-permute-start.18
  4.2 1.3 %collective-permute-start.14 = (bf16[528,256]{1,0:T(8,128)(2,1)S(1)}, bf16[528,256]{1,0:T(8,128)(2,1)}, u32[]{:S(2)}, u32[]{:S(2)}) collective-permute-start(bf16[528,256]{1,0:T(8,128)(2,1)S(1)} %slice_dynamic-update-slice_fusion.refs_4_), channel_id=1, source_target_pairs={{0,32},{1,33},{2,34},{3,35},{4,36},{5,37},{6,38},{7,39},{8,40},{9,... | collective-permute-start | bytes 811016 | tf_op jit(solution)/shard_map/ppermute | solution.py:193
  5.5 5.5 %collective-permute-start.2 = (bf16[528,256]{1,0:T(8,128)(2,1)S(1)}, bf16[528,256]{1,0:T(8,128)(2,1)}, u32[]{:S(2)}, u32[]{:S(2)}) collective-permute-start(bf16[528,256]{1,0:T(8,128)(2,1)S(1)} %slice_dynamic-update-slice_fusion.refs_4_), channel_id=1, source_target_pairs={{0,16},{1,17},{2,18},{3,19},{4,20},{5,21},{6,22},{7,23},{8,24},{9,... | collective-permute-start | bytes 811016 | tf_op jit(solution)/shard_map/ppermute | solution.py:193
  11.0 3.5 %collective-permute-start.7 = (bf16[528,256]{1,0:T(8,128)(2,1)S(1)}, bf16[528,256]{1,0:T(8,128)(2,1)S(1)}, u32[]{:S(2)}, u32[]{:S(2)}) collective-permute-start(bf16[528,256]{1,0:T(8,128)(2,1)S(1)} %slice_dynamic-update-slice_fusion.refs_4_), channel_id=1, source_target_pairs={{0,2},{1,3},{2,4},{3,5},{4,6},{5,7},{6,8},{7,9},{8,10},{9,11},{10,... | collective-permute-start | bytes 811016 | tf_op jit(solution)/shard_map/ppermute | solution.py:193
  14.6 0.1 select_reduce_fusion
  14.8 0.6 fusion.7
  15.5 0.1 copy.31
  15.7 9.4 %collective-permute-done.2.refs_5_ = bf16[528,256]{1,0:T(8,128)(2,1)} collective-permute-done((bf16[528,256]{1,0:T(8,128)(2,1)S(1)}, bf16[528,256]{1,0:T(8,128)(2,1)}, u32[]{:S(2)}, u32[]{:S(2)}) %collective-permute-start.2) | collective-permute-done | bytes 270368 | tf_op jit(solution)/shard_map/ppermute | solution.py:193
  25.1 4.6 %collective-permute-start.11 = (bf16[528,256]{1,0:T(8,128)(2,1)}, bf16[528,256]{1,0:T(8,128)(2,1)}, u32[]{:S(2)}, u32[]{:S(2)}) collective-permute-start(bf16[528,256]{1,0:T(8,128)(2,1)} %collective-permute-done.2.refs_5_), channel_id=1, source_target_pairs={{0,62},{1,63},{2,0},{3,1},{4,2},{5,3},{16,14},{17,15},{18,16},{19,... | collective-permute-start | bytes 811016 | tf_op jit(solution)/shard_map/ppermute | solution.py:193
  29.7 1.9 %collective-permute-start.3 = (bf16[528,256]{1,0:T(8,128)(2,1)}, bf16[528,256]{1,0:T(8,128)(2,1)}, u32[]{:S(2)}, u32[]{:S(2)}) collective-permute-start(bf16[528,256]{1,0:T(8,128)(2,1)} %collective-permute-done.2.refs_5_), channel_id=1, source_target_pairs={{16,18},{17,19},{18,20},{19,21},{20,22},{21,23},{22,24},{23,25},{2... | collective-permute-start | bytes 811016 | tf_op jit(solution)/shard_map/ppermute | solution.py:193
  31.7 5.5 %collective-permute-start.15 = (bf16[528,256]{1,0:T(8,128)(2,1)}, bf16[528,256]{1,0:T(8,128)(2,1)}, u32[]{:S(2)}, u32[]{:S(2)}) collective-permute-start(bf16[528,256]{1,0:T(8,128)(2,1)} %collective-permute-done.14.refs_6_), channel_id=1, source_target_pairs={{0,62},{1,63},{2,0},{3,1},{4,2},{5,3},{32,30},{33,31},{34,32},{35,... | collective-permute-start | bytes 811016 | tf_op jit(solution)/shard_map/ppermute | solution.py:193
  37.2 1.9 %collective-permute-start.8 = (bf16[528,256]{1,0:T(8,128)(2,1)S(1)}, bf16[528,256]{1,0:T(8,128)(2,1)}, u32[]{:S(2)}, u32[]{:S(2)}) collective-permute-start(bf16[528,256]{1,0:T(8,128)(2,1)S(1)} %collective-permute-done.7.refs_4_), channel_id=1, source_target_pairs={{2,4},{3,5},{4,6},{5,7},{6,8},{7,9},{8,10},{9,11},{10,12},{11,13},... | collective-permute-start | bytes 811016 | tf_op jit(solution)/shard_map/ppermute | solution.py:193
  39.1 1.1 pad_maximum_fusion
  40.4 0.9 copy-done.12
  41.4 1.7 %shard_map.64 = (f32[8,256,128]{2,1,0:T(8,128)S(1)}, f32[8,256,128]{2,1,0:T(8,128)S(1)}, f32[8,256,256]{2,1,0:T(8,128)S(1)}) custom-call(s32[1,4]{1,0:T(1,128)S(1)} %slice.71.refs_0_, s32[1]{0:T(128)} %bitcast.17.refs_1_, bf16[2048,256]{1,0:T(8,128)(2,1)S(1)} %bitcast.33, f32[256,128]{1,0:T(8,128)S(1)} %broadcast_in_dim.56.refs_3_, ...), custom_call_target="tpu_custom_call" | custom-call | flops 536870912 | bytes 9270000 | tf_op jit(solution)/shard_map/pallas_call | solution.py:171
  43.1 1.9 %collective-permute-start.4 = (bf16[528,256]{1,0:T(8,128)(2,1)}, bf16[528,256]{1,0:T(8,128)(2,1)}, u32[]{:S(2)}, u32[]{:S(2)}) collective-permute-start(bf16[528,256]{1,0:T(8,128)(2,1)} %collective-permute-done.3.refs_5_), channel_id=1, source_target_pairs={{18,20},{19,21},{20,22},{21,23},{22,24},{23,25},{24,26},{25,27},{2... | collective-permute-start | bytes 811016 | tf_op jit(solution)/shard_map/ppermute | solution.py:193
  45.0 4.0 %shard_map.65 = (f32[8,256,128]{2,1,0:T(8,128)S(1)}, f32[8,256,128]{2,1,0:T(8,128)S(1)}, f32[8,256,256]{2,1,0:T(8,128)S(1)}) custom-call(s32[3,4]{1,0:T(4,128)S(1)} %copy.32.refs_0_, s32[1]{0:T(128)} %bitcast.17.refs_1_, bf16[2048,256]{1,0:T(8,128)(2,1)S(1)} %bitcast.34, ...), custom_call_target="tpu_custom_call", output_to_operand_aliasing={{0}: (7, {}), {1}: (8, {}), {2}: (9, {})} | custom-call | flops 1610612736 | bytes 9810000 | tf_op jit(solution)/shard_map/pallas_call | solution.py:171
  49.0 1.0 copy-done
  50.0 1.0 copy-done.4
  51.0 5.5 %collective-permute-start.16 = (bf16[528,256]{1,0:T(8,128)(2,1)}, bf16[528,256]{1,0:T(8,128)(2,1)}, u32[]{:S(2)}, u32[]{:S(2)}) collective-permute-start(bf16[528,256]{1,0:T(8,128)(2,1)} %collective-permute-done.15.refs_7_), channel_id=1, source_target_pairs={{0,62},{1,63},{2,0},{3,1},{30,28},{31,29},{32,30},{33,31},{34,32},... | collective-permute-start | bytes 811016 | tf_op jit(solution)/shard_map/ppermute | solution.py:193
  56.5 3.4 %collective-permute-start.12 = (bf16[528,256]{1,0:T(8,128)(2,1)}, bf16[528,256]{1,0:T(8,128)(2,1)}, u32[]{:S(2)}, u32[]{:S(2)}) collective-permute-start(bf16[528,256]{1,0:T(8,128)(2,1)} %collective-permute-done.11.refs_6_), channel_id=1, source_target_pairs={{0,62},{1,63},{2,0},{3,1},{14,12},{15,13},{16,14},{17,15},{18,16},... | collective-permute-start | bytes 811016 | tf_op jit(solution)/shard_map/ppermute | solution.py:193
  59.9 1.9 %collective-permute-start.9 = (bf16[528,256]{1,0:T(8,128)(2,1)}, bf16[528,256]{1,0:T(8,128)(2,1)}, u32[]{:S(2)}, u32[]{:S(2)}) collective-permute-start(bf16[528,256]{1,0:T(8,128)(2,1)} %collective-permute-done.8.refs_4_), channel_id=1, source_target_pairs={{4,6},{5,7},{6,8},{7,9},{8,10},{9,11},{10,12},{11,13},{12,14},{13,... | collective-permute-start | bytes 811016 | tf_op jit(solution)/shard_map/ppermute | solution.py:193
  61.8 0.1 copy.33
  62.0 1.9 %collective-permute-start.5 = (bf16[528,256]{1,0:T(8,128)(2,1)}, bf16[528,256]{1,0:T(8,128)(2,1)}, u32[]{:S(2)}, u32[]{:S(2)}) collective-permute-start(bf16[528,256]{1,0:T(8,128)(2,1)} %collective-permute-done.4.refs_5_), channel_id=1, source_target_pairs={{20,22},{21,23},{22,24},{23,25},{24,26},{25,27},{26,28},{27,29},{2... | collective-permute-start | bytes 811016 | tf_op jit(solution)/shard_map/ppermute | solution.py:193
  63.9 1.2 %copy-done.1 = f32[8,256,128]{2,1,0:T(8,128)S(1)} copy-done((f32[8,256,128]{2,1,0:T(8,128)S(1)}, f32[8,256,128]{2,1,0:T(8,128)}, u32[]{:S(2)}) %copy-start.1) | copy-done | bytes 1048600
  65.2 1.2 %copy-done.5 = f32[8,256,128]{2,1,0:T(8,128)S(1)} copy-done((f32[8,256,128]{2,1,0:T(8,128)S(1)}, f32[8,256,128]{2,1,0:T(8,128)}, u32[]{:S(2)}) %copy-start.5) | copy-done | bytes 1048600
  66.4 5.3 %shard_map.66 = (f32[8,256,128]{2,1,0:T(8,128)S(1)}, f32[8,256,128]{2,1,0:T(8,128)S(1)}, f32[8,256,256]{2,1,0:T(8,128)S(1)}) custom-call(s32[4,4]{1,0:T(4,128)S(1)} %copy.34.refs_0_, s32[1]{0:T(128)} %bitcast.17.refs_1_, bf16[2048,256]{1,0:T(8,128)(2,1)S(1)} %bitcast.35, ...), custom_call_target="tpu_custom_call", output_to_operand_aliasing={{0}: (8, {}), {1}: (9, {}), {2}: (10, {})} | custom-call | flops 2147483648 | bytes 10080000 | tf_op jit(solution)/shard_map/pallas_call | solution.py:171
  71.7 1.0 copy-done.2
  72.6 1.0 copy-done.6
  73.6 5.5 %collective-permute-start.17 = (bf16[528,256]{1,0:T(8,128)(2,1)}, bf16[528,256]{1,0:T(8,128)(2,1)}, u32[]{:S(2)}, u32[]{:S(2)}) collective-permute-start(bf16[528,256]{1,0:T(8,128)(2,1)} %collective-permute-done.16.refs_7_), channel_id=1, source_target_pairs={{0,62},{1,63},{28,26},{29,27},{30,28},{31,29},{32,30},{33,31},{34,... | collective-permute-start | bytes 811016 | tf_op jit(solution)/shard_map/ppermute | solution.py:193
  79.1 1.9 %collective-permute-start.10 = (bf16[528,256]{1,0:T(8,128)(2,1)}, bf16[528,256]{1,0:T(8,128)(2,1)}, u32[]{:S(2)}, u32[]{:S(2)}) collective-permute-start(bf16[528,256]{1,0:T(8,128)(2,1)} %collective-permute-done.9.refs_4_), channel_id=1, source_target_pairs={{6,8},{7,9},{8,10},{9,11},{10,12},{11,13},{12,14},{13,15},{14,16},... | collective-permute-start | bytes 811016 | tf_op jit(solution)/shard_map/ppermute | solution.py:193
  81.0 5.5 %collective-permute-start.13 = (bf16[528,256]{1,0:T(8,128)(2,1)}, bf16[528,256]{1,0:T(8,128)(2,1)}, u32[]{:S(2)}, u32[]{:S(2)}) collective-permute-start(bf16[528,256]{1,0:T(8,128)(2,1)} %collective-permute-done.12.refs_6_), channel_id=1, source_target_pairs={{0,62},{1,63},{12,10},{13,11},{14,12},{15,13},{16,14},{17,15},{18,... | collective-permute-start | bytes 811016 | tf_op jit(solution)/shard_map/ppermute | solution.py:193
  86.5 0.1 copy.35
  86.7 0.1 copy.30
  87.0 2.1 %collective-permute-start.6 = (bf16[528,256]{1,0:T(8,128)(2,1)}, bf16[528,256]{1,0:T(8,128)(2,1)S(1)}, u32[]{:S(2)}, u32[]{:S(2)}) collective-permute-start(bf16[528,256]{1,0:T(8,128)(2,1)} %collective-permute-done.5.refs_5_), channel_id=1, source_target_pairs={{22,24},{23,25},{24,26},{25,27},{26,28},{27,29},{28,30},{29,31},{3... | collective-permute-start | bytes 811016 | tf_op jit(solution)/shard_map/ppermute | solution.py:193
  89.1 1.2 %copy-done.3 = f32[8,256,128]{2,1,0:T(8,128)S(1)} copy-done((f32[8,256,128]{2,1,0:T(8,128)S(1)}, f32[8,256,128]{2,1,0:T(8,128)}, u32[]{:S(2)}) %copy-start.3) | copy-done | bytes 1048600
  90.3 1.2 %copy-done.7 = f32[8,256,128]{2,1,0:T(8,128)S(1)} copy-done((f32[8,256,128]{2,1,0:T(8,128)S(1)}, f32[8,256,128]{2,1,0:T(8,128)}, u32[]{:S(2)}) %copy-start.7) | copy-done | bytes 1048600
  91.6 5.3 %shard_map.67 = (f32[8,256,128]{2,1,0:T(8,128)S(1)}, f32[8,256,128]{2,1,0:T(8,128)S(1)}, f32[8,256,256]{2,1,0:T(8,128)S(1)}) custom-call(s32[4,4]{1,0:T(4,128)S(1)} %copy.36.refs_0_, s32[1]{0:T(128)} %bitcast.17.refs_1_, bf16[2048,256]{1,0:T(8,128)(2,1)S(1)} %bitcast.36, ...), custom_call_target="tpu_custom_call", output_to_operand_aliasing={{0}: (8, {}), {1}: (9, {}), {2}: (10, {})} | custom-call | flops 2147483648 | bytes 10080000 | tf_op jit(solution)/shard_map/pallas_call | solution.py:171
  96.9 5.4 %shard_map.68 = (f32[8,256,128]{2,1,0:T(8,128)S(1)}, f32[8,256,128]{2,1,0:T(8,128)S(1)}, f32[8,256,256]{2,1,0:T(8,128)S(1)}) custom-call(s32[4,4]{1,0:T(4,128)S(1)} %copy.37.refs_0_, s32[1]{0:T(128)} %bitcast.17.refs_1_, bf16[2048,256]{1,0:T(8,128)(2,1)S(1)} %bitcast.37, ...), custom_call_target="tpu_custom_call", output_to_operand_aliasing={{0}: (8, {}), {1}: (9, {}), {2}: (10, {})} | custom-call | flops 2147483648 | bytes 10080000 | tf_op jit(solution)/shard_map/pallas_call | solution.py:171
  102.3 3.6 %shard_map.69 = (bf16[128,2048]{1,0:T(8,128)(2,1)S(1)}, bf16[128,2048]{1,0:T(8,128)(2,1)}) custom-call(s32[1,4]{1,0:T(1,128)S(1)} %slice.62.refs_0_, s32[1]{0:T(128)} %bitcast.17.refs_1_, bf16[2048,256]{1,0:T(8,128)(2,1)S(1)} %bitcast.38, f32[256,128]{1,0:T(8,128)S(1)} %broadcast_in_dim.56.refs_3_, bf16[528,256]{1,0:T(8,128)(2,1)S(1)} %collective-permute-done.6.refs_4_, ...), custom_call_target="tpu_custom_call" | custom-call | flops 536870912 | bytes 9270000 | tf_op jit(solution)/shard_map/pallas_call | solution.py:171
  105.9 0.8 copy-done.10
  106.7 3.5 %collective-permute-start.19 = (bf16[128,2048]{1,0:T(8,128)(2,1)}, bf16[128,2048]{1,0:T(8,128)(2,1)S(1)}, u32[]{:S(2)}, u32[]{:S(2)}) collective-permute-start(bf16[128,2048]{1,0:T(8,128)(2,1)} %get-tuple-element.62), channel_id=1, source_target_pairs={{0,1},{1,0},{2,3},{3,2},{4,5},{5,4},{6,7},{7,6},{8,9},{9,8},{10,11... | collective-permute-start | bytes 1572872 | tf_op jit(solution)/shard_map/ppermute | solution.py:193
  110.2 1.7 %collective-permute-done.19 = bf16[128,2048]{1,0:T(8,128)(2,1)S(1)} collective-permute-done((bf16[128,2048]{1,0:T(8,128)(2,1)}, bf16[128,2048]{1,0:T(8,128)(2,1)S(1)}, u32[]{:S(2)}, u32[]{:S(2)}) %collective-permute-start.19) | collective-permute-done | bytes 524320 | tf_op jit(solution)/shard_map/ppermute | solution.py:193
  112.0 2.5 %maximum_select_fusion = bf16[128,4096]{1,0:T(8,128)(2,1)} fusion(bf16[128,2048]{1,0:T(8,128)(2,1)S(1)} %collective-permute-done.19, bf16[128,2048]{1,0:T(8,128)(2,1)} %copy-done.10, pred[]{:T(512)S(6)} %eq.21), kind=kLoop, calls=%fused_computation.2 | loop fusion | flops 4718592 | bytes 2097153 | tf_op jit(solution)/shard_map/jit(_where)/select_n | solution.py:279
  (81 shorter events, 1.3 us)
Async XLA Ops:
  0.0 2.2 %copy-start.18 = (s32[1,64]{1,0:T(1,128)S(1)}, s32[1,64]{1,0:T(1,128)}, u32[]{:S(2)}) copy-start(s32[1,64]{1,0:T(1,128)} %param.11) | copy-start | bytes 772
  0.0 2.2 %copy-start.19 = (s32[128]{0:T(128)S(1)}, s32[128]{0:T(128)}, u32[]{:S(2)}) copy-start(s32[128]{0:T(128)} %param.10) | copy-start | bytes 1540
  0.0 2.3 %copy-start.13 = (bf16[128,512]{1,0:T(8,128)(2,1)S(1)}, bf16[128,512]{1,0:T(8,128)(2,1)}, u32[]{:S(2)}) copy-start(bf16[128,512]{1,0:T(8,128)(2,1)} %param.7) | copy-start | bytes 393220
  0.0 2.3 %copy-start.14 = (bf16[128,512]{1,0:T(8,128)(2,1)S(1)}, bf16[128,512]{1,0:T(8,128)(2,1)}, u32[]{:S(2)}) copy-start(bf16[128,512]{1,0:T(8,128)(2,1)} %param.8) | copy-start | bytes 393220
  0.0 2.4 %copy-start.8 = (bf16[128,4096]{1,0:T(8,128)(2,1)S(1)}, bf16[128,4096]{1,0:T(8,128)(2,1)}, u32[]{:S(2)}) copy-start(bf16[128,4096]{1,0:T(8,128)(2,1)} %refs_8_.1) | copy-start | bytes 3145732
  1.4 35.7 %collective-permute-start.1 = (bf16[128,2048]{1,0:T(8,128)(2,1)S(1)}, bf16[128,2048]{1,0:T(8,128)(2,1)}, u32[]{:S(2)}, u32[]{:S(2)}) collective-permute-start(bf16[128,2048]{1,0:T(8,128)(2,1)S(1)} %get-tuple-element.64), channel_id=1, source_target_pairs={{0,1},{1,0},{2,3},{3,2},{4,5},{5,4},{6,7},{7,6},{8,9},{9,8},{10,11... | collective-permute-start | bytes 1572872 | tf_op jit(solution)/shard_map/ppermute | solution.py:193
  2.3 1.8 %collective-permute-start = (bf16[272,256]{1,0:T(8,128)(2,1)S(1)}, bf16[272,256]{1,0:T(8,128)(2,1)S(1)}, u32[]{:S(2)}, u32[]{:S(2)}) collective-permute-start(bf16[272,256]{1,0:T(8,128)(2,1)S(1)} %pad_maximum_fusion.1), channel_id=1, source_target_pairs={{0,1},{1,0},{2,3},{3,2},{4,5},{5,4},{6,7},{7,6},{8,9},{9,8},{10,11... | collective-permute-start | bytes 417800 | tf_op jit(solution)/shard_map/ppermute | solution.py:193
  3.3 98.9 %collective-permute-start.18 = (bf16[128,2048]{1,0:T(8,128)(2,1)}, bf16[128,2048]{1,0:T(8,128)(2,1)}, u32[]{:S(2)}, u32[]{:S(2)}) collective-permute-start(bf16[128,2048]{1,0:T(8,128)(2,1)} %constant_dynamic-slice_fusion), channel_id=1, source_target_pairs={{0,1},{1,0},{2,3},{3,2},{4,5},{5,4},{6,7},{7,6},{8,9},{9,8},{10,11... | collective-permute-start | bytes 1572872 | tf_op jit(solution)/shard_map/ppermute | solution.py:193
  4.2 36.1 %copy-start.11 = (bf16[528,256]{1,0:T(8,128)(2,1)}, bf16[528,256]{1,0:T(8,128)(2,1)S(1)}, u32[]{:S(2)}) copy-start(bf16[528,256]{1,0:T(8,128)(2,1)S(1)} %slice_dynamic-update-slice_fusion.refs_4_) | copy-start | bytes 811012
  4.2 25.5 %collective-permute-start.14 = (bf16[528,256]{1,0:T(8,128)(2,1)S(1)}, bf16[528,256]{1,0:T(8,128)(2,1)}, u32[]{:S(2)}, u32[]{:S(2)}) collective-permute-start(bf16[528,256]{1,0:T(8,128)(2,1)S(1)} %slice_dynamic-update-slice_fusion.refs_4_), channel_id=1, source_target_pairs={{0,32},{1,33},{2,34},{3,35},{4,36},{5,37},{6,38},{7,39},{8,40},{9,... | collective-permute-start | bytes 811016 | tf_op jit(solution)/shard_map/ppermute | solution.py:193
  5.5 19.5 %collective-permute-start.2 = (bf16[528,256]{1,0:T(8,128)(2,1)S(1)}, bf16[528,256]{1,0:T(8,128)(2,1)}, u32[]{:S(2)}, u32[]{:S(2)}) collective-permute-start(bf16[528,256]{1,0:T(8,128)(2,1)S(1)} %slice_dynamic-update-slice_fusion.refs_4_), channel_id=1, source_target_pairs={{0,16},{1,17},{2,18},{3,19},{4,20},{5,21},{6,22},{7,23},{8,24},{9,... | collective-permute-start | bytes 811016 | tf_op jit(solution)/shard_map/ppermute | solution.py:193
  11.0 20.7 %collective-permute-start.7 = (bf16[528,256]{1,0:T(8,128)(2,1)S(1)}, bf16[528,256]{1,0:T(8,128)(2,1)S(1)}, u32[]{:S(2)}, u32[]{:S(2)}) collective-permute-start(bf16[528,256]{1,0:T(8,128)(2,1)S(1)} %slice_dynamic-update-slice_fusion.refs_4_), channel_id=1, source_target_pairs={{0,2},{1,3},{2,4},{3,5},{4,6},{5,7},{6,8},{7,9},{8,10},{9,11},{10,... | collective-permute-start | bytes 811016 | tf_op jit(solution)/shard_map/ppermute | solution.py:193
  14.8 25.5 %copy-start.15 = (s32[17,2,2]{2,1,0:T(2,128)}, s32[17,2,2]{2,1,0:T(2,128)S(1)}, u32[]{:S(2)}) copy-start(s32[17,2,2]{2,1,0:T(2,128)S(1)} %convert_element_type.17) | copy-start | bytes 820
  25.1 31.4 %collective-permute-start.11 = (bf16[528,256]{1,0:T(8,128)(2,1)}, bf16[528,256]{1,0:T(8,128)(2,1)}, u32[]{:S(2)}, u32[]{:S(2)}) collective-permute-start(bf16[528,256]{1,0:T(8,128)(2,1)} %collective-permute-done.2.refs_5_), channel_id=1, source_target_pairs={{0,62},{1,63},{2,0},{3,1},{4,2},{5,3},{16,14},{17,15},{18,16},{19,... | collective-permute-start | bytes 811016 | tf_op jit(solution)/shard_map/ppermute | solution.py:193
  29.7 13.3 %collective-permute-start.3 = (bf16[528,256]{1,0:T(8,128)(2,1)}, bf16[528,256]{1,0:T(8,128)(2,1)}, u32[]{:S(2)}, u32[]{:S(2)}) collective-permute-start(bf16[528,256]{1,0:T(8,128)(2,1)} %collective-permute-done.2.refs_5_), channel_id=1, source_target_pairs={{16,18},{17,19},{18,20},{19,21},{20,22},{21,23},{22,24},{23,25},{2... | collective-permute-start | bytes 811016 | tf_op jit(solution)/shard_map/ppermute | solution.py:193
  31.7 19.3 %collective-permute-start.15 = (bf16[528,256]{1,0:T(8,128)(2,1)}, bf16[528,256]{1,0:T(8,128)(2,1)}, u32[]{:S(2)}, u32[]{:S(2)}) collective-permute-start(bf16[528,256]{1,0:T(8,128)(2,1)} %collective-permute-done.14.refs_6_), channel_id=1, source_target_pairs={{0,62},{1,63},{2,0},{3,1},{4,2},{5,3},{32,30},{33,31},{34,32},{35,... | collective-permute-start | bytes 811016 | tf_op jit(solution)/shard_map/ppermute | solution.py:193
  37.2 22.7 %collective-permute-start.8 = (bf16[528,256]{1,0:T(8,128)(2,1)S(1)}, bf16[528,256]{1,0:T(8,128)(2,1)}, u32[]{:S(2)}, u32[]{:S(2)}) collective-permute-start(bf16[528,256]{1,0:T(8,128)(2,1)S(1)} %collective-permute-done.7.refs_4_), channel_id=1, source_target_pairs={{2,4},{3,5},{4,6},{5,7},{6,8},{7,9},{8,10},{9,11},{10,12},{11,13},... | collective-permute-start | bytes 811016 | tf_op jit(solution)/shard_map/ppermute | solution.py:193
  40.4 1.0 copy-start.12
  43.1 18.9 %collective-permute-start.4 = (bf16[528,256]{1,0:T(8,128)(2,1)}, bf16[528,256]{1,0:T(8,128)(2,1)}, u32[]{:S(2)}, u32[]{:S(2)}) collective-permute-start(bf16[528,256]{1,0:T(8,128)(2,1)} %collective-permute-done.3.refs_5_), channel_id=1, source_target_pairs={{18,20},{19,21},{20,22},{21,23},{22,24},{23,25},{24,26},{25,27},{2... | collective-permute-start | bytes 811016 | tf_op jit(solution)/shard_map/ppermute | solution.py:193
  45.0 16.8 %copy-start.16 = (s32[17,2,2]{2,1,0:T(2,128)S(1)}, s32[17,2,2]{2,1,0:T(2,128)}, u32[]{:S(2)}) copy-start(s32[17,2,2]{2,1,0:T(2,128)} %copy-done.15) | copy-start | bytes 820
  49.0 1.0 copy-start
  50.0 1.0 copy-start.4
  51.0 22.6 %collective-permute-start.16 = (bf16[528,256]{1,0:T(8,128)(2,1)}, bf16[528,256]{1,0:T(8,128)(2,1)}, u32[]{:S(2)}, u32[]{:S(2)}) collective-permute-start(bf16[528,256]{1,0:T(8,128)(2,1)} %collective-permute-done.15.refs_7_), channel_id=1, source_target_pairs={{0,62},{1,63},{2,0},{3,1},{30,28},{31,29},{32,30},{33,31},{34,32},... | collective-permute-start | bytes 811016 | tf_op jit(solution)/shard_map/ppermute | solution.py:193
  56.5 24.6 %collective-permute-start.12 = (bf16[528,256]{1,0:T(8,128)(2,1)}, bf16[528,256]{1,0:T(8,128)(2,1)}, u32[]{:S(2)}, u32[]{:S(2)}) collective-permute-start(bf16[528,256]{1,0:T(8,128)(2,1)} %collective-permute-done.11.refs_6_), channel_id=1, source_target_pairs={{0,62},{1,63},{2,0},{3,1},{14,12},{15,13},{16,14},{17,15},{18,16},... | collective-permute-start | bytes 811016 | tf_op jit(solution)/shard_map/ppermute | solution.py:193
  59.9 19.2 %collective-permute-start.9 = (bf16[528,256]{1,0:T(8,128)(2,1)}, bf16[528,256]{1,0:T(8,128)(2,1)}, u32[]{:S(2)}, u32[]{:S(2)}) collective-permute-start(bf16[528,256]{1,0:T(8,128)(2,1)} %collective-permute-done.8.refs_4_), channel_id=1, source_target_pairs={{4,6},{5,7},{6,8},{7,9},{8,10},{9,11},{10,12},{11,13},{12,14},{13,... | collective-permute-start | bytes 811016 | tf_op jit(solution)/shard_map/ppermute | solution.py:193
  61.9 25.0 %copy-start.17 = (s32[1,2,2]{2,1,0:T(2,128)S(1)}, s32[1,2,2]{2,1,0:T(2,128)}, u32[]{:S(2)}) copy-start(s32[1,2,2]{2,1,0:T(2,128)} %get-tuple-element.71) | copy-start | bytes 52
  62.0 25.0 %collective-permute-start.5 = (bf16[528,256]{1,0:T(8,128)(2,1)}, bf16[528,256]{1,0:T(8,128)(2,1)}, u32[]{:S(2)}, u32[]{:S(2)}) collective-permute-start(bf16[528,256]{1,0:T(8,128)(2,1)} %collective-permute-done.4.refs_5_), channel_id=1, source_target_pairs={{20,22},{21,23},{22,24},{23,25},{24,26},{25,27},{26,28},{27,29},{2... | collective-permute-start | bytes 811016 | tf_op jit(solution)/shard_map/ppermute | solution.py:193
  63.9 1.2 %copy-start.1 = (f32[8,256,128]{2,1,0:T(8,128)S(1)}, f32[8,256,128]{2,1,0:T(8,128)}, u32[]{:S(2)}) copy-start(f32[8,256,128]{2,1,0:T(8,128)} %copy-done) | copy-start | bytes 3145732
  65.2 1.2 %copy-start.5 = (f32[8,256,128]{2,1,0:T(8,128)S(1)}, f32[8,256,128]{2,1,0:T(8,128)}, u32[]{:S(2)}) copy-start(f32[8,256,128]{2,1,0:T(8,128)} %copy-done.4) | copy-start | bytes 3145732
  71.7 1.0 copy-start.2
  72.6 1.0 copy-start.6
  73.6 23.2 %collective-permute-start.17 = (bf16[528,256]{1,0:T(8,128)(2,1)}, bf16[528,256]{1,0:T(8,128)(2,1)}, u32[]{:S(2)}, u32[]{:S(2)}) collective-permute-start(bf16[528,256]{1,0:T(8,128)(2,1)} %collective-permute-done.16.refs_7_), channel_id=1, source_target_pairs={{0,62},{1,63},{28,26},{29,27},{30,28},{31,29},{32,30},{33,31},{34,... | collective-permute-start | bytes 811016 | tf_op jit(solution)/shard_map/ppermute | solution.py:193
  79.1 17.7 %collective-permute-start.10 = (bf16[528,256]{1,0:T(8,128)(2,1)}, bf16[528,256]{1,0:T(8,128)(2,1)}, u32[]{:S(2)}, u32[]{:S(2)}) collective-permute-start(bf16[528,256]{1,0:T(8,128)(2,1)} %collective-permute-done.9.refs_4_), channel_id=1, source_target_pairs={{6,8},{7,9},{8,10},{9,11},{10,12},{11,13},{12,14},{13,15},{14,16},... | collective-permute-start | bytes 811016 | tf_op jit(solution)/shard_map/ppermute | solution.py:193
  81.0 15.8 %collective-permute-start.13 = (bf16[528,256]{1,0:T(8,128)(2,1)}, bf16[528,256]{1,0:T(8,128)(2,1)}, u32[]{:S(2)}, u32[]{:S(2)}) collective-permute-start(bf16[528,256]{1,0:T(8,128)(2,1)} %collective-permute-done.12.refs_6_), channel_id=1, source_target_pairs={{0,62},{1,63},{12,10},{13,11},{14,12},{15,13},{16,14},{17,15},{18,... | collective-permute-start | bytes 811016 | tf_op jit(solution)/shard_map/ppermute | solution.py:193
  87.0 15.2 %collective-permute-start.6 = (bf16[528,256]{1,0:T(8,128)(2,1)}, bf16[528,256]{1,0:T(8,128)(2,1)S(1)}, u32[]{:S(2)}, u32[]{:S(2)}) collective-permute-start(bf16[528,256]{1,0:T(8,128)(2,1)} %collective-permute-done.5.refs_5_), channel_id=1, source_target_pairs={{22,24},{23,25},{24,26},{25,27},{26,28},{27,29},{28,30},{29,31},{3... | collective-permute-start | bytes 811016 | tf_op jit(solution)/shard_map/ppermute | solution.py:193
  89.1 1.2 %copy-start.3 = (f32[8,256,128]{2,1,0:T(8,128)S(1)}, f32[8,256,128]{2,1,0:T(8,128)}, u32[]{:S(2)}) copy-start(f32[8,256,128]{2,1,0:T(8,128)} %copy-done.2) | copy-start | bytes 3145732
  90.3 1.2 %copy-start.7 = (f32[8,256,128]{2,1,0:T(8,128)S(1)}, f32[8,256,128]{2,1,0:T(8,128)}, u32[]{:S(2)}) copy-start(f32[8,256,128]{2,1,0:T(8,128)} %copy-done.6) | copy-start | bytes 3145732
  96.8 5.4 %copy-start.9 = (bf16[128,4096]{1,0:T(8,128)(2,1)S(1)}, bf16[128,4096]{1,0:T(8,128)(2,1)}, u32[]{:S(2)}) copy-start(bf16[128,4096]{1,0:T(8,128)(2,1)} %refs_8_.1) | copy-start | bytes 3145732
  105.9 0.8 copy-start.10
  106.7 5.3 %collective-permute-start.19 = (bf16[128,2048]{1,0:T(8,128)(2,1)}, bf16[128,2048]{1,0:T(8,128)(2,1)S(1)}, u32[]{:S(2)}, u32[]{:S(2)}) collective-permute-start(bf16[128,2048]{1,0:T(8,128)(2,1)} %get-tuple-element.62), channel_id=1, source_target_pairs={{0,1},{1,0},{2,3},{3,2},{4,5},{5,4},{6,7},{7,6},{8,9},{9,8},{10,11... | collective-permute-start | bytes 1572872 | tf_op jit(solution)/shard_map/ppermute | solution.py:193

commit v3 on v2

--- a/solution.py
+++ b/solution.py
@@ -23,36 +23,53 @@
 
 
 def pairs_of(links):
-    return [(2 * a + c, 2 * b + c) for a, b in sorted(links) for c in range(2)]
-
-
-def chain_plan(offset, step, length):
-    count = NX * NZ
-
-    def seen_by(chip, s):
-        unit = chip + offset - step * s
-        return 0 <= unit <= chip
-
+    return [
+        ((ax * NZ + az) * 2 + c, (bx * NZ + bz) * 2 + c)
+        for (ax, az), (bx, bz) in sorted(links)
+        for c in range(2)
+    ]
+
+
+CHIPS = [(x, z) for x in range(NX) for z in range(NZ)]
+
+
+def chain_plan(seed, source, visible, length):
     wanted = [set() for _ in range(length + 1)]
     for s in range(length, -1, -1):
-        wanted[s] |= {u for u in range(count) if seen_by(u, s)}
+        wanted[s] |= {chip for chip in CHIPS if visible(*chip, s)}
         if s:
-            wanted[s - 1] |= {(u - step) % count for u in wanted[s]}
-    hops = [pairs_of({((u + offset) % count, u) for u in wanted[0]})]
-    for s in range(1, length + 1):
-        hops.append(pairs_of({((u - step) % count, u) for u in wanted[s]}))
-    return hops
-
-
-def joined(*hops):
-    return sorted(set().union(*[set(h) for h in hops]))
+            wanted[s - 1] |= {source(*chip) for chip in wanted[s]}
+    hops = [
+        pairs_of({(source(*chip), chip) for chip in wanted[s]})
+        for s in range(1, length + 1)
+    ]
+    first, need = [], wanted[0]
+    for back in seed:
+        first.append(pairs_of({(back(*chip), chip) for chip in need}))
+        need = {back(*chip) for chip in need}
+    return first[::-1], hops
 
 
 SWAP = [(i, i ^ 1) for i in range(2 * NX * NZ)]
-NEAR_UP = chain_plan(0, 1, 4)
-MID_UP = chain_plan(-NZ, 1, 4)
-MID_DOWN = chain_plan(-NZ, -1, 3)
-FAR_DOWN = chain_plan(-2 * NZ, -1, 3)
+NEAR = chain_plan(
+    [],
+    lambda x, z: (x, z - 1) if z else ((x - 2) % NX, NZ - 1),
+    lambda x, z, s: z >= s or x >= 2,
+    4,
+)[1]
+FAR_SEED, FAR = chain_plan(
+    [lambda x, z: ((x + 1) % NX, z)] * 2,
+    lambda x, z: (x, z + 1) if z < NZ - 1 else ((x + 2) % NX, 0),
+    lambda x, z, s: z + s >= NZ or x >= 2,
+    3,
+)
+MID_SEED, MID_UP = chain_plan(
+    [lambda x, z: (x - 1, z)],
+    lambda x, z: (x, (z - 1) % NZ),
+    lambda x, z, s: x >= 1,
+    3,
+)
+MID_DOWN = chain_plan([], lambda x, z: (x, (z + 1) % NZ), lambda x, z, s: x >= 1, 4)[1]
 
 
 def attend(own_at, last, count, *refs):
@@ -61,15 +78,17 @@
     rest = list(refs[4 + count :])
     first = own_at is not None
     if not first:
-        m_in, l_in, acc_in = rest[:3]
-        rest = rest[3:]
+        stats_in, acc_in = rest[:2]
+        rest = rest[2:]
     if last:
         gate_mine, gate_other = rest[:2]
         rest = rest[2:]
         out_mine, out_other = rest[:2]
     else:
-        m_out, l_out, acc_out = rest[:3]
-        rest = rest[3:]
+        stats_out, acc_out = rest[:2]
+        rest = rest[2:]
+        spot = lax.broadcasted_iota(jnp.int32, (UNIT, BLK), 1)
+        stats = jnp.zeros((UNIT, BLK), jnp.float32)
     me = core[0]
     lane = lax.broadcasted_iota(jnp.int32, (1, UNIT), 1)
     biases = []
@@ -106,17 +125,14 @@
         for s in scores[1:]:
             top = jnp.maximum(top, s)
         top = jnp.max(top, axis=1, keepdims=True)
-        if first:
-            m_new = jnp.broadcast_to(top, (UNIT, BLK))
-        else:
-            m_old = m_in[h]
-            m_new = jnp.maximum(m_old, top)
-            alpha = jnp.exp2(m_old - m_new)
-        m_wide = jnp.concatenate([m_new, m_new], axis=1)
+        if not first:
+            m_old = stats_in[:, h : h + 1]
+            top = jnp.maximum(m_old, top)
+            alpha = jnp.exp2(m_old - top)
         total = None
         product = None
         for j in range(count):
-            p = jnp.exp2(scores[j] - m_wide)
+            p = jnp.exp2(scores[j] - top)
             part = p[:, :BLK] + p[:, BLK:]
             total = part if total is None else total + part
             pv = jnp.dot(
@@ -125,12 +141,12 @@
                 preferred_element_type=jnp.float32,
             )
             product = pv if product is None else product + pv
+        total = jnp.sum(total, axis=1, keepdims=True)
         if not first:
-            total = total + alpha * l_in[h]
-            wide = jnp.concatenate([alpha, alpha], axis=1)
-            product = product + wide * acc_in[h]
+            total = total + alpha * stats_in[:, GROUPS + h : GROUPS + h + 1]
+            product = product + alpha * acc_in[h]
         if last:
-            inv = 1.0 / jnp.sum(total, axis=1, keepdims=True)
+            inv = 1.0 / total
             att = product * inv
             base = pl.multiple_of(me * HALF + h * HD, HD)
             g = gate_mine[:, pl.ds(base, HD)].astype(jnp.float32)
@@ -142,9 +158,11 @@
                 att[BLK:] * jax.nn.sigmoid(g)
             ).astype(jnp.bfloat16)
         else:
-            m_out[h] = m_new
-            l_out[h] = total
+            stats = jnp.where(spot == h, top, stats)
+            stats = jnp.where(spot == GROUPS + h, total, stats)
             acc_out[h] = product
+    if not last:
+        stats_out[...] = stats
 
 
 def attend_call(core, flags, q, qdocs, units, state=None, gates=None, own_at=None):
@@ -156,15 +174,14 @@
     aliases = {}
     if state is not None:
         if not last:
-            aliases = {len(args) + i: i for i in range(3)}
+            aliases = {len(args) + i: i for i in range(2)}
         args += list(state)
     if last:
         args += list(gates)
         shapes = [jax.ShapeDtypeStruct((BLK, HALF), jnp.bfloat16)] * 2
     else:
         shapes = [
-            jax.ShapeDtypeStruct((GROUPS, UNIT, BLK), jnp.float32),
-            jax.ShapeDtypeStruct((GROUPS, UNIT, BLK), jnp.float32),
+            jax.ShapeDtypeStruct((UNIT, BLK), jnp.float32),
             jax.ShapeDtypeStruct((GROUPS, UNIT, HD), jnp.float32),
         ]
     specs = [smem, smem] + [vmem] * (len(args) - 2)
@@ -174,7 +191,7 @@
         in_specs=specs,
         out_specs=[vmem] * len(shapes),
         input_output_aliases=aliases,
-        compiler_params=pltpu.CompilerParams(vmem_limit_bytes=32 << 20),
+        compiler_params=pltpu.CompilerParams(vmem_limit_bytes=16 << 20),
         cost_estimate=pl.CostEstimate(
             flops=4 * ROWS * UNIT * HD * count,
             bytes_accessed=count * 270000 + 9000000,
@@ -217,16 +234,12 @@
         ],
         axis=0,
     )
-    near = [unit, send(unit, NEAR_UP[1])]
-    mid = [send(unit, joined(MID_UP[0], MID_DOWN[0]))]
-    far = [send(unit, FAR_DOWN[0])]
+    near, mid, far = [unit], [send(unit, MID_SEED[0])], []
+    near.append(send(unit, NEAR[0]))
+    relay = send(unit, FAR_SEED[0])
+    far.append(send(relay, FAR_SEED[1]))
     back_mid = [mid[0]]
-    rings = (near, NEAR_UP), (mid, MID_UP), (back_mid, MID_DOWN), (far, FAR_DOWN)
-
-    def advance(s):
-        for chain, hops in rings:
-            if len(chain) == s and s < len(hops):
-                chain.append(send(chain[-1], hops[s]))
+    rings = (near, NEAR), (mid, MID_UP), (back_mid, MID_DOWN), (far, FAR)
 
     q_other = send(take(query_rows, 1 - core, HALF), SWAP)
     gate_other = send(take(gate_rows, 1 - core, HALF), SWAP)
@@ -236,20 +249,25 @@
     qdocs = jnp.broadcast_to(meta[0][:, None], (UNIT, BLK))
     lists = jnp.stack([meta[1, :64], meta[1, BLK : BLK + 64]])
 
+    def near_id(s):
+        return jnp.where(z >= s, chip - s, jnp.where(x >= 2, chip - s - NZ, -1))
+
+    def far_id(s):
+        return jnp.where(
+            z + s < NZ, jnp.where(x >= 2, chip - 2 * NZ + s, -1), chip + s - NZ
+        )
+
+    def mid_id(s):
+        return jnp.where(x >= 1, (x - 1) * NZ + lax.rem(z + s + NZ, NZ), -1)
+
     steps = [
         [(near, 0, chip)],
-        [(near, 1, chip - 1), (mid, 0, chip - 8), (far, 0, chip - 16)],
+        [(near, 1, near_id(1)), (mid, 0, mid_id(0))],
+        [(near, 2, near_id(2)), (mid, 1, mid_id(-1)), (back_mid, 1, mid_id(1)), (far, 0, far_id(0))],
+        [(near, 3, near_id(3)), (mid, 2, mid_id(-2)), (back_mid, 2, mid_id(2)), (far, 1, far_id(1))],
+        [(near, 4, near_id(4)), (mid, 3, mid_id(-3)), (back_mid, 3, mid_id(3)), (far, 2, far_id(2))],
+        [(back_mid, 4, mid_id(4)), (far, 3, far_id(3))],
     ]
-    for s in range(1, 4):
-        steps.append(
-            [
-                (near, s + 1, chip - s - 1),
-                (mid, s, chip - 8 - s),
-                (back_mid, s, chip - 8 + s),
-                (far, s, chip - 16 + s),
-            ]
-        )
-    steps.append([(mid, 4, chip - 12)])
     ids = jnp.stack([i for step in steps for _, _, i in step])
     cols = 2 * ids[:, None] + jnp.stack([core, 1 - core])[None, :]
     cols = jnp.where(ids[:, None] >= 0, cols, -1)
@@ -264,16 +282,16 @@
         flags = table[at : at + len(step)]
         at += len(step)
         gates = (gate_rows, gate_other) if n == len(steps) - 1 else None
+        for chain, hops in rings:
+            due = n - 1 if chain is far else n + 1 if chain is near else n
+            if len(chain) == due and due <= len(hops):
+                chain.append(send(chain[-1], hops[due - 1]))
         units = [chain[k] for chain, k, _ in step]
-        if n >= 1 and n < len(steps) - 1:
-            if len(near) == n + 1 and n + 1 < len(NEAR_UP):
-                near.append(send(near[-1], NEAR_UP[n + 1]))
-            advance(n)
         state = attend_call(
             core1, flags, q, qdocs, units, state, gates, 0 if n == 0 else None
         )
         if 1 <= n < len(steps) - 2:
-            far[-1], state = lax.optimization_barrier((far[-1], state))
+            back_mid[-1], state = lax.optimization_barrier((back_mid[-1], state))
     mine, other = state
     back = send(other, SWAP)
     return jnp.where(

time: 115 us -> 117 us (1.017)
  waiting for transfers between devices: 11.2 us -> 5.04 us
  Pallas kernels: 25.2 us -> 30.9 us
  starting transfers between devices: 58.7 us -> 63 us
  other arithmetic: 4.04 us -> 1.74 us
    ppermute x20 -> x21, waiting for transfers between devices: 11.2 us -> 5.04 us  [send(): return lax.ppermute(value, 'cp', pairs)]
    pallas_call x6, Pallas kernels: 25.2 us -> 30.9 us  [attend_call(): pl.pallas_call(functools.partial(attend, own_at, last, count), out_shape=...]
    ppermute x20 -> x21, starting transfers between devices: 58.7 us -> 63 us  [send(): return lax.ppermute(value, 'cp', pairs)]
    unnamed x43 -> x33, local copies, waits for them, and re-layouts: 10.7 us -> 12.1 us
    select_n x1, other arithmetic: 2.47 us -> 1.21 us  [on_device(): jnp.where(core == 0, jnp.concatenate([mine, back], axis=1), jnp.concatena...]
  transfers between devices with their start and end apart: 20 -> 21, of which waited for: 2 -> 5; matrix products, arithmetic and copies ran while one was open for 4% -> 2% of each run, Pallas kernels for 19% -> 22%
where the time goes in v3:
time: 117 us
  starting transfers between devices  63 us (54%)
  Pallas kernels  30.9 us (26%)
  local copies, waits for them, and re-layouts  15.4 us (13%)
  waiting for transfers between devices  5.04 us (4%)
  other arithmetic  1.74 us (1%)
    ppermute x21, starting transfers between devices, send(): return lax.ppermute(value, 'cp', pairs)  63 us
    pallas_call x6, Pallas kernels, attend_call(): pl.pallas_call(functools.partial(attend, own_at, last, count), out_shape=...  30.9 us
    unnamed x33, local copies, waits for them, and re-layouts  12.1 us
    ppermute x21, waiting for transfers between devices, send(): return lax.ppermute(value, 'cp', pairs)  5.04 us
  transfers between devices with their start and end apart: 21, of which 5 were waited for; matrix products, arithmetic and copies ran while one was open for 2% of the time, Pallas kernels for 22%

profile of v3, /device:TPU:15, one launch (start us, length us, event | category | flops | bytes accessed | tf_op | source)
XLA Modules:
  0.0 116.6 jit_solution(10263756800510711132)
XLA Ops:
  0.0 1.3 %constant_dynamic-slice_fusion.2 = (bf16[128,2048]{1,0:T(8,128)(2,1)S(1)}, bf16[128,2048]{1,0:T(8,128)(2,1)S(1)}) fusion(bf16[128,4096]{1,0:T(8,128)(2,1)} %param.6, s32[]{:T(128)S(6)} %select_n.146, s32[]{:T(128)S(6)} %select_n.147), kind=kLoop, calls=%fused_computation.23 | loop fusion | bytes 2097160 | tf_op jit(solution)/shard_map/dynamic_slice | solution.py:213
  1.4 0.8 collective-permute-start.1
  2.3 0.1 collective-permute-start
  2.9 1.0 collective-permute-done
  3.9 1.3 %collective-permute-start.2 = (bf16[528,256]{1,0:T(8,128)(2,1)S(1)}, bf16[528,256]{1,0:T(8,128)(2,1)S(1)}, u32[]{:S(2)}, u32[]{:S(2)}) collective-permute-start(bf16[528,256]{1,0:T(8,128)(2,1)S(1)} %slice_dynamic-update-slice_fusion.refs_4_), channel_id=1, source_target_pairs={{0,16},{1,17},{2,18},{3,19},{4,20},{5,21},{6,22},{7,23},{8,24},{9,... | collective-permute-start | bytes 811016 | tf_op jit(solution)/shard_map/ppermute | solution.py:210
  5.2 3.5 %collective-permute-start.4 = (bf16[528,256]{1,0:T(8,128)(2,1)S(1)}, bf16[528,256]{1,0:T(8,128)(2,1)}, u32[]{:S(2)}, u32[]{:S(2)}) collective-permute-start(bf16[528,256]{1,0:T(8,128)(2,1)S(1)} %slice_dynamic-update-slice_fusion.refs_4_), channel_id=1, source_target_pairs={{0,2},{1,3},{2,4},{3,5},{4,6},{5,7},{6,8},{7,9},{8,10},{9,11},{10,... | collective-permute-start | bytes 811016 | tf_op jit(solution)/shard_map/ppermute | solution.py:210
  8.8 4.0 %collective-permute-start.8 = (bf16[528,256]{1,0:T(8,128)(2,1)S(1)}, bf16[528,256]{1,0:T(8,128)(2,1)}, u32[]{:S(2)}, u32[]{:S(2)}) collective-permute-start(bf16[528,256]{1,0:T(8,128)(2,1)S(1)} %slice_dynamic-update-slice_fusion.refs_4_), channel_id=1, source_target_pairs={{0,48},{1,49},{2,50},{3,51},{4,52},{5,53},{6,54},{7,55},{8,56},{9,... | collective-permute-start | bytes 811016 | tf_op jit(solution)/shard_map/ppermute | solution.py:210
  12.8 0.1 select_reduce_fusion
  13.2 0.3 collective-permute-done.2.refs_5_
  13.5 7.6 %collective-permute-start.3 = (bf16[528,256]{1,0:T(8,128)(2,1)S(1)}, bf16[528,256]{1,0:T(8,128)(2,1)}, u32[]{:S(2)}, u32[]{:S(2)}) collective-permute-start(bf16[528,256]{1,0:T(8,128)(2,1)S(1)} %collective-permute-done.2.refs_5_), channel_id=1, source_target_pairs={{16,30},{17,31},{18,16},{19,17},{20,18},{21,19},{22,20},{23,21},{2... | collective-permute-start | bytes 811016 | tf_op jit(solution)/shard_map/ppermute | solution.py:210
  21.1 1.9 %collective-permute-start.7 = (bf16[528,256]{1,0:T(8,128)(2,1)S(1)}, bf16[528,256]{1,0:T(8,128)(2,1)S(1)}, u32[]{:S(2)}, u32[]{:S(2)}) collective-permute-start(bf16[528,256]{1,0:T(8,128)(2,1)S(1)} %collective-permute-done.2.refs_5_), channel_id=1, source_target_pairs={{16,18},{17,19},{18,20},{19,21},{20,22},{21,23},{22,24},{23,25},{2... | collective-permute-start | bytes 811016 | tf_op jit(solution)/shard_map/ppermute | solution.py:210
  23.0 1.9 %collective-permute-start.6 = (bf16[528,256]{1,0:T(8,128)(2,1)}, bf16[528,256]{1,0:T(8,128)(2,1)S(1)}, u32[]{:S(2)}, u32[]{:S(2)}) collective-permute-start(bf16[528,256]{1,0:T(8,128)(2,1)} %collective-permute-done.4.refs_4_), channel_id=1, source_target_pairs={{2,4},{3,5},{4,6},{5,7},{6,8},{7,9},{8,10},{9,11},{10,12},{11,13},... | collective-permute-start | bytes 811016 | tf_op jit(solution)/shard_map/ppermute | solution.py:210
  25.0 0.3 collective-permute-done.8
  25.2 2.2 %collective-permute-start.9 = (bf16[528,256]{1,0:T(8,128)(2,1)}, bf16[528,256]{1,0:T(8,128)(2,1)}, u32[]{:S(2)}, u32[]{:S(2)}) collective-permute-start(bf16[528,256]{1,0:T(8,128)(2,1)} %collective-permute-done.8), channel_id=1, source_target_pairs={{0,48},{1,49},{2,50},{3,51},{4,52},{5,53},{6,54},{7,55},{8,56},{9,... | collective-permute-start | bytes 811016 | tf_op jit(solution)/shard_map/ppermute | solution.py:210
  27.7 1.7 %shard_map.64 = (f32[256,128]{1,0:T(8,128)S(1)}, f32[8,256,256]{2,1,0:T(8,128)S(1)}) custom-call(s32[1,4]{1,0:T(1,128)S(1)} %slice.69.refs_0_, s32[1]{0:T(128)} %bitcast.17.refs_1_, bf16[2048,256]{1,0:T(8,128)(2,1)S(1)} %bitcast.32, f32[256,128]{1,0:T(8,128)S(1)} %broadcast_in_dim.56.refs_3_, bf16[528,256]{1,0:T(8,128)(2,1)S(1)} %slice_dynamic-update-slice_fusion.refs_4_), custom_call_target="tpu_custom_call" | custom-call | flops 536870912 | bytes 9270000 | tf_op jit(solution)/shard_map/pallas_call | solution.py:188
  29.4 5.2 %shard_map.65 = (f32[256,128]{1,0:T(8,128)S(1)}, f32[8,256,256]{2,1,0:T(8,128)S(1)}) custom-call(s32[2,4]{1,0:T(2,128)S(1)} %slice.67.refs_0_, s32[1]{0:T(128)} %bitcast.17.refs_1_, bf16[2048,256]{1,0:T(8,128)(2,1)S(1)} %bitcast.33, f32[256,128]{1,0:T(8,128)S(1)} %broadcast_in_dim.56.refs_3_, ...), custom_call_target="tpu_custom_call", output_to_operand_aliasing={{0}: (6, {}), {1}: (7, {})} | custom-call | flops 1073741824 | bytes 9540000 | tf_op jit(solution)/shard_map/pallas_call | solution.py:188
  34.7 1.3 %copy-done.1 = f32[8,256,256]{2,1,0:T(8,128)} copy-done((f32[8,256,256]{2,1,0:T(8,128)}, f32[8,256,256]{2,1,0:T(8,128)S(1)}, u32[]{:S(2)}) %copy-start.1) | copy-done | bytes 2097176
  36.0 3.9 %collective-permute-start.5 = (bf16[528,256]{1,0:T(8,128)(2,1)}, bf16[528,256]{1,0:T(8,128)(2,1)}, u32[]{:S(2)}, u32[]{:S(2)}) collective-permute-start(bf16[528,256]{1,0:T(8,128)(2,1)} %collective-permute-done.3.refs_6_), channel_id=1, source_target_pairs={{16,30},{17,31},{18,16},{19,17},{20,18},{21,19},{22,20},{23,21},{2... | collective-permute-start | bytes 811016 | tf_op jit(solution)/shard_map/ppermute | solution.py:210
  40.0 1.7 %collective-permute-done.9.refs_7_ = bf16[528,256]{1,0:T(8,128)(2,1)} collective-permute-done((bf16[528,256]{1,0:T(8,128)(2,1)}, bf16[528,256]{1,0:T(8,128)(2,1)}, u32[]{:S(2)}, u32[]{:S(2)}) %collective-permute-start.9) | collective-permute-done | bytes 270368 | tf_op jit(solution)/shard_map/ppermute | solution.py:210
  41.7 2.2 %collective-permute-start.13 = (bf16[528,256]{1,0:T(8,128)(2,1)}, bf16[528,256]{1,0:T(8,128)(2,1)}, u32[]{:S(2)}, u32[]{:S(2)}) collective-permute-start(bf16[528,256]{1,0:T(8,128)(2,1)} %collective-permute-done.9.refs_7_), channel_id=1, source_target_pairs={{0,46},{1,47},{2,0},{3,1},{4,2},{5,3},{16,62},{17,63},{18,16},{19,... | collective-permute-start | bytes 811016 | tf_op jit(solution)/shard_map/ppermute | solution.py:210
  43.9 0.1 copy.28
  44.1 3.2 %collective-permute-start.11 = (bf16[528,256]{1,0:T(8,128)(2,1)S(1)}, bf16[528,256]{1,0:T(8,128)(2,1)}, u32[]{:S(2)}, u32[]{:S(2)}) collective-permute-start(bf16[528,256]{1,0:T(8,128)(2,1)S(1)} %collective-permute-done.6.refs_4_), channel_id=1, source_target_pairs={{4,6},{5,7},{6,8},{7,9},{8,10},{9,11},{10,12},{11,13},{12,14},{13,... | collective-permute-start | bytes 811016 | tf_op jit(solution)/shard_map/ppermute | solution.py:210
  47.3 2.1 %collective-permute-start.12 = (bf16[528,256]{1,0:T(8,128)(2,1)S(1)}, bf16[528,256]{1,0:T(8,128)(2,1)}, u32[]{:S(2)}, u32[]{:S(2)}) collective-permute-start(bf16[528,256]{1,0:T(8,128)(2,1)S(1)} %collective-permute-done.7.refs_5_), channel_id=1, source_target_pairs={{16,18},{17,19},{18,20},{19,21},{20,22},{21,23},{22,24},{23,25},{2... | collective-permute-start | bytes 811016 | tf_op jit(solution)/shard_map/ppermute | solution.py:210
  49.4 1.6 %copy-done.2 = f32[8,256,256]{2,1,0:T(8,128)S(1)} copy-done((f32[8,256,256]{2,1,0:T(8,128)S(1)}, f32[8,256,256]{2,1,0:T(8,128)}, u32[]{:S(2)}) %copy-start.2) | copy-done | bytes 2097176
  51.0 6.1 %shard_map.66 = (f32[256,128]{1,0:T(8,128)S(1)}, f32[8,256,256]{2,1,0:T(8,128)S(1)}) custom-call(s32[4,4]{1,0:T(4,128)S(1)} %copy.29.refs_0_, s32[1]{0:T(128)} %bitcast.17.refs_1_, bf16[2048,256]{1,0:T(8,128)(2,1)S(1)} %bitcast.34, f32[256,128]{1,0:T(8,128)S(1)} %broadcast_in_dim.56.refs_3_, ...), custom_call_target="tpu_custom_call", output_to_operand_aliasing={{0}: (8, {}), {1}: (9, {})} | custom-call | flops 2147483648 | bytes 10080000 | tf_op jit(solution)/shard_map/pallas_call | solution.py:188
  57.1 1.3 %copy-done.3 = f32[8,256,256]{2,1,0:T(8,128)} copy-done((f32[8,256,256]{2,1,0:T(8,128)}, f32[8,256,256]{2,1,0:T(8,128)S(1)}, u32[]{:S(2)}) %copy-start.3) | copy-done | bytes 2097176
  58.5 4.6 %collective-permute-start.10 = (bf16[528,256]{1,0:T(8,128)(2,1)}, bf16[528,256]{1,0:T(8,128)(2,1)}, u32[]{:S(2)}, u32[]{:S(2)}) collective-permute-start(bf16[528,256]{1,0:T(8,128)(2,1)} %collective-permute-done.5.refs_6_), channel_id=1, source_target_pairs={{16,30},{17,31},{18,16},{19,17},{20,18},{21,19},{22,20},{23,21},{2... | collective-permute-start | bytes 811016 | tf_op jit(solution)/shard_map/ppermute | solution.py:210
  63.1 4.6 %collective-permute-start.15 = (bf16[528,256]{1,0:T(8,128)(2,1)}, bf16[528,256]{1,0:T(8,128)(2,1)}, u32[]{:S(2)}, u32[]{:S(2)}) collective-permute-start(bf16[528,256]{1,0:T(8,128)(2,1)} %collective-permute-done.13.refs_7_), channel_id=1, source_target_pairs={{0,46},{1,47},{2,0},{3,1},{14,12},{15,13},{16,62},{17,63},{18,16},... | collective-permute-start | bytes 811016 | tf_op jit(solution)/shard_map/ppermute | solution.py:210
  67.7 0.8 constant_dynamic-slice_fusion
  68.5 3.5 %collective-permute-start.19 = (bf16[128,2048]{1,0:T(8,128)(2,1)}, bf16[128,2048]{1,0:T(8,128)(2,1)S(1)}, u32[]{:S(2)}, u32[]{:S(2)}) collective-permute-start(bf16[128,2048]{1,0:T(8,128)(2,1)} %constant_dynamic-slice_fusion), channel_id=1, source_target_pairs={{0,1},{1,0},{2,3},{3,2},{4,5},{5,4},{6,7},{7,6},{8,9},{9,8},{10,11... | collective-permute-start | bytes 1572872 | tf_op jit(solution)/shard_map/ppermute | solution.py:210
  72.2 1.9 %collective-permute-start.17 = (bf16[528,256]{1,0:T(8,128)(2,1)}, bf16[528,256]{1,0:T(8,128)(2,1)}, u32[]{:S(2)}, u32[]{:S(2)}) collective-permute-start(bf16[528,256]{1,0:T(8,128)(2,1)} %collective-permute-done.11.refs_4_), channel_id=1, source_target_pairs={{6,8},{7,9},{8,10},{9,11},{10,12},{11,13},{12,14},{13,15},{14,32},... | collective-permute-start | bytes 811016 | tf_op jit(solution)/shard_map/ppermute | solution.py:210
  74.2 1.9 %collective-permute-start.18 = (bf16[528,256]{1,0:T(8,128)(2,1)}, bf16[528,256]{1,0:T(8,128)(2,1)}, u32[]{:S(2)}, u32[]{:S(2)}) collective-permute-start(bf16[528,256]{1,0:T(8,128)(2,1)} %collective-permute-done.12.refs_5_), channel_id=1, source_target_pairs={{16,18},{17,19},{18,20},{19,21},{20,22},{21,23},{22,24},{23,25},{2... | collective-permute-start | bytes 811016 | tf_op jit(solution)/shard_map/ppermute | solution.py:210
  76.1 1.6 %copy-done.4 = f32[8,256,256]{2,1,0:T(8,128)S(1)} copy-done((f32[8,256,256]{2,1,0:T(8,128)S(1)}, f32[8,256,256]{2,1,0:T(8,128)}, u32[]{:S(2)}) %copy-start.4) | copy-done | bytes 2097176
  77.7 6.3 %shard_map.67 = (f32[256,128]{1,0:T(8,128)S(1)}, f32[8,256,256]{2,1,0:T(8,128)S(1)}) custom-call(s32[4,4]{1,0:T(4,128)S(1)} %copy.31.refs_0_, s32[1]{0:T(128)} %bitcast.17.refs_1_, bf16[2048,256]{1,0:T(8,128)(2,1)S(1)} %bitcast.35, f32[256,128]{1,0:T(8,128)S(1)} %broadcast_in_dim.56.refs_3_, ...), custom_call_target="tpu_custom_call", output_to_operand_aliasing={{0}: (8, {}), {1}: (9, {})} | custom-call | flops 2147483648 | bytes 10080000 | tf_op jit(solution)/shard_map/pallas_call | solution.py:188
  84.0 1.3 %copy-done.5 = f32[8,256,256]{2,1,0:T(8,128)} copy-done((f32[8,256,256]{2,1,0:T(8,128)}, f32[8,256,256]{2,1,0:T(8,128)S(1)}, u32[]{:S(2)}) %copy-start.5) | copy-done | bytes 2097176
  85.4 4.6 %collective-permute-start.14 = (bf16[528,256]{1,0:T(8,128)(2,1)}, bf16[528,256]{1,0:T(8,128)(2,1)S(1)}, u32[]{:S(2)}, u32[]{:S(2)}) collective-permute-start(bf16[528,256]{1,0:T(8,128)(2,1)} %collective-permute-done.10.refs_6_), channel_id=1, source_target_pairs={{16,30},{17,31},{18,16},{19,17},{20,18},{21,19},{22,20},{23,21},{2... | collective-permute-start | bytes 811016 | tf_op jit(solution)/shard_map/ppermute | solution.py:210
  89.9 6.0 %collective-permute-start.16 = (bf16[528,256]{1,0:T(8,128)(2,1)}, bf16[528,256]{1,0:T(8,128)(2,1)S(1)}, u32[]{:S(2)}, u32[]{:S(2)}) collective-permute-start(bf16[528,256]{1,0:T(8,128)(2,1)} %collective-permute-done.15.refs_7_), channel_id=1, source_target_pairs={{0,46},{1,47},{12,10},{13,11},{14,12},{15,13},{16,62},{17,63},{28,... | collective-permute-start | bytes 811016 | tf_op jit(solution)/shard_map/ppermute | solution.py:210
  95.9 0.1 copy.32
  96.2 1.6 %copy-done.6 = f32[8,256,256]{2,1,0:T(8,128)S(1)} copy-done((f32[8,256,256]{2,1,0:T(8,128)S(1)}, f32[8,256,256]{2,1,0:T(8,128)}, u32[]{:S(2)}) %copy-start.6) | copy-done | bytes 2097176
  97.8 6.3 %shard_map.68 = (f32[256,128]{1,0:T(8,128)S(1)}, f32[8,256,256]{2,1,0:T(8,128)S(1)}) custom-call(s32[4,4]{1,0:T(4,128)S(1)} %copy.33.refs_0_, s32[1]{0:T(128)} %bitcast.17.refs_1_, bf16[2048,256]{1,0:T(8,128)(2,1)S(1)} %bitcast.36, f32[256,128]{1,0:T(8,128)S(1)} %broadcast_in_dim.56.refs_3_, ...), custom_call_target="tpu_custom_call", output_to_operand_aliasing={{0}: (8, {}), {1}: (9, {})} | custom-call | flops 2147483648 | bytes 10080000 | tf_op jit(solution)/shard_map/pallas_call | solution.py:188
  104.2 0.6 copy-done.9
  104.8 0.7 copy-done.7
  105.5 1.0 copy-done.8
  106.5 0.9 copy-done.10
  107.4 5.1 %shard_map.69 = (bf16[128,2048]{1,0:T(8,128)(2,1)S(1)}, bf16[128,2048]{1,0:T(8,128)(2,1)}) custom-call(s32[2,4]{1,0:T(2,128)S(1)} %slice.62.refs_0_, s32[1]{0:T(128)} %bitcast.17.refs_1_, bf16[2048,256]{1,0:T(8,128)(2,1)S(1)} %bitcast.37, f32[256,128]{1,0:T(8,128)S(1)} %broadcast_in_dim.56.refs_3_, bf16[528,256]{1,0:T(8,128)(2,1)S(1)} %collective-permute-done.14.refs_4_, ...), custom_call_target="tpu_custom_call" | custom-call | flops 1073741824 | bytes 9540000 | tf_op jit(solution)/shard_map/pallas_call | solution.py:188
  112.5 1.1 collective-permute-start.20
  113.6 1.7 %collective-permute-done.20 = bf16[128,2048]{1,0:T(8,128)(2,1)S(1)} collective-permute-done((bf16[128,2048]{1,0:T(8,128)(2,1)}, bf16[128,2048]{1,0:T(8,128)(2,1)S(1)}, u32[]{:S(2)}, u32[]{:S(2)}) %collective-permute-start.20) | collective-permute-done | bytes 524320 | tf_op jit(solution)/shard_map/ppermute | solution.py:210
  115.4 1.2 %maximum_select_fusion = bf16[128,4096]{1,0:T(8,128)(2,1)} fusion(bf16[128,2048]{1,0:T(8,128)(2,1)S(1)} %collective-permute-done.20, bf16[128,2048]{1,0:T(8,128)(2,1)S(1)} %get-tuple-element.45, pred[]{:T(512)S(6)} %eq.21), kind=kLoop, calls=%fused_computation.2 | loop fusion | flops 4718592 | bytes 2097153 | tf_op jit(solution)/shard_map/jit(_where)/select_n | solution.py:297
  (72 shorter events, 1.4 us)
Async XLA Ops:
  0.0 2.1 %copy-start.13 = (s32[1,64]{1,0:T(1,128)S(1)}, s32[1,64]{1,0:T(1,128)}, u32[]{:S(2)}) copy-start(s32[1,64]{1,0:T(1,128)} %param.11) | copy-start | bytes 772
  0.0 2.2 %copy-start.14 = (s32[128]{0:T(128)S(1)}, s32[128]{0:T(128)}, u32[]{:S(2)}) copy-start(s32[128]{0:T(128)} %param.10) | copy-start | bytes 1540
  0.0 2.2 %copy-start.11 = (bf16[128,512]{1,0:T(8,128)(2,1)S(1)}, bf16[128,512]{1,0:T(8,128)(2,1)}, u32[]{:S(2)}) copy-start(bf16[128,512]{1,0:T(8,128)(2,1)} %param.7) | copy-start | bytes 393220
  0.0 2.2 %copy-start.12 = (bf16[128,512]{1,0:T(8,128)(2,1)S(1)}, bf16[128,512]{1,0:T(8,128)(2,1)}, u32[]{:S(2)}) copy-start(bf16[128,512]{1,0:T(8,128)(2,1)} %param.8) | copy-start | bytes 393220
  1.4 26.1 %collective-permute-start.1 = (bf16[128,2048]{1,0:T(8,128)(2,1)S(1)}, bf16[128,2048]{1,0:T(8,128)(2,1)S(1)}, u32[]{:S(2)}, u32[]{:S(2)}) collective-permute-start(bf16[128,2048]{1,0:T(8,128)(2,1)S(1)} %get-tuple-element.48), channel_id=1, source_target_pairs={{0,1},{1,0},{2,3},{3,2},{4,5},{5,4},{6,7},{7,6},{8,9},{9,8},{10,11... | collective-permute-start | bytes 1572872 | tf_op jit(solution)/shard_map/ppermute | solution.py:210
  2.3 1.6 %collective-permute-start = (bf16[272,256]{1,0:T(8,128)(2,1)S(1)}, bf16[272,256]{1,0:T(8,128)(2,1)S(1)}, u32[]{:S(2)}, u32[]{:S(2)}) collective-permute-start(bf16[272,256]{1,0:T(8,128)(2,1)S(1)} %pad_maximum_fusion.1), channel_id=1, source_target_pairs={{0,1},{1,0},{2,3},{3,2},{4,5},{5,4},{6,7},{7,6},{8,9},{9,8},{10,11... | collective-permute-start | bytes 417800 | tf_op jit(solution)/shard_map/ppermute | solution.py:210
  3.9 9.6 %collective-permute-start.2 = (bf16[528,256]{1,0:T(8,128)(2,1)S(1)}, bf16[528,256]{1,0:T(8,128)(2,1)S(1)}, u32[]{:S(2)}, u32[]{:S(2)}) collective-permute-start(bf16[528,256]{1,0:T(8,128)(2,1)S(1)} %slice_dynamic-update-slice_fusion.refs_4_), channel_id=1, source_target_pairs={{0,16},{1,17},{2,18},{3,19},{4,20},{5,21},{6,22},{7,23},{8,24},{9,... | collective-permute-start | bytes 811016 | tf_op jit(solution)/shard_map/ppermute | solution.py:210
  5.2 17.8 %collective-permute-start.4 = (bf16[528,256]{1,0:T(8,128)(2,1)S(1)}, bf16[528,256]{1,0:T(8,128)(2,1)}, u32[]{:S(2)}, u32[]{:S(2)}) collective-permute-start(bf16[528,256]{1,0:T(8,128)(2,1)S(1)} %slice_dynamic-update-slice_fusion.refs_4_), channel_id=1, source_target_pairs={{0,2},{1,3},{2,4},{3,5},{4,6},{5,7},{6,8},{7,9},{8,10},{9,11},{10,... | collective-permute-start | bytes 811016 | tf_op jit(solution)/shard_map/ppermute | solution.py:210
  8.8 16.4 %collective-permute-start.8 = (bf16[528,256]{1,0:T(8,128)(2,1)S(1)}, bf16[528,256]{1,0:T(8,128)(2,1)}, u32[]{:S(2)}, u32[]{:S(2)}) collective-permute-start(bf16[528,256]{1,0:T(8,128)(2,1)S(1)} %slice_dynamic-update-slice_fusion.refs_4_), channel_id=1, source_target_pairs={{0,48},{1,49},{2,50},{3,51},{4,52},{5,53},{6,54},{7,55},{8,56},{9,... | collective-permute-start | bytes 811016 | tf_op jit(solution)/shard_map/ppermute | solution.py:210
  13.5 22.5 %collective-permute-start.3 = (bf16[528,256]{1,0:T(8,128)(2,1)S(1)}, bf16[528,256]{1,0:T(8,128)(2,1)}, u32[]{:S(2)}, u32[]{:S(2)}) collective-permute-start(bf16[528,256]{1,0:T(8,128)(2,1)S(1)} %collective-permute-done.2.refs_5_), channel_id=1, source_target_pairs={{16,30},{17,31},{18,16},{19,17},{20,18},{21,19},{22,20},{23,21},{2... | collective-permute-start | bytes 811016 | tf_op jit(solution)/shard_map/ppermute | solution.py:210
  21.1 26.2 %collective-permute-start.7 = (bf16[528,256]{1,0:T(8,128)(2,1)S(1)}, bf16[528,256]{1,0:T(8,128)(2,1)S(1)}, u32[]{:S(2)}, u32[]{:S(2)}) collective-permute-start(bf16[528,256]{1,0:T(8,128)(2,1)S(1)} %collective-permute-done.2.refs_5_), channel_id=1, source_target_pairs={{16,18},{17,19},{18,20},{19,21},{20,22},{21,23},{22,24},{23,25},{2... | collective-permute-start | bytes 811016 | tf_op jit(solution)/shard_map/ppermute | solution.py:210
  23.0 21.0 %collective-permute-start.6 = (bf16[528,256]{1,0:T(8,128)(2,1)}, bf16[528,256]{1,0:T(8,128)(2,1)S(1)}, u32[]{:S(2)}, u32[]{:S(2)}) collective-permute-start(bf16[528,256]{1,0:T(8,128)(2,1)} %collective-permute-done.4.refs_4_), channel_id=1, source_target_pairs={{2,4},{3,5},{4,6},{5,7},{6,8},{7,9},{8,10},{9,11},{10,12},{11,13},... | collective-permute-start | bytes 811016 | tf_op jit(solution)/shard_map/ppermute | solution.py:210
  25.2 16.4 %collective-permute-start.9 = (bf16[528,256]{1,0:T(8,128)(2,1)}, bf16[528,256]{1,0:T(8,128)(2,1)}, u32[]{:S(2)}, u32[]{:S(2)}) collective-permute-start(bf16[528,256]{1,0:T(8,128)(2,1)} %collective-permute-done.8), channel_id=1, source_target_pairs={{0,48},{1,49},{2,50},{3,51},{4,52},{5,53},{6,54},{7,55},{8,56},{9,... | collective-permute-start | bytes 811016 | tf_op jit(solution)/shard_map/ppermute | solution.py:210
  34.7 1.4 %copy-start.1 = (f32[8,256,256]{2,1,0:T(8,128)}, f32[8,256,256]{2,1,0:T(8,128)S(1)}, u32[]{:S(2)}) copy-start(f32[8,256,256]{2,1,0:T(8,128)S(1)} %get-tuple-element.32.refs_9_) | copy-start | bytes 6291460
  36.0 22.5 %collective-permute-start.5 = (bf16[528,256]{1,0:T(8,128)(2,1)}, bf16[528,256]{1,0:T(8,128)(2,1)}, u32[]{:S(2)}, u32[]{:S(2)}) collective-permute-start(bf16[528,256]{1,0:T(8,128)(2,1)} %collective-permute-done.3.refs_6_), channel_id=1, source_target_pairs={{16,30},{17,31},{18,16},{19,17},{20,18},{21,19},{22,20},{23,21},{2... | collective-permute-start | bytes 811016 | tf_op jit(solution)/shard_map/ppermute | solution.py:210
  41.7 21.4 %collective-permute-start.13 = (bf16[528,256]{1,0:T(8,128)(2,1)}, bf16[528,256]{1,0:T(8,128)(2,1)}, u32[]{:S(2)}, u32[]{:S(2)}) collective-permute-start(bf16[528,256]{1,0:T(8,128)(2,1)} %collective-permute-done.9.refs_7_), channel_id=1, source_target_pairs={{0,46},{1,47},{2,0},{3,1},{4,2},{5,3},{16,62},{17,63},{18,16},{19,... | collective-permute-start | bytes 811016 | tf_op jit(solution)/shard_map/ppermute | solution.py:210
  44.0 23.6 %copy-start = (bf16[128,4096]{1,0:T(8,128)(2,1)S(1)}, bf16[128,4096]{1,0:T(8,128)(2,1)}, u32[]{:S(2)}) copy-start(bf16[128,4096]{1,0:T(8,128)(2,1)} %refs_8_.1) | copy-start | bytes 3145732
  44.1 28.2 %collective-permute-start.11 = (bf16[528,256]{1,0:T(8,128)(2,1)S(1)}, bf16[528,256]{1,0:T(8,128)(2,1)}, u32[]{:S(2)}, u32[]{:S(2)}) collective-permute-start(bf16[528,256]{1,0:T(8,128)(2,1)S(1)} %collective-permute-done.6.refs_4_), channel_id=1, source_target_pairs={{4,6},{5,7},{6,8},{7,9},{8,10},{9,11},{10,12},{11,13},{12,14},{13,... | collective-permute-start | bytes 811016 | tf_op jit(solution)/shard_map/ppermute | solution.py:210
  47.3 26.9 %collective-permute-start.12 = (bf16[528,256]{1,0:T(8,128)(2,1)S(1)}, bf16[528,256]{1,0:T(8,128)(2,1)}, u32[]{:S(2)}, u32[]{:S(2)}) collective-permute-start(bf16[528,256]{1,0:T(8,128)(2,1)S(1)} %collective-permute-done.7.refs_5_), channel_id=1, source_target_pairs={{16,18},{17,19},{18,20},{19,21},{20,22},{21,23},{22,24},{23,25},{2... | collective-permute-start | bytes 811016 | tf_op jit(solution)/shard_map/ppermute | solution.py:210
  49.4 1.6 %copy-start.2 = (f32[8,256,256]{2,1,0:T(8,128)S(1)}, f32[8,256,256]{2,1,0:T(8,128)}, u32[]{:S(2)}) copy-start(f32[8,256,256]{2,1,0:T(8,128)} %copy-done.1) | copy-start | bytes 6291460
  57.1 1.4 %copy-start.3 = (f32[8,256,256]{2,1,0:T(8,128)}, f32[8,256,256]{2,1,0:T(8,128)S(1)}, u32[]{:S(2)}) copy-start(f32[8,256,256]{2,1,0:T(8,128)S(1)} %get-tuple-element.37.refs_9_) | copy-start | bytes 6291460
  58.5 26.9 %collective-permute-start.10 = (bf16[528,256]{1,0:T(8,128)(2,1)}, bf16[528,256]{1,0:T(8,128)(2,1)}, u32[]{:S(2)}, u32[]{:S(2)}) collective-permute-start(bf16[528,256]{1,0:T(8,128)(2,1)} %collective-permute-done.5.refs_6_), channel_id=1, source_target_pairs={{16,30},{17,31},{18,16},{19,17},{20,18},{21,19},{22,20},{23,21},{2... | collective-permute-start | bytes 811016 | tf_op jit(solution)/shard_map/ppermute | solution.py:210
  63.1 26.9 %collective-permute-start.15 = (bf16[528,256]{1,0:T(8,128)(2,1)}, bf16[528,256]{1,0:T(8,128)(2,1)}, u32[]{:S(2)}, u32[]{:S(2)}) collective-permute-start(bf16[528,256]{1,0:T(8,128)(2,1)} %collective-permute-done.13.refs_7_), channel_id=1, source_target_pairs={{0,46},{1,47},{2,0},{3,1},{14,12},{15,13},{16,62},{17,63},{18,16},... | collective-permute-start | bytes 811016 | tf_op jit(solution)/shard_map/ppermute | solution.py:210
  68.5 36.3 %collective-permute-start.19 = (bf16[128,2048]{1,0:T(8,128)(2,1)}, bf16[128,2048]{1,0:T(8,128)(2,1)S(1)}, u32[]{:S(2)}, u32[]{:S(2)}) collective-permute-start(bf16[128,2048]{1,0:T(8,128)(2,1)} %constant_dynamic-slice_fusion), channel_id=1, source_target_pairs={{0,1},{1,0},{2,3},{3,2},{4,5},{5,4},{6,7},{7,6},{8,9},{9,8},{10,11... | collective-permute-start | bytes 1572872 | tf_op jit(solution)/shard_map/ppermute | solution.py:210
  72.2 24.0 %collective-permute-start.17 = (bf16[528,256]{1,0:T(8,128)(2,1)}, bf16[528,256]{1,0:T(8,128)(2,1)}, u32[]{:S(2)}, u32[]{:S(2)}) collective-permute-start(bf16[528,256]{1,0:T(8,128)(2,1)} %collective-permute-done.11.refs_4_), channel_id=1, source_target_pairs={{6,8},{7,9},{8,10},{9,11},{10,12},{11,13},{12,14},{13,15},{14,32},... | collective-permute-start | bytes 811016 | tf_op jit(solution)/shard_map/ppermute | solution.py:210
  74.2 22.1 %collective-permute-start.18 = (bf16[528,256]{1,0:T(8,128)(2,1)}, bf16[528,256]{1,0:T(8,128)(2,1)}, u32[]{:S(2)}, u32[]{:S(2)}) collective-permute-start(bf16[528,256]{1,0:T(8,128)(2,1)} %collective-permute-done.12.refs_5_), channel_id=1, source_target_pairs={{16,18},{17,19},{18,20},{19,21},{20,22},{21,23},{22,24},{23,25},{2... | collective-permute-start | bytes 811016 | tf_op jit(solution)/shard_map/ppermute | solution.py:210
  76.1 1.6 %copy-start.4 = (f32[8,256,256]{2,1,0:T(8,128)S(1)}, f32[8,256,256]{2,1,0:T(8,128)}, u32[]{:S(2)}) copy-start(f32[8,256,256]{2,1,0:T(8,128)} %copy-done.3) | copy-start | bytes 6291460
  84.0 1.4 %copy-start.5 = (f32[8,256,256]{2,1,0:T(8,128)}, f32[8,256,256]{2,1,0:T(8,128)S(1)}, u32[]{:S(2)}) copy-start(f32[8,256,256]{2,1,0:T(8,128)S(1)} %get-tuple-element.42.refs_9_) | copy-start | bytes 6291460
  85.4 19.4 %collective-permute-start.14 = (bf16[528,256]{1,0:T(8,128)(2,1)}, bf16[528,256]{1,0:T(8,128)(2,1)S(1)}, u32[]{:S(2)}, u32[]{:S(2)}) collective-permute-start(bf16[528,256]{1,0:T(8,128)(2,1)} %collective-permute-done.10.refs_6_), channel_id=1, source_target_pairs={{16,30},{17,31},{18,16},{19,17},{20,18},{21,19},{22,20},{23,21},{2... | collective-permute-start | bytes 811016 | tf_op jit(solution)/shard_map/ppermute | solution.py:210
  89.9 14.9 %collective-permute-start.16 = (bf16[528,256]{1,0:T(8,128)(2,1)}, bf16[528,256]{1,0:T(8,128)(2,1)S(1)}, u32[]{:S(2)}, u32[]{:S(2)}) collective-permute-start(bf16[528,256]{1,0:T(8,128)(2,1)} %collective-permute-done.15.refs_7_), channel_id=1, source_target_pairs={{0,46},{1,47},{12,10},{13,11},{14,12},{15,13},{16,62},{17,63},{28,... | collective-permute-start | bytes 811016 | tf_op jit(solution)/shard_map/ppermute | solution.py:210
  96.2 1.6 %copy-start.6 = (f32[8,256,256]{2,1,0:T(8,128)S(1)}, f32[8,256,256]{2,1,0:T(8,128)}, u32[]{:S(2)}) copy-start(f32[8,256,256]{2,1,0:T(8,128)} %copy-done.5) | copy-start | bytes 6291460
  104.1 0.7 copy-start.9
  104.8 0.7 copy-start.7
  105.5 1.0 copy-start.8
  106.5 0.9 copy-start.10
  112.5 2.9 %collective-permute-start.20 = (bf16[128,2048]{1,0:T(8,128)(2,1)}, bf16[128,2048]{1,0:T(8,128)(2,1)S(1)}, u32[]{:S(2)}, u32[]{:S(2)}) collective-permute-start(bf16[128,2048]{1,0:T(8,128)(2,1)} %get-tuple-element.46), channel_id=1, source_target_pairs={{0,1},{1,0},{2,3},{3,2},{4,5},{5,4},{6,7},{7,6},{8,9},{9,8},{10,11... | collective-permute-start | bytes 1572872 | tf_op jit(solution)/shard_map/ppermute | solution.py:210

commit v4 on v1

--- a/solution.py
+++ b/solution.py
@@ -22,35 +22,77 @@
 NEG = -1e30
 
 
-def permutation(target):
-    pairs = []
-    for x in range(NX):
-        for z in range(NZ):
-            for core in range(2):
-                goal = target(x, z, core)
-                if goal is not None:
-                    gx, gz, gc = goal
-                    pairs.append(((x * NZ + z) * 2 + core, (gx * NZ + gz) * 2 + gc))
-    return pairs
-
-
-SWAP = permutation(lambda x, z, c: (x, z, 1 - c))
-ONE_X = permutation(lambda x, z, c: (x + 1, z, c) if x < 3 else None)
-TWO_X = permutation(lambda x, z, c: ((x + 2) % NX, z, c))
-NEAR_UP = permutation(
-    lambda x, z, c: (x, z + 1, c) if z < 7 else ((x + 2, 0, c) if x < 2 else None)
+def pairs_of(links):
+    return [
+        ((ax * NZ + az) * 2 + c, (bx * NZ + bz) * 2 + c)
+        for (ax, az), (bx, bz) in sorted(links)
+        for c in range(2)
+    ]
+
+
+CHIPS = [(x, z) for x in range(NX) for z in range(NZ)]
+
+
+def chain_plan(seed, source, visible, length):
+    wanted = [set() for _ in range(length + 1)]
+    for s in range(length, -1, -1):
+        wanted[s] |= {chip for chip in CHIPS if visible(*chip, s)}
+        if s:
+            wanted[s - 1] |= {source(*chip) for chip in wanted[s]}
+    hops = [
+        pairs_of({(source(*chip), chip) for chip in wanted[s]})
+        for s in range(1, length + 1)
+    ]
+    first, need = [], wanted[0]
+    for back in seed:
+        first.append(pairs_of({(back(*chip), chip) for chip in need}))
+        need = {back(*chip) for chip in need}
+    return first[::-1], hops
+
+
+SWAP = [(i, i ^ 1) for i in range(2 * NX * NZ)]
+NEAR = chain_plan([], lambda x, z: (x, z - 1), lambda x, z, s: z >= s, 4)[1]
+FAR_SEED, FAR = chain_plan(
+    [lambda x, z: ((x + 1) % NX, z)] * 2,
+    lambda x, z: (x, z + 1),
+    lambda x, z, s: x >= 2 and z + s < NZ,
+    3,
 )
-NEAR_DOWN = permutation(
-    lambda x, z, c: (x, z - 1, c) if z > 0 else ((x + 2) % NX, 7, c)
+MID_SEED, MID_UP = chain_plan(
+    [lambda x, z: ((x - 1) % NX, z)],
+    lambda x, z: (x, (z - 1) % NZ),
+    lambda x, z, s: x >= 1,
+    3,
 )
-MID_UP = permutation(lambda x, z, c: (x, (z + 1) % NZ, c) if x > 0 else None)
-MID_DOWN = permutation(lambda x, z, c: (x, (z - 1) % NZ, c) if x > 0 else None)
-
-
-def attend(own_at, last, count, *refs):
+MID_SEED_DOWN, MID_DOWN = chain_plan(
+    [lambda x, z: ((x - 1) % NX, z)],
+    lambda x, z: (x, (z + 1) % NZ),
+    lambda x, z, s: x >= 1 or (z + s >= NZ and s < 4),
+    4,
+)
+MID_SEED = sorted(set(MID_SEED[0]) | set(MID_SEED_DOWN[0]))
+SIDE_NEAR = [
+    pairs_of({((x - 1, z), (x, z)) for x, z in CHIPS if x >= 2 and z < s})
+    for s in range(1, 5)
+]
+SIDE_FAR = [
+    pairs_of({(((x + 1) % NX, z), (x, z)) for x, z in CHIPS if z + s >= NZ})
+    for s in range(1, 4)
+]
+
+
+def attend(own_at, last, paired, *refs):
     flags, core, q, qdocs = refs[:4]
-    units = refs[4 : 4 + count]
-    rest = list(refs[4 + count :])
+    rest = list(refs[4:])
+    units = []
+    for j, two in enumerate(paired):
+        if two:
+            other = flags[j, 4] == 1
+            units.append(jnp.where(other, rest[1][...], rest[0][...]))
+        else:
+            units.append(rest[0])
+        rest = rest[2 if two else 1 :]
+    count = len(paired)
     first = own_at is not None
     if not first:
         m_in, l_in, acc_in = rest[:3]
@@ -141,6 +183,8 @@
 
 def attend_call(core, flags, q, qdocs, units, state=None, gates=None, own_at=None):
     count = len(units)
+    paired = tuple(len(u) == 2 for u in units)
+    units = [v for u in units for v in u]
     last = gates is not None
     smem = pl.BlockSpec(memory_space=pltpu.SMEM)
     vmem = pl.BlockSpec(memory_space=pltpu.VMEM)
@@ -161,12 +205,12 @@
         ]
     specs = [smem, smem] + [vmem] * (len(args) - 2)
     return pl.pallas_call(
-        functools.partial(attend, own_at, last, count),
+        functools.partial(attend, own_at, last, paired),
         out_shape=shapes,
         in_specs=specs,
         out_specs=[vmem] * len(shapes),
         input_output_aliases=aliases,
-        compiler_params=pltpu.CompilerParams(vmem_limit_bytes=32 << 20),
+        compiler_params=pltpu.CompilerParams(vmem_limit_bytes=24 << 20),
         cost_estimate=pl.CostEstimate(
             flops=4 * ROWS * UNIT * HD * count,
             bytes_accessed=count * 270000 + 9000000,
@@ -209,17 +253,22 @@
         ],
         axis=0,
     )
-    up = [unit]
-    mid0 = send(unit, ONE_X)
-    low0 = send(unit, TWO_X)
-    down = [low0]
-    mup, mdown = [mid0], [mid0]
+    near, mid, far = [unit], [send(unit, MID_SEED)], []
+    near.append(send(unit, NEAR[0]))
+    relay = send(unit, FAR_SEED[0])
+    far.append(send(relay, FAR_SEED[1]))
+    low, high = [mid[0]], [mid[0]]
+    side_near, side_far = [None], [None]
     for s in range(4):
-        up.append(send(up[-1], NEAR_UP))
-        mup.append(send(mup[-1], MID_UP))
+        high.append(send(high[-1], MID_DOWN[s]))
         if s < 3:
-            down.append(send(down[-1], NEAR_DOWN))
-            mdown.append(send(mdown[-1], MID_DOWN))
+            low.append(send(low[-1], MID_UP[s]))
+            near.append(send(near[-1], NEAR[s + 1]))
+            far.append(send(far[-1], FAR[s]))
+            side_near.append(send(low[-1], SIDE_NEAR[s]))
+            side_far.append(send(high[-1], SIDE_FAR[s]))
+        else:
+            side_near.append(send(high[-1], SIDE_NEAR[s]))
 
     q_other = send(take(query_rows, 1 - core, HALF), SWAP)
     gate_other = send(take(gate_rows, 1 - core, HALF), SWAP)
@@ -229,36 +278,39 @@
     qdocs = jnp.broadcast_to(meta[0][:, None], (UNIT, BLK))
     lists = jnp.stack([meta[1, :64], meta[1, BLK : BLK + 64]])
 
-    def up_id(s):
-        return jnp.where(z >= s, chip - s, jnp.where(x >= 2, chip - s - NZ, -1))
-
-    def down_id(s):
-        return jnp.where(
-            z + s < NZ, jnp.where(x >= 2, chip - 2 * NZ + s, -1), chip + s - NZ
+    def mid_unit(s):
+        unit_id = jnp.where(x >= 1, (x - 1) * NZ + lax.rem(z + s + NZ, NZ), -1)
+        return ((low[-s] if s <= 0 else high[s]),), unit_id, jnp.int32(0)
+
+    def near_unit(s):
+        over = z < s
+        unit_id = jnp.where(over, jnp.where(x >= 2, chip - s - NZ, -1), chip - s)
+        return (near[s], side_near[s]), unit_id, over.astype(jnp.int32)
+
+    def far_unit(s):
+        if s == 0:
+            return (far[0],), jnp.where(x >= 2, chip - 2 * NZ, -1), jnp.int32(0)
+        over = z + s >= NZ
+        unit_id = jnp.where(
+            over, chip + s - NZ, jnp.where(x >= 2, chip - 2 * NZ + s, -1)
         )
-
-    def mid_id(s):
-        return jnp.where(x >= 1, (x - 1) * NZ + lax.rem(z + s + NZ, NZ), -1)
+        return (far[s], side_far[s]), unit_id, over.astype(jnp.int32)
 
     groups = [
-        [(up[0], chip)],
-        [(up[1], up_id(1)), (down[0], down_id(0)), (mup[0], mid_id(0))],
-        [(up[2], up_id(2)), (down[1], down_id(1)), (mup[1], mid_id(-1)), (mdown[1], mid_id(1))],
-        [(up[3], up_id(3)), (down[2], down_id(2)), (mup[2], mid_id(-2)), (mdown[2], mid_id(2))],
-        [
-            (up[4], up_id(4)),
-            (down[3], down_id(3)),
-            (mup[3], mid_id(-3)),
-            (mdown[3], mid_id(3)),
-            (mup[4], mid_id(-4)),
-        ],
+        [((unit,), chip, jnp.int32(0))],
+        [mid_unit(0), mid_unit(-1), mid_unit(1), far_unit(0)],
+        [mid_unit(-2), mid_unit(2), near_unit(1), far_unit(1)],
+        [mid_unit(-3), mid_unit(3), near_unit(2), far_unit(2)],
+        [mid_unit(4), near_unit(3), far_unit(3), near_unit(4)],
     ]
-    ids = jnp.stack([i for group in groups for _, i in group])
+    ids = jnp.stack([i for group in groups for _, i, _ in group])
     cols = 2 * ids[:, None] + jnp.stack([core, 1 - core])[None, :]
     cols = jnp.where(ids[:, None] >= 0, cols, -1)
     hot = cols[:, None, :, None] == jnp.arange(64, dtype=jnp.int32)[None, None, None, :]
     table = jnp.sum(jnp.where(hot, lists[None, :, None, :], 0.0), axis=-1)
     table = table.astype(jnp.int32).reshape(ids.shape[0], 4)
+    picks = jnp.stack([k for group in groups for _, _, k in group])
+    table = jnp.concatenate([table, picks[:, None]], axis=1)
 
     core1 = core.reshape(1)
     state = None
@@ -268,7 +320,7 @@
         at += len(group)
         gates = (gate_rows, gate_other) if n == len(groups) - 1 else None
         state = attend_call(
-            core1, flags, q, qdocs, [u for u, _ in group], state, gates, 0 if n == 0 else None
+            core1, flags, q, qdocs, [u for u, _, _ in group], state, gates, 0 if n == 0 else None
         )
     mine, other = state
     back = send(other, SWAP)

time: 92.1 us -> 101 us (1.097)
  the two profiles are of different devices: /device:TPU:15 before, /device:TPU:51 now
where the time goes in v4:
time: 101 us
  starting transfers between devices  66.1 us (65%)
  Pallas kernels  21.9 us (22%)
  waiting for transfers between devices  5.45 us (5%)
  local copies, waits for them, and re-layouts  3.51 us (3%)
  other arithmetic  2.96 us (3%)
    ppermute x28, starting transfers between devices, send(): return lax.ppermute(value, 'cp', pairs)  66.1 us
    pallas_call x5, Pallas kernels, attend_call(): pl.pallas_call(functools.partial(attend, own_at, last, paired), out_shape...  21.9 us
    ppermute x28, waiting for transfers between devices, send(): return lax.ppermute(value, 'cp', pairs)  5.45 us
    dynamic_slice x2, local copies, waits for them, and re-layouts, take(): return lax.dynamic_slice_in_dim(rows, which * width, width, 1)  2.44 us
  transfers between devices with their start and end apart: 28, of which 4 were waited for; matrix products, arithmetic and copies ran while one was open for 3% of the time, Pallas kernels for 17%

profile of v4, /device:TPU:51, one launch (start us, length us, event | category | flops | bytes accessed | tf_op | source)
XLA Modules:
  0.0 100.6 jit_solution(8724879715999497716)
XLA Ops:
  0.0 2.4 %constant_dynamic-slice_fusion.2 = (bf16[128,2048]{1,0:T(8,128)(2,1)}, bf16[128,2048]{1,0:T(8,128)(2,1)}) fusion(bf16[128,4096]{1,0:T(8,128)(2,1)} %param.6, s32[]{:T(128)S(6)} %select_n.142, s32[]{:T(128)S(6)} %select_n.143), kind=kLoop, calls=%fused_computation.24 | loop fusion | bytes 2097160 | tf_op jit(solution)/shard_map/dynamic_slice | solution.py:232
  2.4 0.7 collective-permute-start.1
  3.3 0.1 collective-permute-start
  3.5 0.1 stack.128
  3.7 1.1 %collective-permute-done = bf16[272,256]{1,0:T(8,128)(2,1)S(1)} collective-permute-done((bf16[272,256]{1,0:T(8,128)(2,1)S(1)}, bf16[272,256]{1,0:T(8,128)(2,1)S(1)}, u32[]{:S(2)}, u32[]{:S(2)}) %collective-permute-start) | collective-permute-done | bytes 139296 | tf_op jit(solution)/shard_map/ppermute | solution.py:229
  4.9 3.1 %collective-permute-start.2 = (bf16[528,256]{1,0:T(8,128)(2,1)S(1)}, bf16[528,256]{1,0:T(8,128)(2,1)S(1)}, u32[]{:S(2)}, u32[]{:S(2)}) collective-permute-start(bf16[528,256]{1,0:T(8,128)(2,1)S(1)} %slice_dynamic-update-slice_fusion.refs_4_), channel_id=1, source_target_pairs={{0,16},{1,17},{2,18},{3,19},{4,20},{5,21},{6,22},{7,23},{8,24},{9,... | collective-permute-start | bytes 811016 | tf_op jit(solution)/shard_map/ppermute | solution.py:229
  8.1 2.9 %collective-permute-start.14 = (bf16[528,256]{1,0:T(8,128)(2,1)S(1)}, bf16[528,256]{1,0:T(8,128)(2,1)}, u32[]{:S(2)}, u32[]{:S(2)}) collective-permute-start(bf16[528,256]{1,0:T(8,128)(2,1)S(1)} %slice_dynamic-update-slice_fusion.refs_4_), channel_id=1, source_target_pairs={{0,48},{1,49},{2,50},{3,51},{4,52},{5,53},{6,54},{7,55},{8,56},{9,... | collective-permute-start | bytes 811016 | tf_op jit(solution)/shard_map/ppermute | solution.py:229
  11.1 3.5 %collective-permute-start.7 = (bf16[528,256]{1,0:T(8,128)(2,1)S(1)}, bf16[528,256]{1,0:T(8,128)(2,1)S(1)}, u32[]{:S(2)}, u32[]{:S(2)}) collective-permute-start(bf16[528,256]{1,0:T(8,128)(2,1)S(1)} %slice_dynamic-update-slice_fusion.refs_4_), channel_id=1, source_target_pairs={{0,2},{1,3},{2,4},{3,5},{4,6},{5,7},{6,8},{7,9},{8,10},{9,11},{10,... | collective-permute-start | bytes 811016 | tf_op jit(solution)/shard_map/ppermute | solution.py:229
  14.6 3.6 %collective-permute-start.10 = (bf16[528,256]{1,0:T(8,128)(2,1)S(1)}, bf16[528,256]{1,0:T(8,128)(2,1)S(1)}, u32[]{:S(2)}, u32[]{:S(2)}) collective-permute-start(bf16[528,256]{1,0:T(8,128)(2,1)S(1)} %collective-permute-done.2.refs_4_), channel_id=1, source_target_pairs={{16,18},{17,19},{18,20},{19,21},{20,22},{21,23},{22,24},{23,25},{2... | collective-permute-start | bytes 811016 | tf_op jit(solution)/shard_map/ppermute | solution.py:229
  18.2 1.9 %collective-permute-start.3 = (bf16[528,256]{1,0:T(8,128)(2,1)S(1)}, bf16[528,256]{1,0:T(8,128)(2,1)}, u32[]{:S(2)}, u32[]{:S(2)}) collective-permute-start(bf16[528,256]{1,0:T(8,128)(2,1)S(1)} %collective-permute-done.2.refs_4_), channel_id=1, source_target_pairs={{0,14},{1,15},{2,0},{3,1},{4,2},{5,3},{16,30},{17,31},{18,16},{19,... | collective-permute-start | bytes 811016 | tf_op jit(solution)/shard_map/ppermute | solution.py:229
  20.3 1.7 %collective-permute-start.26 = (bf16[128,2048]{1,0:T(8,128)(2,1)S(1)}, bf16[128,2048]{1,0:T(8,128)(2,1)S(1)}, u32[]{:S(2)}, u32[]{:S(2)}) collective-permute-start(bf16[128,2048]{1,0:T(8,128)(2,1)S(1)} %constant_dynamic-slice_fusion), channel_id=1, source_target_pairs={{0,1},{1,0},{2,3},{3,2},{4,5},{5,4},{6,7},{7,6},{8,9},{9,8},{10,11... | collective-permute-start | bytes 1572872 | tf_op jit(solution)/shard_map/ppermute | solution.py:229
  22.0 1.4 %collective-permute-start.15 = (bf16[528,256]{1,0:T(8,128)(2,1)}, bf16[528,256]{1,0:T(8,128)(2,1)}, u32[]{:S(2)}, u32[]{:S(2)}) collective-permute-start(bf16[528,256]{1,0:T(8,128)(2,1)} %collective-permute-done.14), channel_id=1, source_target_pairs={{0,48},{1,49},{2,50},{3,51},{4,52},{5,53},{6,54},{7,55},{8,56},{9,... | collective-permute-start | bytes 811016 | tf_op jit(solution)/shard_map/ppermute | solution.py:229
  23.4 4.7 %collective-permute-start.8 = (bf16[528,256]{1,0:T(8,128)(2,1)S(1)}, bf16[528,256]{1,0:T(8,128)(2,1)S(1)}, u32[]{:S(2)}, u32[]{:S(2)}) collective-permute-start(bf16[528,256]{1,0:T(8,128)(2,1)S(1)} %collective-permute-done.7.refs_6_), channel_id=1, source_target_pairs={{2,4},{3,5},{4,6},{5,7},{6,8},{7,9},{8,10},{9,11},{10,12},{11,13},... | collective-permute-start | bytes 811016 | tf_op jit(solution)/shard_map/ppermute | solution.py:229
  28.0 3.6 %collective-permute-start.11 = (bf16[528,256]{1,0:T(8,128)(2,1)S(1)}, bf16[528,256]{1,0:T(8,128)(2,1)}, u32[]{:S(2)}, u32[]{:S(2)}) collective-permute-start(bf16[528,256]{1,0:T(8,128)(2,1)S(1)} %collective-permute-done.10.refs_5_), channel_id=1, source_target_pairs={{16,18},{17,19},{18,20},{19,21},{20,22},{21,23},{22,24},{23,25},{2... | collective-permute-start | bytes 811016 | tf_op jit(solution)/shard_map/ppermute | solution.py:229
  31.7 1.9 %collective-permute-start.4 = (bf16[528,256]{1,0:T(8,128)(2,1)}, bf16[528,256]{1,0:T(8,128)(2,1)}, u32[]{:S(2)}, u32[]{:S(2)}) collective-permute-start(bf16[528,256]{1,0:T(8,128)(2,1)} %collective-permute-done.3.refs_6_), channel_id=1, source_target_pairs={{0,14},{1,15},{2,0},{3,1},{14,12},{15,13},{16,30},{17,31},{18,16},... | collective-permute-start | bytes 811016 | tf_op jit(solution)/shard_map/ppermute | solution.py:229
  33.7 0.1 select_reduce_fusion
  33.8 0.1 copy.32
  33.9 1.4 %collective-permute-start.24 = (bf16[528,256]{1,0:T(8,128)(2,1)S(1)}, bf16[528,256]{1,0:T(8,128)(2,1)}, u32[]{:S(2)}, u32[]{:S(2)}) collective-permute-start(bf16[528,256]{1,0:T(8,128)(2,1)S(1)} %collective-permute-done.10.refs_5_), channel_id=1, source_target_pairs={{16,32},{17,33},{32,48},{33,49},{80,96},{81,97},{96,112},{97,113},... | collective-permute-start | bytes 811016 | tf_op jit(solution)/shard_map/ppermute | solution.py:229
  35.3 1.4 %collective-permute-start.25 = (bf16[528,256]{1,0:T(8,128)(2,1)}, bf16[528,256]{1,0:T(8,128)(2,1)}, u32[]{:S(2)}, u32[]{:S(2)}) collective-permute-start(bf16[528,256]{1,0:T(8,128)(2,1)} %collective-permute-done.3.refs_6_), channel_id=1, source_target_pairs={{14,62},{15,63},{30,14},{31,15},{46,30},{47,31},{62,46},{63,47},{7... | collective-permute-start | bytes 811016 | tf_op jit(solution)/shard_map/ppermute | solution.py:229
  36.6 1.4 %collective-permute-start.16 = (bf16[528,256]{1,0:T(8,128)(2,1)}, bf16[528,256]{1,0:T(8,128)(2,1)}, u32[]{:S(2)}, u32[]{:S(2)}) collective-permute-start(bf16[528,256]{1,0:T(8,128)(2,1)} %collective-permute-done.15.refs_7_), channel_id=1, source_target_pairs={{34,32},{35,33},{36,34},{37,35},{38,36},{39,37},{40,38},{41,39},{4... | collective-permute-start | bytes 811016 | tf_op jit(solution)/shard_map/ppermute | solution.py:229
  38.0 1.5 %collective-permute-done.11.refs_4_ = bf16[528,256]{1,0:T(8,128)(2,1)} collective-permute-done((bf16[528,256]{1,0:T(8,128)(2,1)S(1)}, bf16[528,256]{1,0:T(8,128)(2,1)}, u32[]{:S(2)}, u32[]{:S(2)}) %collective-permute-start.11) | collective-permute-done | bytes 270368 | tf_op jit(solution)/shard_map/ppermute | solution.py:229
  39.5 0.7 collective-permute-start.9
  40.2 1.2 %collective-permute-done.4.refs_5_ = bf16[528,256]{1,0:T(8,128)(2,1)} collective-permute-done((bf16[528,256]{1,0:T(8,128)(2,1)}, bf16[528,256]{1,0:T(8,128)(2,1)}, u32[]{:S(2)}, u32[]{:S(2)}) %collective-permute-start.4) | collective-permute-done | bytes 270368 | tf_op jit(solution)/shard_map/ppermute | solution.py:229
  41.4 2.1 %collective-permute-start.5 = (bf16[528,256]{1,0:T(8,128)(2,1)}, bf16[528,256]{1,0:T(8,128)(2,1)}, u32[]{:S(2)}, u32[]{:S(2)}) collective-permute-start(bf16[528,256]{1,0:T(8,128)(2,1)} %collective-permute-done.4.refs_5_), channel_id=1, source_target_pairs={{0,14},{1,15},{12,10},{13,11},{14,12},{15,13},{16,30},{17,31},{18,... | collective-permute-start | bytes 811016 | tf_op jit(solution)/shard_map/ppermute | solution.py:229
  43.5 0.1 copy.43.refs_0_
  43.7 0.1 copy.42.refs_0_
  43.8 0.1 copy.41.refs_0_
  43.9 0.1 copy.40.refs_0_
  44.0 0.1 copy.39.refs_0_
  44.1 5.3 %collective-permute-start.12 = (bf16[528,256]{1,0:T(8,128)(2,1)}, bf16[528,256]{1,0:T(8,128)(2,1)S(1)}, u32[]{:S(2)}, u32[]{:S(2)}) collective-permute-start(bf16[528,256]{1,0:T(8,128)(2,1)} %collective-permute-done.11.refs_4_), channel_id=1, source_target_pairs={{16,18},{17,19},{18,20},{19,21},{20,22},{21,23},{22,24},{23,25},{2... | collective-permute-start | bytes 811016 | tf_op jit(solution)/shard_map/ppermute | solution.py:229
  49.4 5.7 %collective-permute-start.22 = (bf16[528,256]{1,0:T(8,128)(2,1)}, bf16[528,256]{1,0:T(8,128)(2,1)S(1)}, u32[]{:S(2)}, u32[]{:S(2)}) collective-permute-start(bf16[528,256]{1,0:T(8,128)(2,1)} %collective-permute-done.11.refs_4_), channel_id=1, source_target_pairs={{16,32},{17,33},{18,34},{19,35},{32,48},{33,49},{34,50},{35,51},{8... | collective-permute-start | bytes 811016 | tf_op jit(solution)/shard_map/ppermute | solution.py:229
  55.1 0.7 collective-permute-start.23
  55.8 0.7 collective-permute-start.17
  56.5 2.0 %collective-permute-start.6 = (bf16[528,256]{1,0:T(8,128)(2,1)}, bf16[528,256]{1,0:T(8,128)(2,1)S(1)}, u32[]{:S(2)}, u32[]{:S(2)}) collective-permute-start(bf16[528,256]{1,0:T(8,128)(2,1)} %collective-permute-done.5.refs_5_), channel_id=1, source_target_pairs={{16,30},{17,31},{18,16},{19,17},{20,18},{21,19},{22,20},{23,21},{2... | collective-permute-start | bytes 811016 | tf_op jit(solution)/shard_map/ppermute | solution.py:229
  58.5 1.3 %pad_maximum_fusion = bf16[256,2048]{1,0:T(8,128)(2,1)S(1)} fusion(bf16[128,2048]{1,0:T(8,128)(2,1)} %collective-permute-done.1, bf16[128,2048]{1,0:T(8,128)(2,1)} %get-tuple-element.33), kind=kLoop, calls=%fused_computation.1 | loop fusion | flops 2097152 | bytes 2097152 | tf_op jit(solution)/shard_map/concatenate | solution.py:275
  60.0 1.7 %shard_map.64 = (f32[8,256,128]{2,1,0:T(8,128)S(1)}, f32[8,256,128]{2,1,0:T(8,128)S(1)}, f32[8,256,256]{2,1,0:T(8,128)S(1)}) custom-call(s32[1,5]{1,0:T(1,128)S(1)} %copy.43.refs_0_, s32[1]{0:T(128)} %bitcast.17.refs_1_, bf16[2048,256]{1,0:T(8,128)(2,1)S(1)} %bitcast.39, f32[256,128]{1,0:T(8,128)S(1)} %broadcast_in_dim.60.refs_3_, ...), custom_call_target="tpu_custom_call" | custom-call | flops 536870912 | bytes 9270000 | tf_op jit(solution)/shard_map/pallas_call | solution.py:207
  61.7 5.2 %shard_map.65 = (f32[8,256,128]{2,1,0:T(8,128)S(1)}, f32[8,256,128]{2,1,0:T(8,128)S(1)}, f32[8,256,256]{2,1,0:T(8,128)S(1)}) custom-call(s32[4,5]{1,0:T(4,128)S(1)} %copy.42.refs_0_, s32[1]{0:T(128)} %bitcast.17.refs_1_, bf16[2048,256]{1,0:T(8,128)(2,1)S(1)} %bitcast.40, ...), custom_call_target="tpu_custom_call", output_to_operand_aliasing={{0}: (8, {}), {1}: (9, {}), {2}: (10, {})} | custom-call | flops 2147483648 | bytes 10080000 | tf_op jit(solution)/shard_map/pallas_call | solution.py:207
  66.9 0.7 collective-permute-start.20
  67.6 0.7 collective-permute-start.19
  68.3 5.2 %collective-permute-start.13 = (bf16[528,256]{1,0:T(8,128)(2,1)S(1)}, bf16[528,256]{1,0:T(8,128)(2,1)S(1)}, u32[]{:S(2)}, u32[]{:S(2)}) collective-permute-start(bf16[528,256]{1,0:T(8,128)(2,1)S(1)} %collective-permute-done.12.refs_4_), channel_id=1, source_target_pairs={{16,32},{17,33},{18,34},{19,35},{20,36},{21,37},{32,48},{33,49},{3... | collective-permute-start | bytes 811016 | tf_op jit(solution)/shard_map/ppermute | solution.py:229
  73.5 0.7 collective-permute-start.18
  74.2 3.3 %collective-permute-start.21 = (bf16[528,256]{1,0:T(8,128)(2,1)S(1)}, bf16[528,256]{1,0:T(8,128)(2,1)S(1)}, u32[]{:S(2)}, u32[]{:S(2)}) collective-permute-start(bf16[528,256]{1,0:T(8,128)(2,1)S(1)} %collective-permute-done.6.refs_4_), channel_id=1, source_target_pairs={{16,32},{17,33},{18,34},{19,35},{20,36},{21,37},{22,38},{23,39},{3... | collective-permute-start | bytes 811016 | tf_op jit(solution)/shard_map/ppermute | solution.py:229
  77.5 5.1 %shard_map.66 = (f32[8,256,128]{2,1,0:T(8,128)S(1)}, f32[8,256,128]{2,1,0:T(8,128)S(1)}, f32[8,256,256]{2,1,0:T(8,128)S(1)}) custom-call(s32[4,5]{1,0:T(4,128)S(1)} %copy.41.refs_0_, s32[1]{0:T(128)} %bitcast.17.refs_1_, bf16[2048,256]{1,0:T(8,128)(2,1)S(1)} %bitcast.41, ...), custom_call_target="tpu_custom_call", output_to_operand_aliasing={{0}: (10, {}), {1}: (11, {}), {2}: (12, {})} | custom-call | flops 2147483648 | bytes 10080000 | tf_op jit(solution)/shard_map/pallas_call | solution.py:207
  82.6 5.0 %shard_map.67 = (f32[8,256,128]{2,1,0:T(8,128)S(1)}, f32[8,256,128]{2,1,0:T(8,128)S(1)}, f32[8,256,256]{2,1,0:T(8,128)S(1)}) custom-call(s32[4,5]{1,0:T(4,128)S(1)} %copy.40.refs_0_, s32[1]{0:T(128)} %bitcast.17.refs_1_, bf16[2048,256]{1,0:T(8,128)(2,1)S(1)} %bitcast.42, ...), custom_call_target="tpu_custom_call", output_to_operand_aliasing={{0}: (10, {}), {1}: (11, {}), {2}: (12, {})} | custom-call | flops 2147483648 | bytes 10080000 | tf_op jit(solution)/shard_map/pallas_call | solution.py:207
  87.7 4.9 %shard_map.68 = (bf16[128,2048]{1,0:T(8,128)(2,1)S(1)}, bf16[128,2048]{1,0:T(8,128)(2,1)S(1)}) custom-call(s32[4,5]{1,0:T(4,128)S(1)} %copy.39.refs_0_, s32[1]{0:T(128)} %bitcast.17.refs_1_, bf16[2048,256]{1,0:T(8,128)(2,1)S(1)} %bitcast.43, f32[256,128]{1,0:T(8,128)S(1)} %broadcast_in_dim.60.refs_3_, bf16[528,256]{1,0:T(8,128)(2,1)S(1)} %collective-permute-done.6.refs_4_, ...), custom_call_target="tpu_custom_call" | custom-call | flops 2147483648 | bytes 10080000 | tf_op jit(solution)/shard_map/pallas_call | solution.py:207
  92.6 5.3 %collective-permute-start.27 = (bf16[128,2048]{1,0:T(8,128)(2,1)S(1)}, bf16[128,2048]{1,0:T(8,128)(2,1)S(1)}, u32[]{:S(2)}, u32[]{:S(2)}) collective-permute-start(bf16[128,2048]{1,0:T(8,128)(2,1)S(1)} %get-tuple-element.32), channel_id=1, source_target_pairs={{0,1},{1,0},{2,3},{3,2},{4,5},{5,4},{6,7},{7,6},{8,9},{9,8},{10,11... | collective-permute-start | bytes 1572872 | tf_op jit(solution)/shard_map/ppermute | solution.py:229
  97.9 1.5 %collective-permute-done.27 = bf16[128,2048]{1,0:T(8,128)(2,1)S(1)} collective-permute-done((bf16[128,2048]{1,0:T(8,128)(2,1)S(1)}, bf16[128,2048]{1,0:T(8,128)(2,1)S(1)}, u32[]{:S(2)}, u32[]{:S(2)}) %collective-permute-start.27) | collective-permute-done | bytes 524320 | tf_op jit(solution)/shard_map/ppermute | solution.py:229
  99.4 1.2 %maximum_select_fusion = bf16[128,4096]{1,0:T(8,128)(2,1)} fusion(bf16[128,2048]{1,0:T(8,128)(2,1)S(1)} %collective-permute-done.27, bf16[128,2048]{1,0:T(8,128)(2,1)S(1)} %get-tuple-element.31, pred[]{:T(512)S(6)} %eq.21), kind=kLoop, calls=%fused_computation.2 | loop fusion | flops 4718592 | bytes 2097153 | tf_op jit(solution)/shard_map/jit(_where)/select_n | solution.py:327
  (64 shorter events, 0.8 us)
Async XLA Ops:
  0.0 3.1 %copy-start.3 = (s32[1,64]{1,0:T(1,128)S(1)}, s32[1,64]{1,0:T(1,128)}, u32[]{:S(2)}) copy-start(s32[1,64]{1,0:T(1,128)} %param.11) | copy-start | bytes 772
  0.0 3.1 %copy-start.4 = (s32[128]{0:T(128)S(1)}, s32[128]{0:T(128)}, u32[]{:S(2)}) copy-start(s32[128]{0:T(128)} %param.10) | copy-start | bytes 1540
  0.0 3.2 %copy-start.1 = (bf16[128,512]{1,0:T(8,128)(2,1)S(1)}, bf16[128,512]{1,0:T(8,128)(2,1)}, u32[]{:S(2)}) copy-start(bf16[128,512]{1,0:T(8,128)(2,1)} %param.7) | copy-start | bytes 393220
  0.0 3.2 %copy-start.2 = (bf16[128,512]{1,0:T(8,128)(2,1)S(1)}, bf16[128,512]{1,0:T(8,128)(2,1)}, u32[]{:S(2)}) copy-start(bf16[128,512]{1,0:T(8,128)(2,1)} %param.8) | copy-start | bytes 393220
  0.0 3.6 %copy-start = (bf16[128,4096]{1,0:T(8,128)(2,1)S(1)}, bf16[128,4096]{1,0:T(8,128)(2,1)}, u32[]{:S(2)}) copy-start(bf16[128,4096]{1,0:T(8,128)(2,1)} %refs_14_.1) | copy-start | bytes 3145732
  2.4 20.9 %collective-permute-start.1 = (bf16[128,2048]{1,0:T(8,128)(2,1)}, bf16[128,2048]{1,0:T(8,128)(2,1)}, u32[]{:S(2)}, u32[]{:S(2)}) collective-permute-start(bf16[128,2048]{1,0:T(8,128)(2,1)} %get-tuple-element.34), channel_id=1, source_target_pairs={{0,1},{1,0},{2,3},{3,2},{4,5},{5,4},{6,7},{7,6},{8,9},{9,8},{10,11... | collective-permute-start | bytes 1572872 | tf_op jit(solution)/shard_map/ppermute | solution.py:229
  3.3 1.6 %collective-permute-start = (bf16[272,256]{1,0:T(8,128)(2,1)S(1)}, bf16[272,256]{1,0:T(8,128)(2,1)S(1)}, u32[]{:S(2)}, u32[]{:S(2)}) collective-permute-start(bf16[272,256]{1,0:T(8,128)(2,1)S(1)} %pad_maximum_fusion.1), channel_id=1, source_target_pairs={{0,1},{1,0},{2,3},{3,2},{4,5},{5,4},{6,7},{7,6},{8,9},{9,8},{10,11... | collective-permute-start | bytes 417800 | tf_op jit(solution)/shard_map/ppermute | solution.py:229
  4.9 9.7 %collective-permute-start.2 = (bf16[528,256]{1,0:T(8,128)(2,1)S(1)}, bf16[528,256]{1,0:T(8,128)(2,1)S(1)}, u32[]{:S(2)}, u32[]{:S(2)}) collective-permute-start(bf16[528,256]{1,0:T(8,128)(2,1)S(1)} %slice_dynamic-update-slice_fusion.refs_4_), channel_id=1, source_target_pairs={{0,16},{1,17},{2,18},{3,19},{4,20},{5,21},{6,22},{7,23},{8,24},{9,... | collective-permute-start | bytes 811016 | tf_op jit(solution)/shard_map/ppermute | solution.py:229
  8.1 12.2 %collective-permute-start.14 = (bf16[528,256]{1,0:T(8,128)(2,1)S(1)}, bf16[528,256]{1,0:T(8,128)(2,1)}, u32[]{:S(2)}, u32[]{:S(2)}) collective-permute-start(bf16[528,256]{1,0:T(8,128)(2,1)S(1)} %slice_dynamic-update-slice_fusion.refs_4_), channel_id=1, source_target_pairs={{0,48},{1,49},{2,50},{3,51},{4,52},{5,53},{6,54},{7,55},{8,56},{9,... | collective-permute-start | bytes 811016 | tf_op jit(solution)/shard_map/ppermute | solution.py:229
  11.1 10.9 %collective-permute-start.7 = (bf16[528,256]{1,0:T(8,128)(2,1)S(1)}, bf16[528,256]{1,0:T(8,128)(2,1)S(1)}, u32[]{:S(2)}, u32[]{:S(2)}) collective-permute-start(bf16[528,256]{1,0:T(8,128)(2,1)S(1)} %slice_dynamic-update-slice_fusion.refs_4_), channel_id=1, source_target_pairs={{0,2},{1,3},{2,4},{3,5},{4,6},{5,7},{6,8},{7,9},{8,10},{9,11},{10,... | collective-permute-start | bytes 811016 | tf_op jit(solution)/shard_map/ppermute | solution.py:229
  14.6 13.4 %collective-permute-start.10 = (bf16[528,256]{1,0:T(8,128)(2,1)S(1)}, bf16[528,256]{1,0:T(8,128)(2,1)S(1)}, u32[]{:S(2)}, u32[]{:S(2)}) collective-permute-start(bf16[528,256]{1,0:T(8,128)(2,1)S(1)} %collective-permute-done.2.refs_4_), channel_id=1, source_target_pairs={{16,18},{17,19},{18,20},{19,21},{20,22},{21,23},{22,24},{23,25},{2... | collective-permute-start | bytes 811016 | tf_op jit(solution)/shard_map/ppermute | solution.py:229
  18.2 13.5 %collective-permute-start.3 = (bf16[528,256]{1,0:T(8,128)(2,1)S(1)}, bf16[528,256]{1,0:T(8,128)(2,1)}, u32[]{:S(2)}, u32[]{:S(2)}) collective-permute-start(bf16[528,256]{1,0:T(8,128)(2,1)S(1)} %collective-permute-done.2.refs_4_), channel_id=1, source_target_pairs={{0,14},{1,15},{2,0},{3,1},{4,2},{5,3},{16,30},{17,31},{18,16},{19,... | collective-permute-start | bytes 811016 | tf_op jit(solution)/shard_map/ppermute | solution.py:229
  20.3 13.6 %collective-permute-start.26 = (bf16[128,2048]{1,0:T(8,128)(2,1)S(1)}, bf16[128,2048]{1,0:T(8,128)(2,1)S(1)}, u32[]{:S(2)}, u32[]{:S(2)}) collective-permute-start(bf16[128,2048]{1,0:T(8,128)(2,1)S(1)} %constant_dynamic-slice_fusion), channel_id=1, source_target_pairs={{0,1},{1,0},{2,3},{3,2},{4,5},{5,4},{6,7},{7,6},{8,9},{9,8},{10,11... | collective-permute-start | bytes 1572872 | tf_op jit(solution)/shard_map/ppermute | solution.py:229
  22.0 13.3 %collective-permute-start.15 = (bf16[528,256]{1,0:T(8,128)(2,1)}, bf16[528,256]{1,0:T(8,128)(2,1)}, u32[]{:S(2)}, u32[]{:S(2)}) collective-permute-start(bf16[528,256]{1,0:T(8,128)(2,1)} %collective-permute-done.14), channel_id=1, source_target_pairs={{0,48},{1,49},{2,50},{3,51},{4,52},{5,53},{6,54},{7,55},{8,56},{9,... | collective-permute-start | bytes 811016 | tf_op jit(solution)/shard_map/ppermute | solution.py:229
  23.4 13.3 %collective-permute-start.8 = (bf16[528,256]{1,0:T(8,128)(2,1)S(1)}, bf16[528,256]{1,0:T(8,128)(2,1)S(1)}, u32[]{:S(2)}, u32[]{:S(2)}) collective-permute-start(bf16[528,256]{1,0:T(8,128)(2,1)S(1)} %collective-permute-done.7.refs_6_), channel_id=1, source_target_pairs={{2,4},{3,5},{4,6},{5,7},{6,8},{7,9},{8,10},{9,11},{10,12},{11,13},... | collective-permute-start | bytes 811016 | tf_op jit(solution)/shard_map/ppermute | solution.py:229
  28.0 11.5 %collective-permute-start.11 = (bf16[528,256]{1,0:T(8,128)(2,1)S(1)}, bf16[528,256]{1,0:T(8,128)(2,1)}, u32[]{:S(2)}, u32[]{:S(2)}) collective-permute-start(bf16[528,256]{1,0:T(8,128)(2,1)S(1)} %collective-permute-done.10.refs_5_), channel_id=1, source_target_pairs={{16,18},{17,19},{18,20},{19,21},{20,22},{21,23},{22,24},{23,25},{2... | collective-permute-start | bytes 811016 | tf_op jit(solution)/shard_map/ppermute | solution.py:229
  31.7 9.7 %collective-permute-start.4 = (bf16[528,256]{1,0:T(8,128)(2,1)}, bf16[528,256]{1,0:T(8,128)(2,1)}, u32[]{:S(2)}, u32[]{:S(2)}) collective-permute-start(bf16[528,256]{1,0:T(8,128)(2,1)} %collective-permute-done.3.refs_6_), channel_id=1, source_target_pairs={{0,14},{1,15},{2,0},{3,1},{14,12},{15,13},{16,30},{17,31},{18,16},... | collective-permute-start | bytes 811016 | tf_op jit(solution)/shard_map/ppermute | solution.py:229
  33.9 15.5 %collective-permute-start.24 = (bf16[528,256]{1,0:T(8,128)(2,1)S(1)}, bf16[528,256]{1,0:T(8,128)(2,1)}, u32[]{:S(2)}, u32[]{:S(2)}) collective-permute-start(bf16[528,256]{1,0:T(8,128)(2,1)S(1)} %collective-permute-done.10.refs_5_), channel_id=1, source_target_pairs={{16,32},{17,33},{32,48},{33,49},{80,96},{81,97},{96,112},{97,113},... | collective-permute-start | bytes 811016 | tf_op jit(solution)/shard_map/ppermute | solution.py:229
  35.3 19.8 %collective-permute-start.25 = (bf16[528,256]{1,0:T(8,128)(2,1)}, bf16[528,256]{1,0:T(8,128)(2,1)}, u32[]{:S(2)}, u32[]{:S(2)}) collective-permute-start(bf16[528,256]{1,0:T(8,128)(2,1)} %collective-permute-done.3.refs_6_), channel_id=1, source_target_pairs={{14,62},{15,63},{30,14},{31,15},{46,30},{47,31},{62,46},{63,47},{7... | collective-permute-start | bytes 811016 | tf_op jit(solution)/shard_map/ppermute | solution.py:229
  36.6 7.4 %collective-permute-start.16 = (bf16[528,256]{1,0:T(8,128)(2,1)}, bf16[528,256]{1,0:T(8,128)(2,1)}, u32[]{:S(2)}, u32[]{:S(2)}) collective-permute-start(bf16[528,256]{1,0:T(8,128)(2,1)} %collective-permute-done.15.refs_7_), channel_id=1, source_target_pairs={{34,32},{35,33},{36,34},{37,35},{38,36},{39,37},{40,38},{41,39},{4... | collective-permute-start | bytes 811016 | tf_op jit(solution)/shard_map/ppermute | solution.py:229
  39.5 16.3 %collective-permute-start.9 = (bf16[528,256]{1,0:T(8,128)(2,1)S(1)}, bf16[528,256]{1,0:T(8,128)(2,1)S(1)}, u32[]{:S(2)}, u32[]{:S(2)}) collective-permute-start(bf16[528,256]{1,0:T(8,128)(2,1)S(1)} %collective-permute-done.8.refs_6_), channel_id=1, source_target_pairs={{4,6},{5,7},{6,8},{7,9},{8,10},{9,11},{10,12},{11,13},{12,14},{13,... | collective-permute-start | bytes 811016 | tf_op jit(solution)/shard_map/ppermute | solution.py:229
  41.4 15.1 %collective-permute-start.5 = (bf16[528,256]{1,0:T(8,128)(2,1)}, bf16[528,256]{1,0:T(8,128)(2,1)}, u32[]{:S(2)}, u32[]{:S(2)}) collective-permute-start(bf16[528,256]{1,0:T(8,128)(2,1)} %collective-permute-done.4.refs_5_), channel_id=1, source_target_pairs={{0,14},{1,15},{12,10},{13,11},{14,12},{15,13},{16,30},{17,31},{18,... | collective-permute-start | bytes 811016 | tf_op jit(solution)/shard_map/ppermute | solution.py:229
  44.1 22.8 %collective-permute-start.12 = (bf16[528,256]{1,0:T(8,128)(2,1)}, bf16[528,256]{1,0:T(8,128)(2,1)S(1)}, u32[]{:S(2)}, u32[]{:S(2)}) collective-permute-start(bf16[528,256]{1,0:T(8,128)(2,1)} %collective-permute-done.11.refs_4_), channel_id=1, source_target_pairs={{16,18},{17,19},{18,20},{19,21},{20,22},{21,23},{22,24},{23,25},{2... | collective-permute-start | bytes 811016 | tf_op jit(solution)/shard_map/ppermute | solution.py:229
  49.4 18.9 %collective-permute-start.22 = (bf16[528,256]{1,0:T(8,128)(2,1)}, bf16[528,256]{1,0:T(8,128)(2,1)S(1)}, u32[]{:S(2)}, u32[]{:S(2)}) collective-permute-start(bf16[528,256]{1,0:T(8,128)(2,1)} %collective-permute-done.11.refs_4_), channel_id=1, source_target_pairs={{16,32},{17,33},{18,34},{19,35},{32,48},{33,49},{34,50},{35,51},{8... | collective-permute-start | bytes 811016 | tf_op jit(solution)/shard_map/ppermute | solution.py:229
  55.1 18.3 %collective-permute-start.23 = (bf16[528,256]{1,0:T(8,128)(2,1)}, bf16[528,256]{1,0:T(8,128)(2,1)S(1)}, u32[]{:S(2)}, u32[]{:S(2)}) collective-permute-start(bf16[528,256]{1,0:T(8,128)(2,1)} %collective-permute-done.4.refs_5_), channel_id=1, source_target_pairs={{12,60},{13,61},{14,62},{15,63},{28,12},{29,13},{30,14},{31,15},{4... | collective-permute-start | bytes 811016 | tf_op jit(solution)/shard_map/ppermute | solution.py:229
  55.8 11.7 %collective-permute-start.17 = (bf16[528,256]{1,0:T(8,128)(2,1)}, bf16[528,256]{1,0:T(8,128)(2,1)S(1)}, u32[]{:S(2)}, u32[]{:S(2)}) collective-permute-start(bf16[528,256]{1,0:T(8,128)(2,1)} %collective-permute-done.16.refs_8_), channel_id=1, source_target_pairs={{34,32},{35,33},{36,34},{37,35},{38,36},{39,37},{40,38},{41,39},{4... | collective-permute-start | bytes 811016 | tf_op jit(solution)/shard_map/ppermute | solution.py:229
  56.5 17.6 %collective-permute-start.6 = (bf16[528,256]{1,0:T(8,128)(2,1)}, bf16[528,256]{1,0:T(8,128)(2,1)S(1)}, u32[]{:S(2)}, u32[]{:S(2)}) collective-permute-start(bf16[528,256]{1,0:T(8,128)(2,1)} %collective-permute-done.5.refs_5_), channel_id=1, source_target_pairs={{16,30},{17,31},{18,16},{19,17},{20,18},{21,19},{22,20},{23,21},{2... | collective-permute-start | bytes 811016 | tf_op jit(solution)/shard_map/ppermute | solution.py:229
  66.9 20.7 %collective-permute-start.20 = (bf16[528,256]{1,0:T(8,128)(2,1)S(1)}, bf16[528,256]{1,0:T(8,128)(2,1)S(1)}, u32[]{:S(2)}, u32[]{:S(2)}) collective-permute-start(bf16[528,256]{1,0:T(8,128)(2,1)S(1)} %collective-permute-done.9.refs_5_), channel_id=1, source_target_pairs={{6,8},{7,9},{8,10},{9,11},{10,12},{11,13},{12,14},{13,15},{22,24},... | collective-permute-start | bytes 811016 | tf_op jit(solution)/shard_map/ppermute | solution.py:229
  67.6 20.1 %collective-permute-start.19 = (bf16[528,256]{1,0:T(8,128)(2,1)}, bf16[528,256]{1,0:T(8,128)(2,1)S(1)}, u32[]{:S(2)}, u32[]{:S(2)}) collective-permute-start(bf16[528,256]{1,0:T(8,128)(2,1)} %collective-permute-done.5.refs_5_), channel_id=1, source_target_pairs={{10,58},{11,59},{12,60},{13,61},{14,62},{15,63},{26,10},{27,11},{2... | collective-permute-start | bytes 811016 | tf_op jit(solution)/shard_map/ppermute | solution.py:229
  68.3 19.4 %collective-permute-start.13 = (bf16[528,256]{1,0:T(8,128)(2,1)S(1)}, bf16[528,256]{1,0:T(8,128)(2,1)S(1)}, u32[]{:S(2)}, u32[]{:S(2)}) collective-permute-start(bf16[528,256]{1,0:T(8,128)(2,1)S(1)} %collective-permute-done.12.refs_4_), channel_id=1, source_target_pairs={{16,32},{17,33},{18,34},{19,35},{20,36},{21,37},{32,48},{33,49},{3... | collective-permute-start | bytes 811016 | tf_op jit(solution)/shard_map/ppermute | solution.py:229
  73.5 14.2 %collective-permute-start.18 = (bf16[528,256]{1,0:T(8,128)(2,1)S(1)}, bf16[528,256]{1,0:T(8,128)(2,1)S(1)}, u32[]{:S(2)}, u32[]{:S(2)}) collective-permute-start(bf16[528,256]{1,0:T(8,128)(2,1)S(1)} %collective-permute-done.17.refs_8_), channel_id=1, source_target_pairs={{34,32},{35,33},{36,34},{37,35},{38,36},{39,37},{40,38},{41,39},{4... | collective-permute-start | bytes 811016 | tf_op jit(solution)/shard_map/ppermute | solution.py:229
  74.2 13.5 %collective-permute-start.21 = (bf16[528,256]{1,0:T(8,128)(2,1)S(1)}, bf16[528,256]{1,0:T(8,128)(2,1)S(1)}, u32[]{:S(2)}, u32[]{:S(2)}) collective-permute-start(bf16[528,256]{1,0:T(8,128)(2,1)S(1)} %collective-permute-done.6.refs_4_), channel_id=1, source_target_pairs={{16,32},{17,33},{18,34},{19,35},{20,36},{21,37},{22,38},{23,39},{3... | collective-permute-start | bytes 811016 | tf_op jit(solution)/shard_map/ppermute | solution.py:229
  92.6 6.8 %collective-permute-start.27 = (bf16[128,2048]{1,0:T(8,128)(2,1)S(1)}, bf16[128,2048]{1,0:T(8,128)(2,1)S(1)}, u32[]{:S(2)}, u32[]{:S(2)}) collective-permute-start(bf16[128,2048]{1,0:T(8,128)(2,1)S(1)} %get-tuple-element.32), channel_id=1, source_target_pairs={{0,1},{1,0},{2,3},{3,2},{4,5},{5,4},{6,7},{7,6},{8,9},{9,8},{10,11... | collective-permute-start | bytes 1572872 | tf_op jit(solution)/shard_map/ppermute | solution.py:229

commit v5 on v1

v5 whole, which is shorter than its diff:
```python
import functools
import math

import jax
import jax.numpy as jnp
from jax import lax
from jax.experimental import pallas as pl
from jax.experimental.pallas import tpu as pltpu
from jax.sharding import PartitionSpec as P

H = 16
KVH = 2
HD = 256
BLK = 128
GROUPS = H // KVH
NX, NZ = 4, 8
UNIT = 2 * BLK
META = 16
WIDE = KVH * HD
LOG2E = 1.4426950408889634
NEG = -1e30


CHIPS = [(x, z) for x in range(NX) for z in range(NZ)]


def pairs_of(core, links):
    return [
        ((ax * NZ + az) * 2 + core, (bx * NZ + bz) * 2 + core)
        for (ax, az), (bx, bz) in sorted(links)
    ]


def chain_plan(seed, source, visible, length):
    wanted = [set() for _ in range(length + 1)]
    for s in range(length, -1, -1):
        wanted[s] |= {chip for chip in CHIPS if visible(*chip, s)}
        if s:
            wanted[s - 1] |= {source(*chip) for chip in wanted[s]}
    first = {(seed(*chip), chip) for chip in wanted[0]} if seed else set()
    hops = [first]
    for s in range(1, length + 1):
        hops.append({(source(*chip), chip) for chip in wanted[s]})
    return hops


NEAR = chain_plan(
    None,
    lambda x, z: (x, z - 1) if z else ((x - 2) % NX, NZ - 1),
    lambda x, z, s: z >= s or x >= 2,
    4,
)
FAR = chain_plan(
    lambda x, z: ((x + 2) % NX, z),
    lambda x, z: (x, z + 1) if z < NZ - 1 else ((x + 2) % NX, 0),
    lambda x, z, s: z + s >= NZ or x >= 2,
    3,
)
MID_UP = chain_plan(
    lambda x, z: (x - 1, z), lambda x, z: (x, (z - 1) % NZ), lambda x, z, s: x >= 1, 3
)
MID_DOWN = chain_plan(
    None, lambda x, z: (x, (z + 1) % NZ), lambda x, z, s: x >= 1, 4
)
SWAP = [(i, i ^ 1) for i in range(2 * NX * NZ)]
UP = [pairs_of(0, NEAR[s]) + pairs_of(1, MID_UP[s - 1]) for s in range(1, 5)]
SEED = pairs_of(0, FAR[0])
DOWN = [pairs_of(0, FAR[s]) + pairs_of(1, MID_DOWN[s]) for s in range(1, 4)]
LAST = pairs_of(1, MID_DOWN[4])


def attend(first, last, paired, *refs):
    flags, core, qdocs, q_mine, q_other = refs[:5]
    rest = list(refs[5:])
    units = []
    for j, two in enumerate(paired):
        if two:
            units.append(jnp.where(core[0] == 1, rest[1][...], rest[0][...]))
        else:
            units.append(rest[0])
        rest = rest[2 if two else 1 :]
    count = len(paired)
    if not first:
        m_in, l_in, acc_in = rest[:3]
        rest = rest[3:]
    spot = lax.broadcasted_iota(jnp.int32, (BLK, BLK), 1)
    if last:
        acc_out, stats_out, share_out, share_stats_out = rest[:4]
        stats = jnp.zeros((BLK, BLK), jnp.float32)
        share_stats = jnp.zeros((BLK, BLK), jnp.float32)
    else:
        m_out, l_out, acc_out = rest[:3]
    me = core[0]
    lane = lax.broadcasted_iota(jnp.int32, (1, UNIT), 1)
    biases = []
    for j in range(count):
        kd = units[j][UNIT : UNIT + META, :UNIT].astype(jnp.float32)[0:1, :]
        halves = []
        for r in range(2):
            listed = jnp.where(lane < BLK, flags[j, 2 * r], flags[j, 2 * r + 1])
            kd_r = jnp.where(listed == 1, kd, -1.0)
            qd = qdocs[r * BLK : (r + 1) * BLK, :]
            qd = jnp.concatenate([qd, qd], axis=1)
            seen = qd == kd_r
            if first and j == 0:
                col = lax.broadcasted_iota(jnp.int32, (BLK, UNIT), 1)
                row = lax.broadcasted_iota(jnp.int32, (BLK, UNIT), 0)
                low = jnp.where(me == 0, col, lax.rem(col + BLK, UNIT))
                place = row + jnp.where(me == r, 0, BLK)
                seen = seen & (low <= place)
            halves.append(jnp.where(seen, 0.0, NEG))
        biases.append(jnp.concatenate(halves, axis=0))
    scale = LOG2E / math.sqrt(HD)
    for h in range(H):
        at = slice(h * HD, (h + 1) * HD)
        kv = slice(h // GROUPS * HD, (h // GROUPS + 1) * HD)
        qh = jnp.concatenate([q_mine[:, at], q_other[:, at]], axis=0)
        scores = []
        for j in range(count):
            s = lax.dot_general(
                qh,
                units[j][0:UNIT, kv],
                (((1,), (1,)), ((), ())),
                preferred_element_type=jnp.float32,
            )
            scores.append(s * scale + biases[j])
        top = scores[0]
        for s in scores[1:]:
            top = jnp.maximum(top, s)
        top = jnp.max(top, axis=1, keepdims=True)
        if first:
            m_new = jnp.broadcast_to(top, (UNIT, BLK))
        else:
            m_old = m_in[h]
            m_new = jnp.maximum(m_old, top)
            alpha = jnp.exp2(m_old - m_new)
        m_wide = jnp.concatenate([m_new, m_new], axis=1)
        total = None
        product = None
        for j in range(count):
            p = jnp.exp2(scores[j] - m_wide)
            part = p[:, :BLK] + p[:, BLK:]
            total = part if total is None else total + part
            pv = jnp.dot(
                p.astype(jnp.bfloat16),
                units[j][UNIT + META :, kv],
                preferred_element_type=jnp.float32,
            )
            product = pv if product is None else product + pv
        if not first:
            total = total + alpha * l_in[h]
            wide = jnp.concatenate([alpha, alpha], axis=1)
            product = product + wide * acc_in[h]
        if last:
            total = jnp.sum(total, axis=1, keepdims=True)
            acc_out[h] = product[:BLK]
            share_out[h] = (product[BLK:] / total[BLK:]).astype(jnp.bfloat16)
            stats = jnp.where(spot == h, m_new[:BLK], stats)
            stats = jnp.where(spot == H + h, total[:BLK], stats)
            share_stats = jnp.where(spot == h, m_new[BLK:], share_stats)
            share_stats = jnp.where(spot == H + h, total[BLK:], share_stats)
        else:
            m_out[h] = m_new
            l_out[h] = total
            acc_out[h] = product
    if last:
        stats_out[...] = stats
        share_stats_out[...] = share_stats


def attend_call(core, flags, queries, qdocs, units, state, last):
    paired = tuple(len(u) == 2 for u in units)
    smem = pl.BlockSpec(memory_space=pltpu.SMEM)
    vmem = pl.BlockSpec(memory_space=pltpu.VMEM)
    args = [flags, core, qdocs, *queries, *[v for u in units for v in u]]
    aliases = {}
    if state is not None:
        if not last:
            aliases = {len(args) + i: i for i in range(3)}
        args += list(state)
    if last:
        shapes = [
            jax.ShapeDtypeStruct((H, BLK, HD), jnp.float32),
            jax.ShapeDtypeStruct((BLK, BLK), jnp.float32),
            jax.ShapeDtypeStruct((H, BLK, HD), jnp.bfloat16),
            jax.ShapeDtypeStruct((BLK, BLK), jnp.float32),
        ]
    else:
        shapes = [
            jax.ShapeDtypeStruct((H, UNIT, BLK), jnp.float32),
            jax.ShapeDtypeStruct((H, UNIT, BLK), jnp.float32),
            jax.ShapeDtypeStruct((H, UNIT, HD), jnp.float32),
        ]
    return pl.pallas_call(
        functools.partial(attend, state is None, last, paired),
        out_shape=shapes,
        in_specs=[smem, smem] + [vmem] * (len(args) - 2),
        out_specs=[vmem] * len(shapes),
        input_output_aliases=aliases,
        compiler_params=pltpu.CompilerParams(vmem_limit_bytes=24 << 20),
        cost_estimate=pl.CostEstimate(
            flops=12 * H * UNIT * UNIT * HD * len(units),
            bytes_accessed=len(units) * 540000 + 9000000,
            transcendentals=H * UNIT * UNIT * len(units),
        ),
    )(*args)


def combine(acc, stats, share, share_stats, gate, out):
    for h in range(H):
        at = slice(h * HD, (h + 1) * HD)
        m0, m1 = stats[:, h : h + 1], share_stats[:, h : h + 1]
        l0, l1 = stats[:, H + h : H + h + 1], share_stats[:, H + h : H + h + 1]
        top = jnp.maximum(m0, m1)
        e0 = jnp.exp2(m0 - top)
        e1 = jnp.exp2(m1 - top) * l1
        inv = 1.0 / (l0 * e0 + e1)
        att = acc[h] * (e0 * inv) + share[h].astype(jnp.float32) * (e1 * inv)
        g = gate[:, at].astype(jnp.float32)
        out[:, at] = (att * jax.nn.sigmoid(g)).astype(jnp.bfloat16)


def combine_call(*args):
    vmem = pl.BlockSpec(memory_space=pltpu.VMEM)
    return pl.pallas_call(
        combine,
        out_shape=jax.ShapeDtypeStruct((BLK, H * HD), jnp.bfloat16),
        in_specs=[vmem] * len(args),
        out_specs=vmem,
        compiler_params=pltpu.CompilerParams(vmem_limit_bytes=24 << 20),
    )(*args)


def on_device(query_rows, key_rows, value_rows, gate_rows, doc_ids, block_lists):
    place = lax.axis_index("cp")
    core = lax.rem(place, 2)
    chip = place // 2
    x, z = chip // NZ, lax.rem(chip, NZ)

    def send(value, pairs):
        return lax.ppermute(value, "cp", pairs)

    docs_row = doc_ids.astype(jnp.bfloat16).reshape(1, BLK)
    lists_row = jnp.pad(
        block_lists.astype(jnp.bfloat16), ((0, 0), (0, BLK - block_lists.shape[1]))
    )
    notes = jnp.concatenate(
        [docs_row, lists_row, jnp.zeros((META - 2, BLK), jnp.bfloat16)], axis=0
    )
    notes_wide = jnp.pad(notes, ((0, 0), (0, WIDE - BLK)))
    parcel = jnp.concatenate([key_rows, value_rows, notes_wide], axis=0)
    got = send(parcel, SWAP)
    unit = jnp.concatenate(
        [
            key_rows,
            got[:BLK],
            jnp.concatenate(
                [notes, got[2 * BLK :, :BLK], jnp.zeros((META, WIDE - UNIT), jnp.bfloat16)],
                axis=1,
            ),
            value_rows,
            got[BLK : 2 * BLK],
        ],
        axis=0,
    )
    query_rows, _ = lax.optimization_barrier((query_rows, parcel))
    queries = (query_rows, send(query_rows, SWAP))

    up = [send(unit, UP[0])]
    seed = send(unit, SEED)
    down = [jnp.where(core == 0, seed, up[0])]
    for s in range(3):
        up.append(send(up[-1], UP[s + 1]))
        down.append(send(down[-1], DOWN[s]))
    end = send(down[-1], LAST)

    meta = unit[UNIT : UNIT + 2, :UNIT].astype(jnp.float32)
    qdocs = jnp.broadcast_to(meta[0][:, None], (UNIT, BLK))
    lists = jnp.stack([meta[1, :64], meta[1, BLK : BLK + 64]])

    def near_id(s):
        return jnp.where(z >= s, chip - s, jnp.where(x >= 2, chip - s - NZ, -1))

    def far_id(s):
        return jnp.where(
            z + s < NZ, jnp.where(x >= 2, chip - 2 * NZ + s, -1), chip + s - NZ
        )

    def mid_id(s):
        return jnp.where(x >= 1, (x - 1) * NZ + lax.rem(z + s + NZ, NZ), -1)

    groups = [
        [((unit,), chip, -1), ((up[0],), near_id(1), mid_id(0))],
        [((up[1],), near_id(2), mid_id(-1)), ((down[1],), far_id(1), mid_id(1))],
        [((up[2],), near_id(3), mid_id(-2)), ((down[2],), far_id(2), mid_id(2))],
        [((up[3],), near_id(4), mid_id(-3)), ((down[3],), far_id(3), mid_id(3))],
        [((seed, end), far_id(0), mid_id(4))],
    ]
    ids = jnp.stack([jnp.where(core == 0, a, b) for group in groups for _, a, b in group])
    cols = 2 * ids[:, None] + jnp.stack([core, 1 - core])[None, :]
    cols = jnp.where(ids[:, None] >= 0, cols, -1)
    hot = cols[:, None, :, None] == jnp.arange(64, dtype=jnp.int32)[None, None, None, :]
    table = jnp.sum(jnp.where(hot, lists[None, :, None, :], 0.0), axis=-1)
    table = table.astype(jnp.int32).reshape(ids.shape[0], 4)

    core1 = core.reshape(1)
    state = None
    at = 0
    for n, group in enumerate(groups):
        flags = table[at : at + len(group)]
        at += len(group)
        state = attend_call(
            core1, flags, queries, qdocs, [g[0] for g in group], state, n == len(groups) - 1
        )
    acc, stats, share, share_stats = state
    return combine_call(acc, stats, send(share, SWAP), send(share_stats, SWAP), gate_rows)


def solution(mesh):
    return jax.shard_map(
        on_device,
        mesh=mesh,
        in_specs=(
            P(("dp", "cp"), None),
            P(("dp", "cp"), None),
            P(("dp", "cp"), None),
            P(("dp", "cp"), None),
            P(("dp", "cp")),
            P(("dp", "cp"), None),
        ),
        out_specs=P(("dp", "cp"), None),
        check_vma=False,
    )
```

time: 92.1 us -> 97.9 us (1.063)
  starting transfers between devices: 59.5 us -> 36 us
  waiting for transfers between devices: 3.37 us -> 23.3 us
  Pallas kernels: 20.7 us -> 32.4 us
  local copies, waits for them, and re-layouts: 4.46 us -> 2.47 us
    ppermute x20 -> x13, starting transfers between devices: 59.5 us -> 36 us  [send(): return lax.ppermute(value, 'cp', pairs)]
    ppermute x20 -> x13, waiting for transfers between devices: 3.37 us -> 23.3 us  [send(): return lax.ppermute(value, 'cp', pairs)]
    pallas_call x5 -> x6, Pallas kernels: 20.7 us -> 32.4 us  [the longest x5 27.5 us: attend_call(): pl.pallas_call(functools.partial(attend, state is None, last, paired), ou...]
    dynamic_slice x2 -> x0, local copies, waits for them, and re-layouts: 3.25 us -> none  [take(): return lax.dynamic_slice_in_dim(rows, which * width, width, 1)]
    unnamed x13 -> x7, local copies, waits for them, and re-layouts: 0.06 us -> 1.85 us
    select_n x1, other arithmetic: 1.21 us -> 0.06 us  [on_device(): down = [jnp.where(core == 0, seed, up[0])]]
  transfers between devices with their start and end apart: 20 -> 13, of which waited for: 3 -> 5; matrix products, arithmetic and copies ran while one was open for 4% -> 3% of each run, Pallas kernels for 16% -> 23%
where the time goes in v5:
time: 97.9 us; the launch traced here: 97.3 us
  starting transfers between devices  36 us (37%)
  Pallas kernels  32.4 us (33%)
  waiting for transfers between devices  23.3 us (24%)
  other arithmetic  2.86 us (3%)
  local copies, waits for them, and re-layouts  2.47 us (3%)
    ppermute x13, starting transfers between devices, send(): return lax.ppermute(value, 'cp', pairs)  36 us
    pallas_call x5, Pallas kernels, attend_call(): pl.pallas_call(functools.partial(attend, state is None, last, paired), ou...  27.5 us
    ppermute x13, waiting for transfers between devices, send(): return lax.ppermute(value, 'cp', pairs)  23.3 us
    pallas_call x1, Pallas kernels, combine_call(): pl.pallas_call(combine, out_shape=jax.ShapeDtypeStruct((BLK, H * HD), jnp...  4.91 us
  transfers between devices with their start and end apart: 13, of which 5 were waited for; matrix products, arithmetic and copies ran while one was open for 3% of the time, Pallas kernels for 23%

profile of v5, /device:TPU:15, one launch (start us, length us, event | category | flops | bytes accessed | tf_op | source)
XLA Modules:
  0.0 97.3 jit_solution(9568997933977027253)
XLA Ops:
  0.0 0.7 convert_element_type.17
  0.8 0.7 convert_bitcast_fusion
  1.4 1.0 %pad_maximum_fusion = bf16[272,512]{1,0:T(8,128)(2,1)S(1)} fusion(bf16[16,512]{1,0:T(8,128)(2,1)S(1)} %fusion.7, bf16[128,512]{1,0:T(8,128)(2,1)} %param.8, bf16[128,512]{1,0:T(8,128)(2,1)} %param.7), kind=kLoop, calls=%fused_computation.1 | loop fusion | flops 835584 | bytes 557056 | tf_op jit(solution)/shard_map/concatenate | solution.py:251
  2.4 0.8 collective-permute-start
  3.2 0.1 collective-permute-start.1
  3.3 0.1 stack.51
  3.4 0.1 pad_add_fusion
  3.5 0.1 add_select_fusion
  3.5 0.9 constant_dynamic-update-slice_fusion.1
  4.5 0.1 iota_compare_fusion.1
  4.6 0.0 collective-permute-done
  4.6 0.9 constant_dynamic-update-slice_fusion
  5.6 1.3 %collective-permute-start.3 = (bf16[528,512]{1,0:T(8,128)(2,1)S(1)}, bf16[528,512]{1,0:T(8,128)(2,1)S(1)}, u32[]{:S(2)}, u32[]{:S(2)}) collective-permute-start(bf16[528,512]{1,0:T(8,128)(2,1)S(1)} %slice_dynamic-update-slice_fusion.refs_5_), channel_id=1, source_target_pairs={{0,2},{2,4},{4,6},{6,8},{8,10},{10,12},{12,14},{14,32},{16,18},{18... | collective-permute-start | bytes 1622024 | tf_op jit(solution)/shard_map/ppermute | solution.py:241
  6.9 0.7 collective-permute-start.2
  7.6 0.1 select_reduce_fusion
  7.8 0.1 slice.68.refs_0_
  7.8 0.1 slice.66.refs_0_
  7.9 0.1 slice.64.refs_0_
  8.0 0.1 slice.62.refs_0_
  8.1 0.1 slice.57.refs_0_
  8.2 9.5 %collective-permute-done.3.refs_6_ = bf16[528,512]{1,0:T(8,128)(2,1)S(1)} collective-permute-done((bf16[528,512]{1,0:T(8,128)(2,1)S(1)}, bf16[528,512]{1,0:T(8,128)(2,1)S(1)}, u32[]{:S(2)}, u32[]{:S(2)}) %collective-permute-start.3) | collective-permute-done | bytes 540704 | tf_op jit(solution)/shard_map/ppermute | solution.py:241
  17.7 0.0 collective-permute-done.2.refs_5_
  17.7 0.1 broadcast_select_fusion
  17.7 5.8 %collective-permute-start.4 = (bf16[528,512]{1,0:T(8,128)(2,1)S(1)}, bf16[528,512]{1,0:T(8,128)(2,1)S(1)}, u32[]{:S(2)}, u32[]{:S(2)}) collective-permute-start(bf16[528,512]{1,0:T(8,128)(2,1)S(1)} %broadcast_select_fusion), channel_id=1, source_target_pairs={{0,46},{2,0},{4,2},{16,62},{18,16},{20,18},{32,14},{34,32},{36,34}... | collective-permute-start | bytes 1622024 | tf_op jit(solution)/shard_map/ppermute | solution.py:241
  23.5 1.9 %collective-permute-start.8 = (bf16[528,512]{1,0:T(8,128)(2,1)S(1)}, bf16[528,512]{1,0:T(8,128)(2,1)S(1)}, u32[]{:S(2)}, u32[]{:S(2)}) collective-permute-start(bf16[528,512]{1,0:T(8,128)(2,1)S(1)} %collective-permute-done.3.refs_6_), channel_id=1, source_target_pairs={{2,4},{4,6},{6,8},{8,10},{10,12},{12,14},{14,32},{18,20},{20,22},{... | collective-permute-start | bytes 1622024 | tf_op jit(solution)/shard_map/ppermute | solution.py:241
  25.5 0.0 collective-permute-done.1.refs_4_
  25.5 0.1 broadcast_in_dim.58.refs_2_
  25.6 4.3 %shard_map.64 = (f32[16,256,128]{2,1,0:T(8,128)S(1)}, f32[16,256,128]{2,1,0:T(8,128)S(1)}, f32[16,256,256]{2,1,0:T(8,128)S(1)}) custom-call(s32[2,4]{1,0:T(2,128)S(1)} %slice.68.refs_0_, s32[1]{0:T(128)} %bitcast.9.refs_1_, f32[256,128]{1,0:T(8,128)S(1)} %broadcast_in_dim.58.refs_2_, bf16[128,4096]{1,0:T(8,128)(2,1)S(1)} %copy-done.1, ...), custom_call_target="tpu_custom_call" | custom-call | flops 6442450944 | bytes 10080000 | tf_op jit(solution)/shard_map/pallas_call | solution.py:194
  29.8 0.0 collective-permute-done.4.refs_6_
  29.9 5.0 %collective-permute-start.5 = (bf16[528,512]{1,0:T(8,128)(2,1)S(1)}, bf16[528,512]{1,0:T(8,128)(2,1)S(1)}, u32[]{:S(2)}, u32[]{:S(2)}) collective-permute-start(bf16[528,512]{1,0:T(8,128)(2,1)S(1)} %collective-permute-done.4.refs_6_), channel_id=1, source_target_pairs={{0,46},{2,0},{14,12},{16,62},{18,16},{30,28},{32,14},{34,32},{36,3... | collective-permute-start | bytes 1622024 | tf_op jit(solution)/shard_map/ppermute | solution.py:241
  34.8 0.0 collective-permute-done.8.refs_5_
  34.8 1.9 %collective-permute-start.9 = (bf16[528,512]{1,0:T(8,128)(2,1)S(1)}, bf16[528,512]{1,0:T(8,128)(2,1)S(1)}, u32[]{:S(2)}, u32[]{:S(2)}) collective-permute-start(bf16[528,512]{1,0:T(8,128)(2,1)S(1)} %collective-permute-done.8.refs_5_), channel_id=1, source_target_pairs={{4,6},{6,8},{8,10},{10,12},{12,14},{14,32},{20,22},{22,24},{24,26}... | collective-permute-start | bytes 1622024 | tf_op jit(solution)/shard_map/ppermute | solution.py:241
  36.8 6.1 %shard_map.65 = (f32[16,256,128]{2,1,0:T(8,128)S(1)}, f32[16,256,128]{2,1,0:T(8,128)S(1)}, f32[16,256,256]{2,1,0:T(8,128)S(1)}) custom-call(s32[2,4]{1,0:T(2,128)S(1)} %slice.66.refs_0_, s32[1]{0:T(128)} %bitcast.9.refs_1_, f32[256,128]{1,0:T(8,128)S(1)} %broadcast_in_dim.58.refs_2_, ...), custom_call_target="tpu_custom_call", output_to_operand_aliasing={{0}: (7, {}), {1}: (8, {}), {2}: (9, {})} | custom-call | flops 6442450944 | bytes 10080000 | tf_op jit(solution)/shard_map/pallas_call | solution.py:194
  42.9 1.3 %collective-permute-done.5.refs_6_ = bf16[528,512]{1,0:T(8,128)(2,1)S(1)} collective-permute-done((bf16[528,512]{1,0:T(8,128)(2,1)S(1)}, bf16[528,512]{1,0:T(8,128)(2,1)S(1)}, u32[]{:S(2)}, u32[]{:S(2)}) %collective-permute-start.5) | collective-permute-done | bytes 540704 | tf_op jit(solution)/shard_map/ppermute | solution.py:241
  44.2 3.3 %collective-permute-start.6 = (bf16[528,512]{1,0:T(8,128)(2,1)S(1)}, bf16[528,512]{1,0:T(8,128)(2,1)S(1)}, u32[]{:S(2)}, u32[]{:S(2)}) collective-permute-start(bf16[528,512]{1,0:T(8,128)(2,1)S(1)} %collective-permute-done.5.refs_6_), channel_id=1, source_target_pairs={{0,46},{12,10},{14,12},{16,62},{28,26},{30,28},{32,14},{34,32},{36... | collective-permute-start | bytes 1622024 | tf_op jit(solution)/shard_map/ppermute | solution.py:241
  47.4 0.0 collective-permute-done.9.refs_5_
  47.5 2.7 %collective-permute-start.10 = (bf16[528,512]{1,0:T(8,128)(2,1)S(1)}, bf16[528,512]{1,0:T(8,128)(2,1)S(1)}, u32[]{:S(2)}, u32[]{:S(2)}) collective-permute-start(bf16[528,512]{1,0:T(8,128)(2,1)S(1)} %collective-permute-done.9.refs_5_), channel_id=1, source_target_pairs={{6,8},{8,10},{10,12},{12,14},{14,32},{22,24},{24,26},{26,28},{28,3... | collective-permute-start | bytes 1622024 | tf_op jit(solution)/shard_map/ppermute | solution.py:241
  50.2 6.1 %shard_map.66 = (f32[16,256,128]{2,1,0:T(8,128)S(1)}, f32[16,256,128]{2,1,0:T(8,128)S(1)}, f32[16,256,256]{2,1,0:T(8,128)S(1)}) custom-call(s32[2,4]{1,0:T(2,128)S(1)} %slice.64.refs_0_, s32[1]{0:T(128)} %bitcast.9.refs_1_, f32[256,128]{1,0:T(8,128)S(1)} %broadcast_in_dim.58.refs_2_, ...), custom_call_target="tpu_custom_call", output_to_operand_aliasing={{0}: (7, {}), {1}: (8, {}), {2}: (9, {})} | custom-call | flops 6442450944 | bytes 10080000 | tf_op jit(solution)/shard_map/pallas_call | solution.py:194
  56.3 3.5 %collective-permute-done.6.refs_6_ = bf16[528,512]{1,0:T(8,128)(2,1)S(1)} collective-permute-done((bf16[528,512]{1,0:T(8,128)(2,1)S(1)}, bf16[528,512]{1,0:T(8,128)(2,1)S(1)}, u32[]{:S(2)}, u32[]{:S(2)}) %collective-permute-start.6) | collective-permute-done | bytes 540704 | tf_op jit(solution)/shard_map/ppermute | solution.py:241
  59.8 2.8 %collective-permute-start.7 = (bf16[528,512]{1,0:T(8,128)(2,1)S(1)}, bf16[528,512]{1,0:T(8,128)(2,1)S(1)}, u32[]{:S(2)}, u32[]{:S(2)}) collective-permute-start(bf16[528,512]{1,0:T(8,128)(2,1)S(1)} %collective-permute-done.6.refs_6_), channel_id=1, source_target_pairs={{17,31},{19,17},{21,19},{23,21},{25,23},{27,25},{29,27},{31,29},{3... | collective-permute-start | bytes 1622024 | tf_op jit(solution)/shard_map/ppermute | solution.py:241
  62.6 0.0 collective-permute-done.10.refs_5_
  62.6 6.3 %shard_map.67 = (f32[16,256,128]{2,1,0:T(8,128)S(1)}, f32[16,256,128]{2,1,0:T(8,128)S(1)}, f32[16,256,256]{2,1,0:T(8,128)S(1)}) custom-call(s32[2,4]{1,0:T(2,128)S(1)} %slice.62.refs_0_, s32[1]{0:T(128)} %bitcast.9.refs_1_, f32[256,128]{1,0:T(8,128)S(1)} %broadcast_in_dim.58.refs_2_, ...), custom_call_target="tpu_custom_call", output_to_operand_aliasing={{0}: (7, {}), {1}: (8, {}), {2}: (9, {})} | custom-call | flops 6442450944 | bytes 10080000 | tf_op jit(solution)/shard_map/pallas_call | solution.py:194
  68.9 6.7 %collective-permute-done.7.refs_6_ = bf16[528,512]{1,0:T(8,128)(2,1)S(1)} collective-permute-done((bf16[528,512]{1,0:T(8,128)(2,1)S(1)}, bf16[528,512]{1,0:T(8,128)(2,1)S(1)}, u32[]{:S(2)}, u32[]{:S(2)}) %collective-permute-start.7) | collective-permute-done | bytes 540704 | tf_op jit(solution)/shard_map/ppermute | solution.py:241
  75.6 4.7 %shard_map.68 = (f32[16,128,256]{2,1,0:T(8,128)S(1)}, f32[128,128]{1,0:T(8,128)S(1)}, bf16[16,128,256]{2,1,0:T(8,128)(2,1)S(1)}, f32[128,128]{1,0:T(8,128)S(1)}) custom-call(s32[1,4]{1,0:T(1,128)S(1)} %slice.57.refs_0_, s32[1]{0:T(128)} %bitcast.9.refs_1_, f32[256,128]{1,0:T(8,128)S(1)} %broadcast_in_dim.58.refs_2_, bf16[128,4096]{1,0:T(8,128)(2,1)S(1)} %copy-done.1, ...), custom_call_target="tpu_custom_call" | custom-call | flops 3221225472 | bytes 9540000 | tf_op jit(solution)/shard_map/pallas_call | solution.py:194
  80.3 9.7 %collective-permute-start.11 = (bf16[16,128,256]{2,1,0:T(8,128)(2,1)S(1)}, bf16[16,128,256]{2,1,0:T(8,128)(2,1)S(1)}, u32[]{:S(2)}, u32[]{:S(2)}) collective-permute-start(bf16[16,128,256]{2,1,0:T(8,128)(2,1)S(1)} %get-tuple-element.37), channel_id=1, source_target_pairs={{0,1},{1,0},{2,3},{3,2},{4,5},{5,4},{6,7},{7,6},{8,9},{9,8},{10,11... | collective-permute-start | bytes 3145736 | tf_op jit(solution)/shard_map/ppermute | solution.py:241
  90.0 0.1 collective-permute-start.12
  90.1 2.3 %collective-permute-done.12.share_stats = f32[128,128]{1,0:T(8,128)S(1)} collective-permute-done((f32[128,128]{1,0:T(8,128)S(1)}, f32[128,128]{1,0:T(8,128)S(1)}, u32[]{:S(2)}, u32[]{:S(2)}) %collective-permute-start.12) | collective-permute-done | bytes 65568 | tf_op jit(solution)/shard_map/ppermute | solution.py:241
  92.4 4.9 %shard_map.69 = bf16[128,4096]{1,0:T(8,128)(2,1)} custom-call(f32[16,128,256]{2,1,0:T(8,128)S(1)} %get-tuple-element.35.acc, f32[128,128]{1,0:T(8,128)S(1)} %get-tuple-element.36.stats, bf16[16,128,256]{2,1,0:T(8,128)(2,1)S(1)} %collective-permute-done.11.share, f32[128,128]{1,0:T(8,128)S(1)} %collective-permute-done.12.share_stats, ...), custom_call_target="tpu_custom_call" | custom-call | tf_op jit(solution)/shard_map/pallas_call | solution.py:225
  (22 shorter events, 0.1 us)
Async XLA Ops:
  0.0 25.6 %copy-start.1 = (bf16[128,4096]{1,0:T(8,128)(2,1)S(1)}, bf16[128,4096]{1,0:T(8,128)(2,1)}, u32[]{:S(2)}) copy-start(bf16[128,4096]{1,0:T(8,128)(2,1)} %refs_3_.4) | copy-start | bytes 3145732
  2.4 2.1 %collective-permute-start = (bf16[272,512]{1,0:T(8,128)(2,1)S(1)}, bf16[272,512]{1,0:T(8,128)(2,1)S(1)}, u32[]{:S(2)}, u32[]{:S(2)}) collective-permute-start(bf16[272,512]{1,0:T(8,128)(2,1)S(1)} %pad_maximum_fusion), channel_id=1, source_target_pairs={{0,1},{1,0},{2,3},{3,2},{4,5},{5,4},{6,7},{7,6},{8,9},{9,8},{10,11... | collective-permute-start | bytes 835592 | tf_op jit(solution)/shard_map/ppermute | solution.py:241
  3.2 22.3 %collective-permute-start.1 = (bf16[128,4096]{1,0:T(8,128)(2,1)}, bf16[128,4096]{1,0:T(8,128)(2,1)}, u32[]{:S(2)}, u32[]{:S(2)}) collective-permute-start(bf16[128,4096]{1,0:T(8,128)(2,1)} %refs_3_.4), channel_id=1, source_target_pairs={{0,1},{1,0},{2,3},{3,2},{4,5},{5,4},{6,7},{7,6},{8,9},{9,8},{10,11... | collective-permute-start | bytes 3145736 | tf_op jit(solution)/shard_map/ppermute | solution.py:241
  5.6 12.1 %collective-permute-start.3 = (bf16[528,512]{1,0:T(8,128)(2,1)S(1)}, bf16[528,512]{1,0:T(8,128)(2,1)S(1)}, u32[]{:S(2)}, u32[]{:S(2)}) collective-permute-start(bf16[528,512]{1,0:T(8,128)(2,1)S(1)} %slice_dynamic-update-slice_fusion.refs_5_), channel_id=1, source_target_pairs={{0,2},{2,4},{4,6},{6,8},{8,10},{10,12},{12,14},{14,32},{16,18},{18... | collective-permute-start | bytes 1622024 | tf_op jit(solution)/shard_map/ppermute | solution.py:241
  6.9 10.8 %collective-permute-start.2 = (bf16[528,512]{1,0:T(8,128)(2,1)S(1)}, bf16[528,512]{1,0:T(8,128)(2,1)S(1)}, u32[]{:S(2)}, u32[]{:S(2)}) collective-permute-start(bf16[528,512]{1,0:T(8,128)(2,1)S(1)} %slice_dynamic-update-slice_fusion.refs_5_), channel_id=1, source_target_pairs={{0,32},{2,34},{4,36},{6,38},{8,40},{10,42},{12,44},{14,46},{16,48}... | collective-permute-start | bytes 1622024 | tf_op jit(solution)/shard_map/ppermute | solution.py:241
  17.7 12.1 %collective-permute-start.4 = (bf16[528,512]{1,0:T(8,128)(2,1)S(1)}, bf16[528,512]{1,0:T(8,128)(2,1)S(1)}, u32[]{:S(2)}, u32[]{:S(2)}) collective-permute-start(bf16[528,512]{1,0:T(8,128)(2,1)S(1)} %broadcast_select_fusion), channel_id=1, source_target_pairs={{0,46},{2,0},{4,2},{16,62},{18,16},{20,18},{32,14},{34,32},{36,34}... | collective-permute-start | bytes 1622024 | tf_op jit(solution)/shard_map/ppermute | solution.py:241
  23.5 11.3 %collective-permute-start.8 = (bf16[528,512]{1,0:T(8,128)(2,1)S(1)}, bf16[528,512]{1,0:T(8,128)(2,1)S(1)}, u32[]{:S(2)}, u32[]{:S(2)}) collective-permute-start(bf16[528,512]{1,0:T(8,128)(2,1)S(1)} %collective-permute-done.3.refs_6_), channel_id=1, source_target_pairs={{2,4},{4,6},{6,8},{8,10},{10,12},{12,14},{14,32},{18,20},{20,22},{... | collective-permute-start | bytes 1622024 | tf_op jit(solution)/shard_map/ppermute | solution.py:241
  29.9 14.3 %collective-permute-start.5 = (bf16[528,512]{1,0:T(8,128)(2,1)S(1)}, bf16[528,512]{1,0:T(8,128)(2,1)S(1)}, u32[]{:S(2)}, u32[]{:S(2)}) collective-permute-start(bf16[528,512]{1,0:T(8,128)(2,1)S(1)} %collective-permute-done.4.refs_6_), channel_id=1, source_target_pairs={{0,46},{2,0},{14,12},{16,62},{18,16},{30,28},{32,14},{34,32},{36,3... | collective-permute-start | bytes 1622024 | tf_op jit(solution)/shard_map/ppermute | solution.py:241
  34.8 12.6 %collective-permute-start.9 = (bf16[528,512]{1,0:T(8,128)(2,1)S(1)}, bf16[528,512]{1,0:T(8,128)(2,1)S(1)}, u32[]{:S(2)}, u32[]{:S(2)}) collective-permute-start(bf16[528,512]{1,0:T(8,128)(2,1)S(1)} %collective-permute-done.8.refs_5_), channel_id=1, source_target_pairs={{4,6},{6,8},{8,10},{10,12},{12,14},{14,32},{20,22},{22,24},{24,26}... | collective-permute-start | bytes 1622024 | tf_op jit(solution)/shard_map/ppermute | solution.py:241
  44.2 15.6 %collective-permute-start.6 = (bf16[528,512]{1,0:T(8,128)(2,1)S(1)}, bf16[528,512]{1,0:T(8,128)(2,1)S(1)}, u32[]{:S(2)}, u32[]{:S(2)}) collective-permute-start(bf16[528,512]{1,0:T(8,128)(2,1)S(1)} %collective-permute-done.5.refs_6_), channel_id=1, source_target_pairs={{0,46},{12,10},{14,12},{16,62},{28,26},{30,28},{32,14},{34,32},{36... | collective-permute-start | bytes 1622024 | tf_op jit(solution)/shard_map/ppermute | solution.py:241
  47.5 15.2 %collective-permute-start.10 = (bf16[528,512]{1,0:T(8,128)(2,1)S(1)}, bf16[528,512]{1,0:T(8,128)(2,1)S(1)}, u32[]{:S(2)}, u32[]{:S(2)}) collective-permute-start(bf16[528,512]{1,0:T(8,128)(2,1)S(1)} %collective-permute-done.9.refs_5_), channel_id=1, source_target_pairs={{6,8},{8,10},{10,12},{12,14},{14,32},{22,24},{24,26},{26,28},{28,3... | collective-permute-start | bytes 1622024 | tf_op jit(solution)/shard_map/ppermute | solution.py:241
  59.8 15.8 %collective-permute-start.7 = (bf16[528,512]{1,0:T(8,128)(2,1)S(1)}, bf16[528,512]{1,0:T(8,128)(2,1)S(1)}, u32[]{:S(2)}, u32[]{:S(2)}) collective-permute-start(bf16[528,512]{1,0:T(8,128)(2,1)S(1)} %collective-permute-done.6.refs_6_), channel_id=1, source_target_pairs={{17,31},{19,17},{21,19},{23,21},{25,23},{27,25},{29,27},{31,29},{3... | collective-permute-start | bytes 1622024 | tf_op jit(solution)/shard_map/ppermute | solution.py:241
  75.6 16.8 %copy-start = (bf16[128,4096]{1,0:T(8,128)(2,1)S(1)}, bf16[128,4096]{1,0:T(8,128)(2,1)}, u32[]{:S(2)}) copy-start(bf16[128,4096]{1,0:T(8,128)(2,1)} %gate.1) | copy-start | bytes 3145732
  80.3 12.0 %collective-permute-start.11 = (bf16[16,128,256]{2,1,0:T(8,128)(2,1)S(1)}, bf16[16,128,256]{2,1,0:T(8,128)(2,1)S(1)}, u32[]{:S(2)}, u32[]{:S(2)}) collective-permute-start(bf16[16,128,256]{2,1,0:T(8,128)(2,1)S(1)} %get-tuple-element.37), channel_id=1, source_target_pairs={{0,1},{1,0},{2,3},{3,2},{4,5},{5,4},{6,7},{7,6},{8,9},{9,8},{10,11... | collective-permute-start | bytes 3145736 | tf_op jit(solution)/shard_map/ppermute | solution.py:241
  90.0 2.4 %collective-permute-start.12 = (f32[128,128]{1,0:T(8,128)S(1)}, f32[128,128]{1,0:T(8,128)S(1)}, u32[]{:S(2)}, u32[]{:S(2)}) collective-permute-start(f32[128,128]{1,0:T(8,128)S(1)} %get-tuple-element.38), channel_id=1, source_target_pairs={{0,1},{1,0},{2,3},{3,2},{4,5},{5,4},{6,7},{7,6},{8,9},{9,8},{10,11... | collective-permute-start | bytes 196616 | tf_op jit(solution)/shard_map/ppermute | solution.py:241

commit v6 on v5

--- a/solution.py
+++ b/solution.py
@@ -65,8 +65,8 @@
 SWAP = [(i, i ^ 1) for i in range(2 * NX * NZ)]
 UP = [pairs_of(0, NEAR[s]) + pairs_of(1, MID_UP[s - 1]) for s in range(1, 5)]
 SEED = pairs_of(0, FAR[0])
-DOWN = [pairs_of(0, FAR[s]) + pairs_of(1, MID_DOWN[s]) for s in range(1, 4)]
-LAST = pairs_of(1, MID_DOWN[4])
+LEAD = pairs_of(1, MID_DOWN[1])
+DOWN = [pairs_of(0, FAR[s]) + pairs_of(1, MID_DOWN[s + 1]) for s in range(1, 4)]
 
 
 def attend(first, last, paired, *refs):
@@ -206,18 +206,37 @@
     )(*args)
 
 
-def combine(acc, stats, share, share_stats, gate, out):
+def gate_sigmoid(gate, out):
     for h in range(H):
         at = slice(h * HD, (h + 1) * HD)
-        m0, m1 = stats[:, h : h + 1], share_stats[:, h : h + 1]
-        l0, l1 = stats[:, H + h : H + h + 1], share_stats[:, H + h : H + h + 1]
-        top = jnp.maximum(m0, m1)
-        e0 = jnp.exp2(m0 - top)
-        e1 = jnp.exp2(m1 - top) * l1
-        inv = 1.0 / (l0 * e0 + e1)
-        att = acc[h] * (e0 * inv) + share[h].astype(jnp.float32) * (e1 * inv)
-        g = gate[:, at].astype(jnp.float32)
-        out[:, at] = (att * jax.nn.sigmoid(g)).astype(jnp.bfloat16)
+        out[:, at] = jax.nn.sigmoid(gate[:, at].astype(jnp.float32))
+
+
+def sigmoid_call(gate_rows):
+    vmem = pl.BlockSpec(memory_space=pltpu.VMEM)
+    return pl.pallas_call(
+        gate_sigmoid,
+        out_shape=jax.ShapeDtypeStruct(gate_rows.shape, jnp.float32),
+        in_specs=[vmem],
+        out_specs=vmem,
+        cost_estimate=pl.CostEstimate(
+            flops=2000000000, bytes_accessed=3000000, transcendentals=1000000
+        ),
+    )(gate_rows)
+
+
+def combine(acc, stats, share, share_stats, sigmoid, out):
+    m0, m1 = stats[...], share_stats[...]
+    l0, l1 = (pltpu.roll(v, BLK - H, 1) for v in (m0, m1))
+    top = jnp.maximum(m0, m1)
+    e0 = jnp.exp2(m0 - top)
+    e1 = jnp.exp2(m1 - top) * l1
+    inv = 1.0 / (l0 * e0 + e1)
+    w0, w1 = e0 * inv, e1 * inv
+    for h in range(H):
+        at = slice(h * HD, (h + 1) * HD)
+        att = acc[h] * w0[:, h : h + 1] + share[h].astype(jnp.float32) * w1[:, h : h + 1]
+        out[:, at] = (att * sigmoid[:, at]).astype(jnp.bfloat16)
 
 
 def combine_call(*args):
@@ -268,11 +287,9 @@
 
     up = [send(unit, UP[0])]
     seed = send(unit, SEED)
-    down = [jnp.where(core == 0, seed, up[0])]
-    for s in range(3):
-        up.append(send(up[-1], UP[s + 1]))
-        down.append(send(down[-1], DOWN[s]))
-    end = send(down[-1], LAST)
+    up.append(send(up[0], UP[1]))
+    lead = send(up[0], LEAD)
+    sigmoid = sigmoid_call(gate_rows)
 
     meta = unit[UNIT : UNIT + 2, :UNIT].astype(jnp.float32)
     qdocs = jnp.broadcast_to(meta[0][:, None], (UNIT, BLK))
@@ -290,13 +307,13 @@
         return jnp.where(x >= 1, (x - 1) * NZ + lax.rem(z + s + NZ, NZ), -1)
 
     groups = [
-        [((unit,), chip, -1), ((up[0],), near_id(1), mid_id(0))],
-        [((up[1],), near_id(2), mid_id(-1)), ((down[1],), far_id(1), mid_id(1))],
-        [((up[2],), near_id(3), mid_id(-2)), ((down[2],), far_id(2), mid_id(2))],
-        [((up[3],), near_id(4), mid_id(-3)), ((down[3],), far_id(3), mid_id(3))],
-        [((seed, end), far_id(0), mid_id(4))],
+        [(chip, -1), (near_id(1), mid_id(0))],
+        [(far_id(0), mid_id(1)), (near_id(2), mid_id(-1))],
+        [(far_id(1), mid_id(2)), (near_id(3), mid_id(-2))],
+        [(far_id(2), mid_id(3)), (near_id(4), mid_id(-3))],
+        [(far_id(3), mid_id(4))],
     ]
-    ids = jnp.stack([jnp.where(core == 0, a, b) for group in groups for _, a, b in group])
+    ids = jnp.stack([jnp.where(core == 0, a, b) for group in groups for a, b in group])
     cols = 2 * ids[:, None] + jnp.stack([core, 1 - core])[None, :]
     cols = jnp.where(ids[:, None] >= 0, cols, -1)
     hot = cols[:, None, :, None] == jnp.arange(64, dtype=jnp.int32)[None, None, None, :]
@@ -304,16 +321,23 @@
     table = table.astype(jnp.int32).reshape(ids.shape[0], 4)
 
     core1 = core.reshape(1)
-    state = None
-    at = 0
-    for n, group in enumerate(groups):
-        flags = table[at : at + len(group)]
-        at += len(group)
-        state = attend_call(
-            core1, flags, queries, qdocs, [g[0] for g in group], state, n == len(groups) - 1
-        )
-    acc, stats, share, share_stats = state
-    return combine_call(acc, stats, send(share, SWAP), send(share_stats, SWAP), gate_rows)
+
+    def step(state, first, units, last=False):
+        flags = table[first : first + len(units)]
+        return attend_call(core1, flags, queries, qdocs, units, state, last)
+
+    state = step(None, 0, [(unit,), (up[0],)])
+    seed, sigmoid, state = lax.optimization_barrier((seed, sigmoid, state))
+    down = [send(jnp.where(core == 0, seed, lead), DOWN[0])]
+    up.append(send(up[1], UP[2]))
+    state = step(state, 2, [(seed, lead), (up[1],)])
+    for s in range(2):
+        down.append(send(down[s], DOWN[s + 1]))
+        if s == 0:
+            up.append(send(up[2], UP[3]))
+        state = step(state, 4 + 2 * s, [(down[s],), (up[s + 2],)])
+    acc, stats, share, share_stats = step(state, 8, [(down[2],)], last=True)
+    return combine_call(acc, stats, send(share, SWAP), send(share_stats, SWAP), sigmoid)
 
 
 def solution(mesh):

time: 97.9 us -> 92.6 us (0.946)
  waiting for transfers between devices: 23.3 us -> 14.6 us
  starting transfers between devices: 36 us -> 44.3 us
  Pallas kernels: 32.4 us -> 29.5 us
  local copies, waits for them, and re-layouts: 2.47 us -> 0.67 us
    ppermute x13, waiting for transfers between devices: 23.3 us -> 14.6 us  [send(): return lax.ppermute(value, 'cp', pairs)]
    ppermute x13, starting transfers between devices: 36 us -> 44.3 us  [send(): return lax.ppermute(value, 'cp', pairs)]
    pallas_call x1, Pallas kernels: 4.91 us -> 1.74 us  [combine_call(): pl.pallas_call(combine, out_shape=jax.ShapeDtypeStruct((BLK, H * HD), jnp...]
    pallas_call x0 -> x1, Pallas kernels: none -> 2.94 us  [sigmoid_call(): pl.pallas_call(gate_sigmoid, out_shape=jax.ShapeDtypeStruct(gate_rows.sha...]
    pallas_call x5, Pallas kernels: 27.5 us -> 24.8 us  [attend_call(): pl.pallas_call(functools.partial(attend, state is None, last, paired), ou...]
    unnamed x7 -> x11, local copies, waits for them, and re-layouts: 1.85 us -> 0.05 us
  transfers between devices with their start and end apart: 13 -> 13, of which waited for: 5 -> 5; matrix products, arithmetic and copies ran while one was open for 3% -> 1% of each run, Pallas kernels for 23% -> 26%
where the time goes in v6:
time: 92.6 us; the launch traced here: 92.2 us
  starting transfers between devices  44.3 us (48%)
  Pallas kernels  29.5 us (32%)
  waiting for transfers between devices  14.6 us (16%)
  other arithmetic  2.78 us (3%)
    ppermute x13, starting transfers between devices, send(): return lax.ppermute(value, 'cp', pairs)  44.3 us
    pallas_call x5, Pallas kernels, attend_call(): pl.pallas_call(functools.partial(attend, state is None, last, paired), ou...  24.8 us
    ppermute x13, waiting for transfers between devices, send(): return lax.ppermute(value, 'cp', pairs)  14.6 us
    pallas_call x1, Pallas kernels, sigmoid_call(): pl.pallas_call(gate_sigmoid, out_shape=jax.ShapeDtypeStruct(gate_rows.sha...  2.94 us
  transfers between devices with their start and end apart: 13, of which 5 were waited for; matrix products, arithmetic and copies ran while one was open for 1% of the time, Pallas kernels for 26%

profile of v6, /device:TPU:15, one launch (start us, length us, event | category | flops | bytes accessed | tf_op | source)
XLA Modules:
  0.0 92.2 jit_solution(8840468194014607775)
XLA Ops:
  0.0 0.7 convert_element_type.17
  0.7 0.7 convert_bitcast_fusion
  1.3 1.0 %pad_maximum_fusion = bf16[272,512]{1,0:T(8,128)(2,1)S(1)} fusion(bf16[16,512]{1,0:T(8,128)(2,1)S(1)} %fusion.7, bf16[128,512]{1,0:T(8,128)(2,1)} %param.8, bf16[128,512]{1,0:T(8,128)(2,1)} %param.7), kind=kLoop, calls=%fused_computation.1 | loop fusion | flops 835584 | bytes 557056 | tf_op jit(solution)/shard_map/concatenate | solution.py:270
  2.3 0.8 collective-permute-start
  3.1 0.1 collective-permute-start.1
  3.2 0.1 stack.51
  3.3 0.0 copy-start.2
  3.3 0.0 copy-start.3
  3.3 0.0 copy-start.1
  3.3 2.9 %shard_map.64.sigmoid = f32[128,4096]{1,0:T(8,128)} custom-call(bf16[128,4096]{1,0:T(8,128)(2,1)} %gate.1), custom_call_target="tpu_custom_call" | custom-call | flops 2000000000 | bytes 3000000 | tf_op jit(solution)/shard_map/pallas_call | solution.py:217
  6.3 0.1 pad_add_fusion
  6.4 0.1 add_select_fusion
  6.5 0.1 iota_compare_fusion.1
  6.6 0.0 collective-permute-done
  6.7 1.3 %collective-permute-start.3 = (bf16[528,512]{1,0:T(8,128)(2,1)S(1)}, bf16[528,512]{1,0:T(8,128)(2,1)}, u32[]{:S(2)}, u32[]{:S(2)}) collective-permute-start(bf16[528,512]{1,0:T(8,128)(2,1)S(1)} %slice_dynamic-update-slice_fusion.refs_5_), channel_id=1, source_target_pairs={{0,2},{2,4},{4,6},{6,8},{8,10},{10,12},{12,14},{14,32},{16,18},{18... | collective-permute-start | bytes 1622024 | tf_op jit(solution)/shard_map/ppermute | solution.py:260
  8.0 0.7 collective-permute-start.2
  8.7 0.1 select_reduce_fusion
  8.8 0.1 slice.62.refs_0_
  8.9 0.1 slice.68.refs_0_
  9.0 0.1 slice.66.refs_0_
  9.1 0.1 slice.64.refs_0_
  9.2 0.1 slice.57.refs_0_
  9.3 8.8 %collective-permute-done.3.refs_6_ = bf16[528,512]{1,0:T(8,128)(2,1)} collective-permute-done((bf16[528,512]{1,0:T(8,128)(2,1)S(1)}, bf16[528,512]{1,0:T(8,128)(2,1)}, u32[]{:S(2)}, u32[]{:S(2)}) %collective-permute-start.3) | collective-permute-done | bytes 540704 | tf_op jit(solution)/shard_map/ppermute | solution.py:260
  18.1 6.5 %collective-permute-start.4 = (bf16[528,512]{1,0:T(8,128)(2,1)}, bf16[528,512]{1,0:T(8,128)(2,1)S(1)}, u32[]{:S(2)}, u32[]{:S(2)}) collective-permute-start(bf16[528,512]{1,0:T(8,128)(2,1)} %collective-permute-done.3.refs_6_), channel_id=1, source_target_pairs={{17,31},{19,17},{21,19},{23,21},{25,23},{27,25},{29,27},{31,29},{3... | collective-permute-start | bytes 1622024 | tf_op jit(solution)/shard_map/ppermute | solution.py:260
  24.6 1.9 %collective-permute-start.8 = (bf16[528,512]{1,0:T(8,128)(2,1)}, bf16[528,512]{1,0:T(8,128)(2,1)S(1)}, u32[]{:S(2)}, u32[]{:S(2)}) collective-permute-start(bf16[528,512]{1,0:T(8,128)(2,1)} %collective-permute-done.3.refs_6_), channel_id=1, source_target_pairs={{2,4},{4,6},{6,8},{8,10},{10,12},{12,14},{14,32},{18,20},{20,22},{... | collective-permute-start | bytes 1622024 | tf_op jit(solution)/shard_map/ppermute | solution.py:260
  26.6 0.0 collective-permute-done.1.refs_4_
  26.6 0.1 broadcast_in_dim.58.refs_2_
  26.7 4.1 %shard_map.65 = (f32[16,256,128]{2,1,0:T(8,128)S(1)}, f32[16,256,128]{2,1,0:T(8,128)S(1)}, f32[16,256,256]{2,1,0:T(8,128)S(1)}) custom-call(s32[2,4]{1,0:T(2,128)S(1)} %slice.62.refs_0_, s32[1]{0:T(128)} %bitcast.9.refs_1_, f32[256,128]{1,0:T(8,128)S(1)} %broadcast_in_dim.58.refs_2_, bf16[128,4096]{1,0:T(8,128)(2,1)S(1)} %copy-done.1, ...), custom_call_target="tpu_custom_call" | custom-call | flops 6442450944 | bytes 10080000 | tf_op jit(solution)/shard_map/pallas_call | solution.py:194
  30.8 0.0 collective-permute-done.2.refs_5_
  30.8 0.5 collective-permute-done.4.refs_6_
  31.2 0.1 broadcast_select_fusion
  31.3 4.9 %collective-permute-start.5 = (bf16[528,512]{1,0:T(8,128)(2,1)S(1)}, bf16[528,512]{1,0:T(8,128)(2,1)S(1)}, u32[]{:S(2)}, u32[]{:S(2)}) collective-permute-start(bf16[528,512]{1,0:T(8,128)(2,1)S(1)} %broadcast_select_fusion), channel_id=1, source_target_pairs={{0,46},{2,0},{4,2},{16,62},{18,16},{20,18},{32,14},{34,32},{36,34}... | collective-permute-start | bytes 1622024 | tf_op jit(solution)/shard_map/ppermute | solution.py:260
  36.2 2.2 %collective-permute-done.8.refs_7_ = bf16[528,512]{1,0:T(8,128)(2,1)S(1)} collective-permute-done((bf16[528,512]{1,0:T(8,128)(2,1)}, bf16[528,512]{1,0:T(8,128)(2,1)S(1)}, u32[]{:S(2)}, u32[]{:S(2)}) %collective-permute-start.8) | collective-permute-done | bytes 540704 | tf_op jit(solution)/shard_map/ppermute | solution.py:260
  38.4 4.0 %collective-permute-start.9 = (bf16[528,512]{1,0:T(8,128)(2,1)S(1)}, bf16[528,512]{1,0:T(8,128)(2,1)S(1)}, u32[]{:S(2)}, u32[]{:S(2)}) collective-permute-start(bf16[528,512]{1,0:T(8,128)(2,1)S(1)} %collective-permute-done.8.refs_7_), channel_id=1, source_target_pairs={{4,6},{6,8},{8,10},{10,12},{12,14},{14,32},{20,22},{22,24},{24,26}... | collective-permute-start | bytes 1622024 | tf_op jit(solution)/shard_map/ppermute | solution.py:260
  42.4 5.5 %shard_map.66 = (f32[16,256,128]{2,1,0:T(8,128)S(1)}, f32[16,256,128]{2,1,0:T(8,128)S(1)}, f32[16,256,256]{2,1,0:T(8,128)S(1)}) custom-call(s32[2,4]{1,0:T(2,128)S(1)} %slice.68.refs_0_, s32[1]{0:T(128)} %bitcast.9.refs_1_, f32[256,128]{1,0:T(8,128)S(1)} %broadcast_in_dim.58.refs_2_, ...), custom_call_target="tpu_custom_call", output_to_operand_aliasing={{0}: (8, {}), {1}: (9, {}), {2}: (10, {})} | custom-call | flops 6442450944 | bytes 10080000 | tf_op jit(solution)/shard_map/pallas_call | solution.py:194
  47.9 0.0 collective-permute-done.5.refs_5_
  47.9 3.7 %collective-permute-start.6 = (bf16[528,512]{1,0:T(8,128)(2,1)S(1)}, bf16[528,512]{1,0:T(8,128)(2,1)S(1)}, u32[]{:S(2)}, u32[]{:S(2)}) collective-permute-start(bf16[528,512]{1,0:T(8,128)(2,1)S(1)} %collective-permute-done.5.refs_5_), channel_id=1, source_target_pairs={{0,46},{2,0},{14,12},{16,62},{18,16},{30,28},{32,14},{34,32},{36,3... | collective-permute-start | bytes 1622024 | tf_op jit(solution)/shard_map/ppermute | solution.py:260
  51.7 4.8 %collective-permute-start.10 = (bf16[528,512]{1,0:T(8,128)(2,1)S(1)}, bf16[528,512]{1,0:T(8,128)(2,1)S(1)}, u32[]{:S(2)}, u32[]{:S(2)}) collective-permute-start(bf16[528,512]{1,0:T(8,128)(2,1)S(1)} %collective-permute-done.9.refs_6_), channel_id=1, source_target_pairs={{6,8},{8,10},{10,12},{12,14},{14,32},{22,24},{24,26},{26,28},{28,3... | collective-permute-start | bytes 1622024 | tf_op jit(solution)/shard_map/ppermute | solution.py:260
  56.5 5.4 %shard_map.67 = (f32[16,256,128]{2,1,0:T(8,128)S(1)}, f32[16,256,128]{2,1,0:T(8,128)S(1)}, f32[16,256,256]{2,1,0:T(8,128)S(1)}) custom-call(s32[2,4]{1,0:T(2,128)S(1)} %slice.66.refs_0_, s32[1]{0:T(128)} %bitcast.9.refs_1_, f32[256,128]{1,0:T(8,128)S(1)} %broadcast_in_dim.58.refs_2_, ...), custom_call_target="tpu_custom_call", output_to_operand_aliasing={{0}: (7, {}), {1}: (8, {}), {2}: (9, {})} | custom-call | flops 6442450944 | bytes 10080000 | tf_op jit(solution)/shard_map/pallas_call | solution.py:194
  61.9 4.7 %collective-permute-start.7 = (bf16[528,512]{1,0:T(8,128)(2,1)S(1)}, bf16[528,512]{1,0:T(8,128)(2,1)S(1)}, u32[]{:S(2)}, u32[]{:S(2)}) collective-permute-start(bf16[528,512]{1,0:T(8,128)(2,1)S(1)} %collective-permute-done.6.refs_5_), channel_id=1, source_target_pairs={{0,46},{12,10},{14,12},{16,62},{28,26},{30,28},{32,14},{34,32},{36... | collective-permute-start | bytes 1622024 | tf_op jit(solution)/shard_map/ppermute | solution.py:260
  66.6 5.6 %shard_map.68 = (f32[16,256,128]{2,1,0:T(8,128)S(1)}, f32[16,256,128]{2,1,0:T(8,128)S(1)}, f32[16,256,256]{2,1,0:T(8,128)S(1)}) custom-call(s32[2,4]{1,0:T(2,128)S(1)} %slice.64.refs_0_, s32[1]{0:T(128)} %bitcast.9.refs_1_, f32[256,128]{1,0:T(8,128)S(1)} %broadcast_in_dim.58.refs_2_, ...), custom_call_target="tpu_custom_call", output_to_operand_aliasing={{0}: (7, {}), {1}: (8, {}), {2}: (9, {})} | custom-call | flops 6442450944 | bytes 10080000 | tf_op jit(solution)/shard_map/pallas_call | solution.py:194
  72.3 0.8 collective-permute-done.7.refs_5_
  73.1 4.2 %shard_map.69 = (f32[16,128,256]{2,1,0:T(8,128)S(1)}, f32[128,128]{1,0:T(8,128)S(1)}, bf16[16,128,256]{2,1,0:T(8,128)(2,1)S(1)}, f32[128,128]{1,0:T(8,128)S(1)}) custom-call(s32[1,4]{1,0:T(1,128)S(1)} %slice.57.refs_0_, s32[1]{0:T(128)} %bitcast.9.refs_1_, f32[256,128]{1,0:T(8,128)S(1)} %broadcast_in_dim.58.refs_2_, bf16[128,4096]{1,0:T(8,128)(2,1)S(1)} %copy-done.1, ...), custom_call_target="tpu_custom_call" | custom-call | flops 3221225472 | bytes 9540000 | tf_op jit(solution)/shard_map/pallas_call | solution.py:194
  77.3 10.8 %collective-permute-start.11 = (bf16[16,128,256]{2,1,0:T(8,128)(2,1)S(1)}, bf16[16,128,256]{2,1,0:T(8,128)(2,1)S(1)}, u32[]{:S(2)}, u32[]{:S(2)}) collective-permute-start(bf16[16,128,256]{2,1,0:T(8,128)(2,1)S(1)} %get-tuple-element.46), channel_id=1, source_target_pairs={{0,1},{1,0},{2,3},{3,2},{4,5},{5,4},{6,7},{7,6},{8,9},{9,8},{10,11... | collective-permute-start | bytes 3145736 | tf_op jit(solution)/shard_map/ppermute | solution.py:260
  88.1 0.1 collective-permute-start.12
  88.2 2.3 %collective-permute-done.12.share_stats = f32[128,128]{1,0:T(8,128)S(1)} collective-permute-done((f32[128,128]{1,0:T(8,128)S(1)}, f32[128,128]{1,0:T(8,128)S(1)}, u32[]{:S(2)}, u32[]{:S(2)}) %collective-permute-start.12) | collective-permute-done | bytes 65568 | tf_op jit(solution)/shard_map/ppermute | solution.py:260
  90.5 0.0 collective-permute-done.11.share
  90.5 1.7 %shard_map.70 = bf16[128,4096]{1,0:T(8,128)(2,1)} custom-call(f32[16,128,256]{2,1,0:T(8,128)S(1)} %get-tuple-element.44.acc, f32[128,128]{1,0:T(8,128)S(1)} %get-tuple-element.45.stats, bf16[16,128,256]{2,1,0:T(8,128)(2,1)S(1)} %collective-permute-done.11.share, f32[128,128]{1,0:T(8,128)S(1)} %collective-permute-done.12.share_stats, f32[128,4096]{1,0:T(8,128)S(1)} %copy-done), custom_call_target="tpu_custom_call" | custom-call | tf_op jit(solution)/shard_map/pallas_call | solution.py:244
  (27 shorter events, 0.2 us)
Async XLA Ops:
  2.3 4.2 %collective-permute-start = (bf16[272,512]{1,0:T(8,128)(2,1)S(1)}, bf16[272,512]{1,0:T(8,128)(2,1)S(1)}, u32[]{:S(2)}, u32[]{:S(2)}) collective-permute-start(bf16[272,512]{1,0:T(8,128)(2,1)S(1)} %pad_maximum_fusion), channel_id=1, source_target_pairs={{0,1},{1,0},{2,3},{3,2},{4,5},{5,4},{6,7},{7,6},{8,9},{9,8},{10,11... | collective-permute-start | bytes 835592 | tf_op jit(solution)/shard_map/ppermute | solution.py:260
  3.1 23.5 %collective-permute-start.1 = (bf16[128,4096]{1,0:T(8,128)(2,1)}, bf16[128,4096]{1,0:T(8,128)(2,1)S(1)}, u32[]{:S(2)}, u32[]{:S(2)}) collective-permute-start(bf16[128,4096]{1,0:T(8,128)(2,1)} %refs_3_.4), channel_id=1, source_target_pairs={{0,1},{1,0},{2,3},{3,2},{4,5},{5,4},{6,7},{7,6},{8,9},{9,8},{10,11... | collective-permute-start | bytes 3145736 | tf_op jit(solution)/shard_map/ppermute | solution.py:260
  3.3 3.1 %copy-start.2 = (bf16[128,512]{1,0:T(8,128)(2,1)S(1)}, bf16[128,512]{1,0:T(8,128)(2,1)}, u32[]{:S(2)}) copy-start(bf16[128,512]{1,0:T(8,128)(2,1)} %param.7) | copy-start | bytes 393220
  3.3 3.3 %copy-start.3 = (bf16[128,512]{1,0:T(8,128)(2,1)S(1)}, bf16[128,512]{1,0:T(8,128)(2,1)}, u32[]{:S(2)}) copy-start(bf16[128,512]{1,0:T(8,128)(2,1)} %param.8) | copy-start | bytes 393220
  3.3 23.4 %copy-start.1 = (bf16[128,4096]{1,0:T(8,128)(2,1)S(1)}, bf16[128,4096]{1,0:T(8,128)(2,1)}, u32[]{:S(2)}) copy-start(bf16[128,4096]{1,0:T(8,128)(2,1)} %refs_3_.4) | copy-start | bytes 3145732
  6.7 11.4 %collective-permute-start.3 = (bf16[528,512]{1,0:T(8,128)(2,1)S(1)}, bf16[528,512]{1,0:T(8,128)(2,1)}, u32[]{:S(2)}, u32[]{:S(2)}) collective-permute-start(bf16[528,512]{1,0:T(8,128)(2,1)S(1)} %slice_dynamic-update-slice_fusion.refs_5_), channel_id=1, source_target_pairs={{0,2},{2,4},{4,6},{6,8},{8,10},{10,12},{12,14},{14,32},{16,18},{18... | collective-permute-start | bytes 1622024 | tf_op jit(solution)/shard_map/ppermute | solution.py:260
  8.0 22.8 %collective-permute-start.2 = (bf16[528,512]{1,0:T(8,128)(2,1)S(1)}, bf16[528,512]{1,0:T(8,128)(2,1)S(1)}, u32[]{:S(2)}, u32[]{:S(2)}) collective-permute-start(bf16[528,512]{1,0:T(8,128)(2,1)S(1)} %slice_dynamic-update-slice_fusion.refs_5_), channel_id=1, source_target_pairs={{0,32},{2,34},{4,36},{6,38},{8,40},{10,42},{12,44},{14,46},{16,48}... | collective-permute-start | bytes 1622024 | tf_op jit(solution)/shard_map/ppermute | solution.py:260
  18.1 13.1 %collective-permute-start.4 = (bf16[528,512]{1,0:T(8,128)(2,1)}, bf16[528,512]{1,0:T(8,128)(2,1)S(1)}, u32[]{:S(2)}, u32[]{:S(2)}) collective-permute-start(bf16[528,512]{1,0:T(8,128)(2,1)} %collective-permute-done.3.refs_6_), channel_id=1, source_target_pairs={{17,31},{19,17},{21,19},{23,21},{25,23},{27,25},{29,27},{31,29},{3... | collective-permute-start | bytes 1622024 | tf_op jit(solution)/shard_map/ppermute | solution.py:260
  24.6 13.8 %collective-permute-start.8 = (bf16[528,512]{1,0:T(8,128)(2,1)}, bf16[528,512]{1,0:T(8,128)(2,1)S(1)}, u32[]{:S(2)}, u32[]{:S(2)}) collective-permute-start(bf16[528,512]{1,0:T(8,128)(2,1)} %collective-permute-done.3.refs_6_), channel_id=1, source_target_pairs={{2,4},{4,6},{6,8},{8,10},{10,12},{12,14},{14,32},{18,20},{20,22},{... | collective-permute-start | bytes 1622024 | tf_op jit(solution)/shard_map/ppermute | solution.py:260
  31.3 16.6 %collective-permute-start.5 = (bf16[528,512]{1,0:T(8,128)(2,1)S(1)}, bf16[528,512]{1,0:T(8,128)(2,1)S(1)}, u32[]{:S(2)}, u32[]{:S(2)}) collective-permute-start(bf16[528,512]{1,0:T(8,128)(2,1)S(1)} %broadcast_select_fusion), channel_id=1, source_target_pairs={{0,46},{2,0},{4,2},{16,62},{18,16},{20,18},{32,14},{34,32},{36,34}... | collective-permute-start | bytes 1622024 | tf_op jit(solution)/shard_map/ppermute | solution.py:260
  38.4 13.3 %collective-permute-start.9 = (bf16[528,512]{1,0:T(8,128)(2,1)S(1)}, bf16[528,512]{1,0:T(8,128)(2,1)S(1)}, u32[]{:S(2)}, u32[]{:S(2)}) collective-permute-start(bf16[528,512]{1,0:T(8,128)(2,1)S(1)} %collective-permute-done.8.refs_7_), channel_id=1, source_target_pairs={{4,6},{6,8},{8,10},{10,12},{12,14},{14,32},{20,22},{22,24},{24,26}... | collective-permute-start | bytes 1622024 | tf_op jit(solution)/shard_map/ppermute | solution.py:260
  47.9 14.0 %collective-permute-start.6 = (bf16[528,512]{1,0:T(8,128)(2,1)S(1)}, bf16[528,512]{1,0:T(8,128)(2,1)S(1)}, u32[]{:S(2)}, u32[]{:S(2)}) collective-permute-start(bf16[528,512]{1,0:T(8,128)(2,1)S(1)} %collective-permute-done.5.refs_5_), channel_id=1, source_target_pairs={{0,46},{2,0},{14,12},{16,62},{18,16},{30,28},{32,14},{34,32},{36,3... | collective-permute-start | bytes 1622024 | tf_op jit(solution)/shard_map/ppermute | solution.py:260
  51.7 14.9 %collective-permute-start.10 = (bf16[528,512]{1,0:T(8,128)(2,1)S(1)}, bf16[528,512]{1,0:T(8,128)(2,1)S(1)}, u32[]{:S(2)}, u32[]{:S(2)}) collective-permute-start(bf16[528,512]{1,0:T(8,128)(2,1)S(1)} %collective-permute-done.9.refs_6_), channel_id=1, source_target_pairs={{6,8},{8,10},{10,12},{12,14},{14,32},{22,24},{24,26},{26,28},{28,3... | collective-permute-start | bytes 1622024 | tf_op jit(solution)/shard_map/ppermute | solution.py:260
  61.9 11.1 %collective-permute-start.7 = (bf16[528,512]{1,0:T(8,128)(2,1)S(1)}, bf16[528,512]{1,0:T(8,128)(2,1)S(1)}, u32[]{:S(2)}, u32[]{:S(2)}) collective-permute-start(bf16[528,512]{1,0:T(8,128)(2,1)S(1)} %collective-permute-done.6.refs_5_), channel_id=1, source_target_pairs={{0,46},{12,10},{14,12},{16,62},{28,26},{30,28},{32,14},{34,32},{36... | collective-permute-start | bytes 1622024 | tf_op jit(solution)/shard_map/ppermute | solution.py:260
  73.1 17.4 %copy-start = (f32[128,4096]{1,0:T(8,128)S(1)}, f32[128,4096]{1,0:T(8,128)}, u32[]{:S(2)}) copy-start(f32[128,4096]{1,0:T(8,128)} %shard_map.64.sigmoid) | copy-start | bytes 6291460
  77.3 13.2 %collective-permute-start.11 = (bf16[16,128,256]{2,1,0:T(8,128)(2,1)S(1)}, bf16[16,128,256]{2,1,0:T(8,128)(2,1)S(1)}, u32[]{:S(2)}, u32[]{:S(2)}) collective-permute-start(bf16[16,128,256]{2,1,0:T(8,128)(2,1)S(1)} %get-tuple-element.46), channel_id=1, source_target_pairs={{0,1},{1,0},{2,3},{3,2},{4,5},{5,4},{6,7},{7,6},{8,9},{9,8},{10,11... | collective-permute-start | bytes 3145736 | tf_op jit(solution)/shard_map/ppermute | solution.py:260
  88.1 2.4 %collective-permute-start.12 = (f32[128,128]{1,0:T(8,128)S(1)}, f32[128,128]{1,0:T(8,128)S(1)}, u32[]{:S(2)}, u32[]{:S(2)}) collective-permute-start(f32[128,128]{1,0:T(8,128)S(1)} %get-tuple-element.47), channel_id=1, source_target_pairs={{0,1},{1,0},{2,3},{3,2},{4,5},{5,4},{6,7},{7,6},{8,9},{9,8},{10,11... | collective-permute-start | bytes 196616 | tf_op jit(solution)/shard_map/ppermute | solution.py:260

commit v7 on v6

--- a/solution.py
+++ b/solution.py
@@ -63,8 +63,11 @@
     None, lambda x, z: (x, (z + 1) % NZ), lambda x, z, s: x >= 1, 4
 )
 SWAP = [(i, i ^ 1) for i in range(2 * NX * NZ)]
+MID_UP[0] |= {(((x - 2) % NX, z), ((x - 1) % NX, z)) for _, (x, z) in FAR[0]}
 UP = [pairs_of(0, NEAR[s]) + pairs_of(1, MID_UP[s - 1]) for s in range(1, 5)]
-SEED = pairs_of(0, FAR[0])
+SEED = [
+    ((((x - 1) % NX) * NZ + z) * 2 + 1, (x * NZ + z) * 2) for _, (x, z) in sorted(FAR[0])
+]
 LEAD = pairs_of(1, MID_DOWN[1])
 DOWN = [pairs_of(0, FAR[s]) + pairs_of(1, MID_DOWN[s + 1]) for s in range(1, 4)]
 
@@ -286,9 +289,10 @@
     queries = (query_rows, send(query_rows, SWAP))
 
     up = [send(unit, UP[0])]
-    seed = send(unit, SEED)
+    seed = send(up[0], SEED)
     up.append(send(up[0], UP[1]))
     lead = send(up[0], LEAD)
+    gate_rows, _ = lax.optimization_barrier((gate_rows, unit))
     sigmoid = sigmoid_call(gate_rows)
 
     meta = unit[UNIT : UNIT + 2, :UNIT].astype(jnp.float32)
@@ -307,14 +311,16 @@
         return jnp.where(x >= 1, (x - 1) * NZ + lax.rem(z + s + NZ, NZ), -1)
 
     groups = [
-        [(chip, -1), (near_id(1), mid_id(0))],
-        [(far_id(0), mid_id(1)), (near_id(2), mid_id(-1))],
-        [(far_id(1), mid_id(2)), (near_id(3), mid_id(-2))],
-        [(far_id(2), mid_id(3)), (near_id(4), mid_id(-3))],
-        [(far_id(3), mid_id(4))],
+        [(chip, -1, 0), (near_id(1), mid_id(0), 0)],
+        [(far_id(0), mid_id(1), 1), (near_id(2), mid_id(-1), 0)],
+        [(far_id(1), mid_id(2), 1), (near_id(3), mid_id(-2), 0)],
+        [(far_id(2), mid_id(3), 1), (near_id(4), mid_id(-3), 0)],
+        [(far_id(3), mid_id(4), 1)],
     ]
-    ids = jnp.stack([jnp.where(core == 0, a, b) for group in groups for a, b in group])
-    cols = 2 * ids[:, None] + jnp.stack([core, 1 - core])[None, :]
+    ids = jnp.stack([jnp.where(core == 0, a, b) for group in groups for a, b, _ in group])
+    turned = jnp.array([t for group in groups for _, _, t in group], jnp.int32)
+    front = jnp.where(core == 0, turned, 1)
+    cols = 2 * ids[:, None] + jnp.stack([front, 1 - front], axis=1)
     cols = jnp.where(ids[:, None] >= 0, cols, -1)
     hot = cols[:, None, :, None] == jnp.arange(64, dtype=jnp.int32)[None, None, None, :]
     table = jnp.sum(jnp.where(hot, lists[None, :, None, :], 0.0), axis=-1)

time: 92.6 us -> 93.2 us (level)
  local copies, waits for them, and re-layouts: 0.67 us -> 2.57 us
  waiting for transfers between devices: 14.6 us -> 12.9 us
    unnamed x11 -> x7, local copies, waits for them, and re-layouts: 0.05 us -> 1.85 us
    ppermute x13, waiting for transfers between devices: 14.6 us -> 12.9 us  [send(): return lax.ppermute(value, 'cp', pairs)]
  transfers between devices with their start and end apart: 13 -> 13, of which waited for: 5 -> 5; matrix products, arithmetic and copies ran while one was open for 1% -> 3% of each run, Pallas kernels for 26% -> 25%
where the time goes in v7:
time: 93.2 us; the launch traced here: 92.8 us
  starting transfers between devices  45.1 us (48%)
  Pallas kernels  29.3 us (31%)
  waiting for transfers between devices  12.9 us (14%)
  other arithmetic  2.64 us (3%)
  local copies, waits for them, and re-layouts  2.57 us (3%)
    ppermute x13, starting transfers between devices, send(): return lax.ppermute(value, 'cp', pairs)  45.1 us
    pallas_call x5, Pallas kernels, attend_call(): pl.pallas_call(functools.partial(attend, state is None, last, paired), ou...  24.6 us
    ppermute x13, waiting for transfers between devices, send(): return lax.ppermute(value, 'cp', pairs)  12.9 us
    pallas_call x1, Pallas kernels, sigmoid_call(): pl.pallas_call(gate_sigmoid, out_shape=jax.ShapeDtypeStruct(gate_rows.sha...  2.93 us
  transfers between devices with their start and end apart: 13, of which 5 were waited for; matrix products, arithmetic and copies ran while one was open for 3% of the time, Pallas kernels for 25%

profile of v7, /device:TPU:15, one launch (start us, length us, event | category | flops | bytes accessed | tf_op | source)
XLA Modules:
  0.0 92.8 jit_solution(2860767497667611887)
XLA Ops:
  0.0 0.7 convert_element_type.17
  0.7 0.7 convert_bitcast_fusion
  1.3 1.0 %pad_maximum_fusion = bf16[272,512]{1,0:T(8,128)(2,1)S(1)} fusion(bf16[16,512]{1,0:T(8,128)(2,1)S(1)} %fusion.7, bf16[128,512]{1,0:T(8,128)(2,1)} %param.9, bf16[128,512]{1,0:T(8,128)(2,1)} %param.8), kind=kLoop, calls=%fused_computation.1 | loop fusion | flops 835584 | bytes 557056 | tf_op jit(solution)/shard_map/concatenate | solution.py:273
  2.3 0.8 collective-permute-start
  3.1 0.1 collective-permute-start.1
  3.2 0.1 stack.51
  3.3 0.9 constant_dynamic-update-slice_fusion.1
  4.3 0.1 copy.18
  4.4 0.1 iota_compare_fusion.1
  4.5 0.0 collective-permute-done
  4.5 0.9 constant_dynamic-update-slice_fusion
  5.5 2.1 %collective-permute-start.2 = (bf16[528,512]{1,0:T(8,128)(2,1)S(1)}, bf16[528,512]{1,0:T(8,128)(2,1)S(1)}, u32[]{:S(2)}, u32[]{:S(2)}) collective-permute-start(bf16[528,512]{1,0:T(8,128)(2,1)S(1)} %slice_dynamic-update-slice_fusion.refs_5_), channel_id=1, source_target_pairs={{0,2},{2,4},{4,6},{6,8},{8,10},{10,12},{12,14},{14,32},{16,18},{18... | collective-permute-start | bytes 1622024 | tf_op jit(solution)/shard_map/ppermute | solution.py:263
  7.6 0.1 select_reduce_fusion
  7.7 0.1 slice.62.refs_0_
  7.8 0.1 slice.68.refs_0_
  7.9 0.1 slice.66.refs_0_
  8.0 0.1 slice.64.refs_0_
  8.1 0.1 slice.57.refs_0_
  8.2 2.9 %shard_map.73.sigmoid = f32[128,4096]{1,0:T(8,128)} custom-call(bf16[128,4096]{1,0:T(8,128)(2,1)} %gate), custom_call_target="tpu_custom_call" | custom-call | flops 2000000000 | bytes 3000000 | tf_op jit(solution)/shard_map/pallas_call | solution.py:220
  11.1 4.5 %collective-permute-done.2.refs_6_ = bf16[528,512]{1,0:T(8,128)(2,1)S(1)} collective-permute-done((bf16[528,512]{1,0:T(8,128)(2,1)S(1)}, bf16[528,512]{1,0:T(8,128)(2,1)S(1)}, u32[]{:S(2)}, u32[]{:S(2)}) %collective-permute-start.2) | collective-permute-done | bytes 540704 | tf_op jit(solution)/shard_map/ppermute | solution.py:263
  15.6 3.6 %collective-permute-start.3 = (bf16[528,512]{1,0:T(8,128)(2,1)S(1)}, bf16[528,512]{1,0:T(8,128)(2,1)S(1)}, u32[]{:S(2)}, u32[]{:S(2)}) collective-permute-start(bf16[528,512]{1,0:T(8,128)(2,1)S(1)} %collective-permute-done.2.refs_6_), channel_id=1, source_target_pairs={{17,32},{19,34},{21,36},{23,38},{25,40},{27,42},{29,44},{31,46},{3... | collective-permute-start | bytes 1622024 | tf_op jit(solution)/shard_map/ppermute | solution.py:263
  19.2 4.8 %collective-permute-start.4 = (bf16[528,512]{1,0:T(8,128)(2,1)S(1)}, bf16[528,512]{1,0:T(8,128)(2,1)S(1)}, u32[]{:S(2)}, u32[]{:S(2)}) collective-permute-start(bf16[528,512]{1,0:T(8,128)(2,1)S(1)} %collective-permute-done.2.refs_6_), channel_id=1, source_target_pairs={{17,31},{19,17},{21,19},{23,21},{25,23},{27,25},{29,27},{31,29},{3... | collective-permute-start | bytes 1622024 | tf_op jit(solution)/shard_map/ppermute | solution.py:263
  24.0 1.9 %collective-permute-start.8 = (bf16[528,512]{1,0:T(8,128)(2,1)S(1)}, bf16[528,512]{1,0:T(8,128)(2,1)S(1)}, u32[]{:S(2)}, u32[]{:S(2)}) collective-permute-start(bf16[528,512]{1,0:T(8,128)(2,1)S(1)} %collective-permute-done.2.refs_6_), channel_id=1, source_target_pairs={{2,4},{4,6},{6,8},{8,10},{10,12},{12,14},{14,32},{18,20},{20,22},{... | collective-permute-start | bytes 1622024 | tf_op jit(solution)/shard_map/ppermute | solution.py:263
  26.0 0.0 collective-permute-done.1.refs_4_
  26.0 0.1 broadcast_in_dim.62.refs_2_
  26.1 3.6 %shard_map.74 = (f32[16,256,128]{2,1,0:T(8,128)S(1)}, f32[16,256,128]{2,1,0:T(8,128)S(1)}, f32[16,256,256]{2,1,0:T(8,128)S(1)}) custom-call(s32[2,4]{1,0:T(2,128)S(1)} %slice.62.refs_0_, s32[1]{0:T(128)} %bitcast.12.refs_1_, f32[256,128]{1,0:T(8,128)S(1)} %broadcast_in_dim.62.refs_2_, bf16[128,4096]{1,0:T(8,128)(2,1)S(1)} %copy-done.1, ...), custom_call_target="tpu_custom_call" | custom-call | flops 6442450944 | bytes 10080000 | tf_op jit(solution)/shard_map/pallas_call | solution.py:197
  29.7 0.0 collective-permute-done.3.refs_5_
  29.7 0.7 collective-permute-done.4.refs_6_
  30.4 0.1 broadcast_select_fusion
  30.4 5.0 %collective-permute-start.5 = (bf16[528,512]{1,0:T(8,128)(2,1)S(1)}, bf16[528,512]{1,0:T(8,128)(2,1)S(1)}, u32[]{:S(2)}, u32[]{:S(2)}) collective-permute-start(bf16[528,512]{1,0:T(8,128)(2,1)S(1)} %broadcast_select_fusion), channel_id=1, source_target_pairs={{0,46},{2,0},{4,2},{16,62},{18,16},{20,18},{32,14},{34,32},{36,34}... | collective-permute-start | bytes 1622024 | tf_op jit(solution)/shard_map/ppermute | solution.py:263
  35.4 2.1 %collective-permute-done.8.refs_7_ = bf16[528,512]{1,0:T(8,128)(2,1)S(1)} collective-permute-done((bf16[528,512]{1,0:T(8,128)(2,1)S(1)}, bf16[528,512]{1,0:T(8,128)(2,1)S(1)}, u32[]{:S(2)}, u32[]{:S(2)}) %collective-permute-start.8) | collective-permute-done | bytes 540704 | tf_op jit(solution)/shard_map/ppermute | solution.py:263
  37.5 4.1 %collective-permute-start.9 = (bf16[528,512]{1,0:T(8,128)(2,1)S(1)}, bf16[528,512]{1,0:T(8,128)(2,1)S(1)}, u32[]{:S(2)}, u32[]{:S(2)}) collective-permute-start(bf16[528,512]{1,0:T(8,128)(2,1)S(1)} %collective-permute-done.8.refs_7_), channel_id=1, source_target_pairs={{4,6},{6,8},{8,10},{10,12},{12,14},{14,32},{20,22},{22,24},{24,26}... | collective-permute-start | bytes 1622024 | tf_op jit(solution)/shard_map/ppermute | solution.py:263
  41.6 5.5 %shard_map.75 = (f32[16,256,128]{2,1,0:T(8,128)S(1)}, f32[16,256,128]{2,1,0:T(8,128)S(1)}, f32[16,256,256]{2,1,0:T(8,128)S(1)}) custom-call(s32[2,4]{1,0:T(2,128)S(1)} %slice.68.refs_0_, s32[1]{0:T(128)} %bitcast.12.refs_1_, f32[256,128]{1,0:T(8,128)S(1)} %broadcast_in_dim.62.refs_2_, ...), custom_call_target="tpu_custom_call", output_to_operand_aliasing={{0}: (8, {}), {1}: (9, {}), {2}: (10, {})} | custom-call | flops 6442450944 | bytes 10080000 | tf_op jit(solution)/shard_map/pallas_call | solution.py:197
  47.2 0.0 collective-permute-done.5.refs_5_
  47.2 3.1 %collective-permute-start.6 = (bf16[528,512]{1,0:T(8,128)(2,1)S(1)}, bf16[528,512]{1,0:T(8,128)(2,1)S(1)}, u32[]{:S(2)}, u32[]{:S(2)}) collective-permute-start(bf16[528,512]{1,0:T(8,128)(2,1)S(1)} %collective-permute-done.5.refs_5_), channel_id=1, source_target_pairs={{0,46},{2,0},{14,12},{16,62},{18,16},{30,28},{32,14},{34,32},{36,3... | collective-permute-start | bytes 1622024 | tf_op jit(solution)/shard_map/ppermute | solution.py:263
  50.3 0.0 collective-permute-done.9.refs_6_
  50.3 4.5 %collective-permute-start.10 = (bf16[528,512]{1,0:T(8,128)(2,1)S(1)}, bf16[528,512]{1,0:T(8,128)(2,1)S(1)}, u32[]{:S(2)}, u32[]{:S(2)}) collective-permute-start(bf16[528,512]{1,0:T(8,128)(2,1)S(1)} %collective-permute-done.9.refs_6_), channel_id=1, source_target_pairs={{6,8},{8,10},{10,12},{12,14},{14,32},{22,24},{24,26},{26,28},{28,3... | collective-permute-start | bytes 1622024 | tf_op jit(solution)/shard_map/ppermute | solution.py:263
  54.7 5.7 %shard_map.76 = (f32[16,256,128]{2,1,0:T(8,128)S(1)}, f32[16,256,128]{2,1,0:T(8,128)S(1)}, f32[16,256,256]{2,1,0:T(8,128)S(1)}) custom-call(s32[2,4]{1,0:T(2,128)S(1)} %slice.66.refs_0_, s32[1]{0:T(128)} %bitcast.12.refs_1_, f32[256,128]{1,0:T(8,128)S(1)} %broadcast_in_dim.62.refs_2_, ...), custom_call_target="tpu_custom_call", output_to_operand_aliasing={{0}: (7, {}), {1}: (8, {}), {2}: (9, {})} | custom-call | flops 6442450944 | bytes 10080000 | tf_op jit(solution)/shard_map/pallas_call | solution.py:197
  60.4 0.0 collective-permute-done.6.refs_5_
  60.4 3.4 %collective-permute-start.7 = (bf16[528,512]{1,0:T(8,128)(2,1)S(1)}, bf16[528,512]{1,0:T(8,128)(2,1)S(1)}, u32[]{:S(2)}, u32[]{:S(2)}) collective-permute-start(bf16[528,512]{1,0:T(8,128)(2,1)S(1)} %collective-permute-done.6.refs_5_), channel_id=1, source_target_pairs={{0,46},{12,10},{14,12},{16,62},{28,26},{30,28},{32,14},{34,32},{36... | collective-permute-start | bytes 1622024 | tf_op jit(solution)/shard_map/ppermute | solution.py:263
  63.9 5.7 %shard_map.77 = (f32[16,256,128]{2,1,0:T(8,128)S(1)}, f32[16,256,128]{2,1,0:T(8,128)S(1)}, f32[16,256,256]{2,1,0:T(8,128)S(1)}) custom-call(s32[2,4]{1,0:T(2,128)S(1)} %slice.64.refs_0_, s32[1]{0:T(128)} %bitcast.12.refs_1_, f32[256,128]{1,0:T(8,128)S(1)} %broadcast_in_dim.62.refs_2_, ...), custom_call_target="tpu_custom_call", output_to_operand_aliasing={{0}: (7, {}), {1}: (8, {}), {2}: (9, {})} | custom-call | flops 6442450944 | bytes 10080000 | tf_op jit(solution)/shard_map/pallas_call | solution.py:197
  69.5 3.3 %collective-permute-done.7.refs_5_ = bf16[528,512]{1,0:T(8,128)(2,1)S(1)} collective-permute-done((bf16[528,512]{1,0:T(8,128)(2,1)S(1)}, bf16[528,512]{1,0:T(8,128)(2,1)S(1)}, u32[]{:S(2)}, u32[]{:S(2)}) %collective-permute-start.7) | collective-permute-done | bytes 540704 | tf_op jit(solution)/shard_map/ppermute | solution.py:263
  72.8 4.2 %shard_map.78 = (f32[16,128,256]{2,1,0:T(8,128)S(1)}, f32[128,128]{1,0:T(8,128)S(1)}, bf16[16,128,256]{2,1,0:T(8,128)(2,1)S(1)}, f32[128,128]{1,0:T(8,128)S(1)}) custom-call(s32[1,4]{1,0:T(1,128)S(1)} %slice.57.refs_0_, s32[1]{0:T(128)} %bitcast.12.refs_1_, f32[256,128]{1,0:T(8,128)S(1)} %broadcast_in_dim.62.refs_2_, bf16[128,4096]{1,0:T(8,128)(2,1)S(1)} %copy-done.1, ...), custom_call_target="tpu_custom_call" | custom-call | flops 3221225472 | bytes 9540000 | tf_op jit(solution)/shard_map/pallas_call | solution.py:197
  77.1 11.6 %collective-permute-start.11 = (bf16[16,128,256]{2,1,0:T(8,128)(2,1)S(1)}, bf16[16,128,256]{2,1,0:T(8,128)(2,1)S(1)}, u32[]{:S(2)}, u32[]{:S(2)}) collective-permute-start(bf16[16,128,256]{2,1,0:T(8,128)(2,1)S(1)} %get-tuple-element.48), channel_id=1, source_target_pairs={{0,1},{1,0},{2,3},{3,2},{4,5},{5,4},{6,7},{7,6},{8,9},{9,8},{10,11... | collective-permute-start | bytes 3145736 | tf_op jit(solution)/shard_map/ppermute | solution.py:263
  88.6 0.1 collective-permute-start.12
  88.7 2.3 %collective-permute-done.12.share_stats = f32[128,128]{1,0:T(8,128)S(1)} collective-permute-done((f32[128,128]{1,0:T(8,128)S(1)}, f32[128,128]{1,0:T(8,128)S(1)}, u32[]{:S(2)}, u32[]{:S(2)}) %collective-permute-start.12) | collective-permute-done | bytes 65568 | tf_op jit(solution)/shard_map/ppermute | solution.py:263
  91.0 0.0 collective-permute-done.11.share
  91.0 1.7 %shard_map.79 = bf16[128,4096]{1,0:T(8,128)(2,1)} custom-call(f32[16,128,256]{2,1,0:T(8,128)S(1)} %get-tuple-element.46.acc, f32[128,128]{1,0:T(8,128)S(1)} %get-tuple-element.47.stats, bf16[16,128,256]{2,1,0:T(8,128)(2,1)S(1)} %collective-permute-done.11.share, f32[128,128]{1,0:T(8,128)S(1)} %collective-permute-done.12.share_stats, f32[128,4096]{1,0:T(8,128)S(1)} %copy-done), custom_call_target="tpu_custom_call" | custom-call | tf_op jit(solution)/shard_map/pallas_call | solution.py:247
  (24 shorter events, 0.2 us)
Async XLA Ops:
  2.3 2.1 %collective-permute-start = (bf16[272,512]{1,0:T(8,128)(2,1)S(1)}, bf16[272,512]{1,0:T(8,128)(2,1)S(1)}, u32[]{:S(2)}, u32[]{:S(2)}) collective-permute-start(bf16[272,512]{1,0:T(8,128)(2,1)S(1)} %pad_maximum_fusion), channel_id=1, source_target_pairs={{0,1},{1,0},{2,3},{3,2},{4,5},{5,4},{6,7},{7,6},{8,9},{9,8},{10,11... | collective-permute-start | bytes 835592 | tf_op jit(solution)/shard_map/ppermute | solution.py:263
  3.1 22.9 %collective-permute-start.1 = (bf16[128,4096]{1,0:T(8,128)(2,1)}, bf16[128,4096]{1,0:T(8,128)(2,1)S(1)}, u32[]{:S(2)}, u32[]{:S(2)}) collective-permute-start(bf16[128,4096]{1,0:T(8,128)(2,1)} %refs_3_.4), channel_id=1, source_target_pairs={{0,1},{1,0},{2,3},{3,2},{4,5},{5,4},{6,7},{7,6},{8,9},{9,8},{10,11... | collective-permute-start | bytes 3145736 | tf_op jit(solution)/shard_map/ppermute | solution.py:263
  5.5 10.1 %collective-permute-start.2 = (bf16[528,512]{1,0:T(8,128)(2,1)S(1)}, bf16[528,512]{1,0:T(8,128)(2,1)S(1)}, u32[]{:S(2)}, u32[]{:S(2)}) collective-permute-start(bf16[528,512]{1,0:T(8,128)(2,1)S(1)} %slice_dynamic-update-slice_fusion.refs_5_), channel_id=1, source_target_pairs={{0,2},{2,4},{4,6},{6,8},{8,10},{10,12},{12,14},{14,32},{16,18},{18... | collective-permute-start | bytes 1622024 | tf_op jit(solution)/shard_map/ppermute | solution.py:263
  8.2 17.9 %copy-start.1 = (bf16[128,4096]{1,0:T(8,128)(2,1)S(1)}, bf16[128,4096]{1,0:T(8,128)(2,1)}, u32[]{:S(2)}) copy-start(bf16[128,4096]{1,0:T(8,128)(2,1)} %refs_3_.4) | copy-start | bytes 3145732
  15.6 14.1 %collective-permute-start.3 = (bf16[528,512]{1,0:T(8,128)(2,1)S(1)}, bf16[528,512]{1,0:T(8,128)(2,1)S(1)}, u32[]{:S(2)}, u32[]{:S(2)}) collective-permute-start(bf16[528,512]{1,0:T(8,128)(2,1)S(1)} %collective-permute-done.2.refs_6_), channel_id=1, source_target_pairs={{17,32},{19,34},{21,36},{23,38},{25,40},{27,42},{29,44},{31,46},{3... | collective-permute-start | bytes 1622024 | tf_op jit(solution)/shard_map/ppermute | solution.py:263
  19.2 11.1 %collective-permute-start.4 = (bf16[528,512]{1,0:T(8,128)(2,1)S(1)}, bf16[528,512]{1,0:T(8,128)(2,1)S(1)}, u32[]{:S(2)}, u32[]{:S(2)}) collective-permute-start(bf16[528,512]{1,0:T(8,128)(2,1)S(1)} %collective-permute-done.2.refs_6_), channel_id=1, source_target_pairs={{17,31},{19,17},{21,19},{23,21},{25,23},{27,25},{29,27},{31,29},{3... | collective-permute-start | bytes 1622024 | tf_op jit(solution)/shard_map/ppermute | solution.py:263
  24.0 13.5 %collective-permute-start.8 = (bf16[528,512]{1,0:T(8,128)(2,1)S(1)}, bf16[528,512]{1,0:T(8,128)(2,1)S(1)}, u32[]{:S(2)}, u32[]{:S(2)}) collective-permute-start(bf16[528,512]{1,0:T(8,128)(2,1)S(1)} %collective-permute-done.2.refs_6_), channel_id=1, source_target_pairs={{2,4},{4,6},{6,8},{8,10},{10,12},{12,14},{14,32},{18,20},{20,22},{... | collective-permute-start | bytes 1622024 | tf_op jit(solution)/shard_map/ppermute | solution.py:263
  30.4 16.7 %collective-permute-start.5 = (bf16[528,512]{1,0:T(8,128)(2,1)S(1)}, bf16[528,512]{1,0:T(8,128)(2,1)S(1)}, u32[]{:S(2)}, u32[]{:S(2)}) collective-permute-start(bf16[528,512]{1,0:T(8,128)(2,1)S(1)} %broadcast_select_fusion), channel_id=1, source_target_pairs={{0,46},{2,0},{4,2},{16,62},{18,16},{20,18},{32,14},{34,32},{36,34}... | collective-permute-start | bytes 1622024 | tf_op jit(solution)/shard_map/ppermute | solution.py:263
  37.5 12.7 %collective-permute-start.9 = (bf16[528,512]{1,0:T(8,128)(2,1)S(1)}, bf16[528,512]{1,0:T(8,128)(2,1)S(1)}, u32[]{:S(2)}, u32[]{:S(2)}) collective-permute-start(bf16[528,512]{1,0:T(8,128)(2,1)S(1)} %collective-permute-done.8.refs_7_), channel_id=1, source_target_pairs={{4,6},{6,8},{8,10},{10,12},{12,14},{14,32},{20,22},{22,24},{24,26}... | collective-permute-start | bytes 1622024 | tf_op jit(solution)/shard_map/ppermute | solution.py:263
  47.2 13.2 %collective-permute-start.6 = (bf16[528,512]{1,0:T(8,128)(2,1)S(1)}, bf16[528,512]{1,0:T(8,128)(2,1)S(1)}, u32[]{:S(2)}, u32[]{:S(2)}) collective-permute-start(bf16[528,512]{1,0:T(8,128)(2,1)S(1)} %collective-permute-done.5.refs_5_), channel_id=1, source_target_pairs={{0,46},{2,0},{14,12},{16,62},{18,16},{30,28},{32,14},{34,32},{36,3... | collective-permute-start | bytes 1622024 | tf_op jit(solution)/shard_map/ppermute | solution.py:263
  50.3 13.6 %collective-permute-start.10 = (bf16[528,512]{1,0:T(8,128)(2,1)S(1)}, bf16[528,512]{1,0:T(8,128)(2,1)S(1)}, u32[]{:S(2)}, u32[]{:S(2)}) collective-permute-start(bf16[528,512]{1,0:T(8,128)(2,1)S(1)} %collective-permute-done.9.refs_6_), channel_id=1, source_target_pairs={{6,8},{8,10},{10,12},{12,14},{14,32},{22,24},{24,26},{26,28},{28,3... | collective-permute-start | bytes 1622024 | tf_op jit(solution)/shard_map/ppermute | solution.py:263
  60.4 12.4 %collective-permute-start.7 = (bf16[528,512]{1,0:T(8,128)(2,1)S(1)}, bf16[528,512]{1,0:T(8,128)(2,1)S(1)}, u32[]{:S(2)}, u32[]{:S(2)}) collective-permute-start(bf16[528,512]{1,0:T(8,128)(2,1)S(1)} %collective-permute-done.6.refs_5_), channel_id=1, source_target_pairs={{0,46},{12,10},{14,12},{16,62},{28,26},{30,28},{32,14},{34,32},{36... | collective-permute-start | bytes 1622024 | tf_op jit(solution)/shard_map/ppermute | solution.py:263
  72.8 18.2 %copy-start = (f32[128,4096]{1,0:T(8,128)S(1)}, f32[128,4096]{1,0:T(8,128)}, u32[]{:S(2)}) copy-start(f32[128,4096]{1,0:T(8,128)} %shard_map.73.sigmoid) | copy-start | bytes 6291460
  77.1 14.0 %collective-permute-start.11 = (bf16[16,128,256]{2,1,0:T(8,128)(2,1)S(1)}, bf16[16,128,256]{2,1,0:T(8,128)(2,1)S(1)}, u32[]{:S(2)}, u32[]{:S(2)}) collective-permute-start(bf16[16,128,256]{2,1,0:T(8,128)(2,1)S(1)} %get-tuple-element.48), channel_id=1, source_target_pairs={{0,1},{1,0},{2,3},{3,2},{4,5},{5,4},{6,7},{7,6},{8,9},{9,8},{10,11... | collective-permute-start | bytes 3145736 | tf_op jit(solution)/shard_map/ppermute | solution.py:263
  88.6 2.4 %collective-permute-start.12 = (f32[128,128]{1,0:T(8,128)S(1)}, f32[128,128]{1,0:T(8,128)S(1)}, u32[]{:S(2)}, u32[]{:S(2)}) collective-permute-start(f32[128,128]{1,0:T(8,128)S(1)} %get-tuple-element.49), channel_id=1, source_target_pairs={{0,1},{1,0},{2,3},{3,2},{4,5},{5,4},{6,7},{7,6},{8,9},{9,8},{10,11... | collective-permute-start | bytes 196616 | tf_op jit(solution)/shard_map/ppermute | solution.py:263

commit v8 on v1

--- a/solution.py
+++ b/solution.py
@@ -221,6 +221,7 @@
             down.append(send(down[-1], NEAR_DOWN))
             mdown.append(send(mdown[-1], MID_DOWN))
 
+    query_rows, gate_rows, _ = lax.optimization_barrier((query_rows, gate_rows, unit))
     q_other = send(take(query_rows, 1 - core, HALF), SWAP)
     gate_other = send(take(gate_rows, 1 - core, HALF), SWAP)
     q = jnp.concatenate([take(query_rows, core, HALF), q_other], axis=0)

time: 92.1 us -> 94.5 us (1.026)
  Pallas kernels: 20.7 us -> 22.7 us
  other arithmetic: 2.95 us -> 4.41 us
  waiting for transfers between devices: 3.37 us -> 2.21 us
    dynamic_slice x2, local copies, waits for them, and re-layouts: 3.25 us -> 1.08 us  [take(): return lax.dynamic_slice_in_dim(rows, which * width, width, 1)]
    pallas_call x5, Pallas kernels: 20.7 us -> 22.7 us  [attend_call(): pl.pallas_call(functools.partial(attend, own_at, last, count), out_shape=...]
    unnamed x13 -> x7, local copies, waits for them, and re-layouts: 0.06 us -> 1.79 us
    ppermute x20, waiting for transfers between devices: 3.37 us -> 2.21 us  [send(): return lax.ppermute(value, 'cp', pairs)]
  transfers between devices with their start and end apart: 20 -> 20, of which waited for: 3 -> 2; matrix products, arithmetic and copies ran while one was open for 4% -> 4% of each run, Pallas kernels for 16% -> 17%
where the time goes in v8:
time: 94.5 us; the launch traced here: 93.9 us
  starting transfers between devices  60.2 us (64%)
  Pallas kernels  22.7 us (24%)
  other arithmetic  4.41 us (5%)
  local copies, waits for them, and re-layouts  4.01 us (4%)
  waiting for transfers between devices  2.21 us (2%)
    ppermute x20, starting transfers between devices, send(): return lax.ppermute(value, 'cp', pairs)  60.2 us
    pallas_call x5, Pallas kernels, attend_call(): pl.pallas_call(functools.partial(attend, own_at, last, count), out_shape=...  22.7 us
    ppermute x20, waiting for transfers between devices, send(): return lax.ppermute(value, 'cp', pairs)  2.21 us
  transfers between devices with their start and end apart: 20, of which 2 were waited for; matrix products, arithmetic and copies ran while one was open for 4% of the time, Pallas kernels for 17%

profile of v8, /device:TPU:15, one launch (start us, length us, event | category | flops | bytes accessed | tf_op | source)
XLA Modules:
  0.0 93.9 jit_solution(12953456251301813732)
XLA Ops:
  0.0 0.8 convert_element_type.15
  0.8 0.7 convert_bitcast_fusion
  1.5 0.9 dynamic-slice_dynamic-update-slice_fusion.1
  2.4 0.8 collective-permute-start
  3.2 0.1 stack.83
  3.3 0.1 pad_add_fusion
  3.5 0.1 iota_compare_fusion
  3.6 0.6 collective-permute-done
  4.2 0.9 dynamic-slice_dynamic-update-slice_fusion
  5.1 1.3 %collective-permute-start.10 = (bf16[528,256]{1,0:T(8,128)(2,1)S(1)}, bf16[528,256]{1,0:T(8,128)(2,1)S(1)}, u32[]{:S(2)}, u32[]{:S(2)}) collective-permute-start(bf16[528,256]{1,0:T(8,128)(2,1)S(1)} %slice_dynamic-update-slice_fusion.refs_4_), channel_id=1, source_target_pairs={{0,16},{1,17},{2,18},{3,19},{4,20},{5,21},{6,22},{7,23},{8,24},{9,... | collective-permute-start | bytes 811016 | tf_op jit(solution)/shard_map/ppermute | solution.py:185
  6.4 3.5 %collective-permute-start.2 = (bf16[528,256]{1,0:T(8,128)(2,1)S(1)}, bf16[528,256]{1,0:T(8,128)(2,1)S(1)}, u32[]{:S(2)}, u32[]{:S(2)}) collective-permute-start(bf16[528,256]{1,0:T(8,128)(2,1)S(1)} %slice_dynamic-update-slice_fusion.refs_4_), channel_id=1, source_target_pairs={{0,2},{1,3},{2,4},{3,5},{4,6},{5,7},{6,8},{7,9},{8,10},{9,11},{10,... | collective-permute-start | bytes 811016 | tf_op jit(solution)/shard_map/ppermute | solution.py:185
  9.9 3.1 %collective-permute-start.6 = (bf16[528,256]{1,0:T(8,128)(2,1)S(1)}, bf16[528,256]{1,0:T(8,128)(2,1)S(1)}, u32[]{:S(2)}, u32[]{:S(2)}) collective-permute-start(bf16[528,256]{1,0:T(8,128)(2,1)S(1)} %slice_dynamic-update-slice_fusion.refs_4_), channel_id=1, source_target_pairs={{0,32},{1,33},{2,34},{3,35},{4,36},{5,37},{6,38},{7,39},{8,40},{9,... | collective-permute-start | bytes 811016 | tf_op jit(solution)/shard_map/ppermute | solution.py:185
  13.0 1.0 %constant_dynamic-slice_fusion.2 = (bf16[128,2048]{1,0:T(8,128)(2,1)}, bf16[128,2048]{1,0:T(8,128)(2,1)}) fusion(bf16[128,4096]{1,0:T(8,128)(2,1)S(1)} %copy-done.1, s32[]{:T(128)S(6)} %select_n.147, s32[]{:T(128)S(6)} %select_n.148), kind=kLoop, calls=%fused_computation.23 | loop fusion | bytes 2097160 | tf_op jit(solution)/shard_map/dynamic_slice | solution.py:188
  14.0 1.2 %collective-permute-start.1 = (bf16[128,2048]{1,0:T(8,128)(2,1)}, bf16[128,2048]{1,0:T(8,128)(2,1)}, u32[]{:S(2)}, u32[]{:S(2)}) collective-permute-start(bf16[128,2048]{1,0:T(8,128)(2,1)} %get-tuple-element.38), channel_id=1, source_target_pairs={{0,1},{1,0},{2,3},{3,2},{4,5},{5,4},{6,7},{7,6},{8,9},{9,8},{10,11... | collective-permute-start | bytes 1572872 | tf_op jit(solution)/shard_map/ppermute | solution.py:185
  15.3 3.5 %collective-permute-start.11 = (bf16[528,256]{1,0:T(8,128)(2,1)S(1)}, bf16[528,256]{1,0:T(8,128)(2,1)S(1)}, u32[]{:S(2)}, u32[]{:S(2)}) collective-permute-start(bf16[528,256]{1,0:T(8,128)(2,1)S(1)} %collective-permute-done.10.refs_6_), channel_id=1, source_target_pairs={{16,18},{17,19},{18,20},{19,21},{20,22},{21,23},{22,24},{23,25},{2... | collective-permute-start | bytes 811016 | tf_op jit(solution)/shard_map/ppermute | solution.py:185
  18.8 0.1 select_reduce_fusion
  19.0 5.3 %collective-permute-start.14 = (bf16[528,256]{1,0:T(8,128)(2,1)S(1)}, bf16[528,256]{1,0:T(8,128)(2,1)S(1)}, u32[]{:S(2)}, u32[]{:S(2)}) collective-permute-start(bf16[528,256]{1,0:T(8,128)(2,1)S(1)} %collective-permute-done.10.refs_6_), channel_id=1, source_target_pairs={{16,30},{17,31},{18,16},{19,17},{20,18},{21,19},{22,20},{23,21},{2... | collective-permute-start | bytes 811016 | tf_op jit(solution)/shard_map/ppermute | solution.py:185
  24.3 1.9 %collective-permute-start.3 = (bf16[528,256]{1,0:T(8,128)(2,1)S(1)}, bf16[528,256]{1,0:T(8,128)(2,1)S(1)}, u32[]{:S(2)}, u32[]{:S(2)}) collective-permute-start(bf16[528,256]{1,0:T(8,128)(2,1)S(1)} %collective-permute-done.2.refs_4_), channel_id=1, source_target_pairs={{0,2},{1,3},{2,4},{3,5},{4,6},{5,7},{6,8},{7,9},{8,10},{9,11},{10,... | collective-permute-start | bytes 811016 | tf_op jit(solution)/shard_map/ppermute | solution.py:185
  26.2 5.1 %collective-permute-start.7 = (bf16[528,256]{1,0:T(8,128)(2,1)S(1)}, bf16[528,256]{1,0:T(8,128)(2,1)S(1)}, u32[]{:S(2)}, u32[]{:S(2)}) collective-permute-start(bf16[528,256]{1,0:T(8,128)(2,1)S(1)} %collective-permute-done.6.refs_5_), channel_id=1, source_target_pairs={{0,46},{1,47},{2,0},{3,1},{4,2},{5,3},{6,4},{7,5},{8,6},{9,7},{10,... | collective-permute-start | bytes 811016 | tf_op jit(solution)/shard_map/ppermute | solution.py:185
  31.4 1.9 %collective-permute-start.12 = (bf16[528,256]{1,0:T(8,128)(2,1)S(1)}, bf16[528,256]{1,0:T(8,128)(2,1)S(1)}, u32[]{:S(2)}, u32[]{:S(2)}) collective-permute-start(bf16[528,256]{1,0:T(8,128)(2,1)S(1)} %collective-permute-done.11.refs_6_), channel_id=1, source_target_pairs={{16,18},{17,19},{18,20},{19,21},{20,22},{21,23},{22,24},{23,25},{2... | collective-permute-start | bytes 811016 | tf_op jit(solution)/shard_map/ppermute | solution.py:185
  33.3 0.1 slice.67.refs_0_
  33.4 0.1 copy.29
  33.5 0.1 copy.30.refs_0_
  33.6 0.1 copy.28
  33.7 0.1 copy.31.refs_0_
  33.8 0.1 copy.27
  33.9 0.1 copy.32.refs_0_
  34.0 0.1 copy.25
  34.1 0.1 copy.33.refs_0_
  34.2 2.9 %collective-permute-start.18 = (bf16[128,2048]{1,0:T(8,128)(2,1)S(1)}, bf16[128,2048]{1,0:T(8,128)(2,1)S(1)}, u32[]{:S(2)}, u32[]{:S(2)}) collective-permute-start(bf16[128,2048]{1,0:T(8,128)(2,1)S(1)} %constant_dynamic-slice_fusion), channel_id=1, source_target_pairs={{0,1},{1,0},{2,3},{3,2},{4,5},{5,4},{6,7},{7,6},{8,9},{9,8},{10,11... | collective-permute-start | bytes 1572872 | tf_op jit(solution)/shard_map/ppermute | solution.py:185
  37.2 4.8 %collective-permute-start.15 = (bf16[528,256]{1,0:T(8,128)(2,1)S(1)}, bf16[528,256]{1,0:T(8,128)(2,1)S(1)}, u32[]{:S(2)}, u32[]{:S(2)}) collective-permute-start(bf16[528,256]{1,0:T(8,128)(2,1)S(1)} %collective-permute-done.14.refs_7_), channel_id=1, source_target_pairs={{16,30},{17,31},{18,16},{19,17},{20,18},{21,19},{22,20},{23,21},{2... | collective-permute-start | bytes 811016 | tf_op jit(solution)/shard_map/ppermute | solution.py:185
  42.0 1.9 %collective-permute-start.4 = (bf16[528,256]{1,0:T(8,128)(2,1)S(1)}, bf16[528,256]{1,0:T(8,128)(2,1)S(1)}, u32[]{:S(2)}, u32[]{:S(2)}) collective-permute-start(bf16[528,256]{1,0:T(8,128)(2,1)S(1)} %collective-permute-done.3.refs_4_), channel_id=1, source_target_pairs={{0,2},{1,3},{2,4},{3,5},{4,6},{5,7},{6,8},{7,9},{8,10},{9,11},{10,... | collective-permute-start | bytes 811016 | tf_op jit(solution)/shard_map/ppermute | solution.py:185
  44.0 5.1 %collective-permute-start.8 = (bf16[528,256]{1,0:T(8,128)(2,1)S(1)}, bf16[528,256]{1,0:T(8,128)(2,1)S(1)}, u32[]{:S(2)}, u32[]{:S(2)}) collective-permute-start(bf16[528,256]{1,0:T(8,128)(2,1)S(1)} %collective-permute-done.7.refs_5_), channel_id=1, source_target_pairs={{0,46},{1,47},{2,0},{3,1},{4,2},{5,3},{6,4},{7,5},{8,6},{9,7},{10,... | collective-permute-start | bytes 811016 | tf_op jit(solution)/shard_map/ppermute | solution.py:185
  49.1 1.9 %collective-permute-start.13 = (bf16[528,256]{1,0:T(8,128)(2,1)S(1)}, bf16[528,256]{1,0:T(8,128)(2,1)S(1)}, u32[]{:S(2)}, u32[]{:S(2)}) collective-permute-start(bf16[528,256]{1,0:T(8,128)(2,1)S(1)} %collective-permute-done.12.refs_6_), channel_id=1, source_target_pairs={{16,18},{17,19},{18,20},{19,21},{20,22},{21,23},{22,24},{23,25},{2... | collective-permute-start | bytes 811016 | tf_op jit(solution)/shard_map/ppermute | solution.py:185
  51.0 1.3 %pad_maximum_fusion = bf16[256,2048]{1,0:T(8,128)(2,1)S(1)} fusion(bf16[128,2048]{1,0:T(8,128)(2,1)} %collective-permute-done.1, bf16[128,2048]{1,0:T(8,128)(2,1)} %get-tuple-element.37), kind=kLoop, calls=%fused_computation.1 | loop fusion | flops 2097152 | bytes 2097152 | tf_op jit(solution)/shard_map/concatenate | solution.py:227
  52.4 0.1 broadcast_in_dim.56.refs_3_
  52.5 1.7 %shard_map.64 = (f32[8,256,128]{2,1,0:T(8,128)S(1)}, f32[8,256,128]{2,1,0:T(8,128)S(1)}, f32[8,256,256]{2,1,0:T(8,128)S(1)}) custom-call(s32[1,4]{1,0:T(1,128)S(1)} %slice.67.refs_0_, s32[1]{0:T(128)} %bitcast.17.refs_1_, bf16[2048,256]{1,0:T(8,128)(2,1)S(1)} %bitcast.33, f32[256,128]{1,0:T(8,128)S(1)} %broadcast_in_dim.56.refs_3_, ...), custom_call_target="tpu_custom_call" | custom-call | flops 536870912 | bytes 9270000 | tf_op jit(solution)/shard_map/pallas_call | solution.py:163
  54.2 4.0 %shard_map.65 = (f32[8,256,128]{2,1,0:T(8,128)S(1)}, f32[8,256,128]{2,1,0:T(8,128)S(1)}, f32[8,256,256]{2,1,0:T(8,128)S(1)}) custom-call(s32[3,4]{1,0:T(4,128)S(1)} %copy.30.refs_0_, s32[1]{0:T(128)} %bitcast.17.refs_1_, bf16[2048,256]{1,0:T(8,128)(2,1)S(1)} %bitcast.34, ...), custom_call_target="tpu_custom_call", output_to_operand_aliasing={{0}: (7, {}), {1}: (8, {}), {2}: (9, {})} | custom-call | flops 1610612736 | bytes 9810000 | tf_op jit(solution)/shard_map/pallas_call | solution.py:163
  58.3 4.6 %collective-permute-start.16 = (bf16[528,256]{1,0:T(8,128)(2,1)S(1)}, bf16[528,256]{1,0:T(8,128)(2,1)S(1)}, u32[]{:S(2)}, u32[]{:S(2)}) collective-permute-start(bf16[528,256]{1,0:T(8,128)(2,1)S(1)} %collective-permute-done.15.refs_7_), channel_id=1, source_target_pairs={{16,30},{17,31},{18,16},{19,17},{20,18},{21,19},{22,20},{23,21},{2... | collective-permute-start | bytes 811016 | tf_op jit(solution)/shard_map/ppermute | solution.py:185
  62.9 1.9 %collective-permute-start.5 = (bf16[528,256]{1,0:T(8,128)(2,1)S(1)}, bf16[528,256]{1,0:T(8,128)(2,1)S(1)}, u32[]{:S(2)}, u32[]{:S(2)}) collective-permute-start(bf16[528,256]{1,0:T(8,128)(2,1)S(1)} %collective-permute-done.4.refs_4_), channel_id=1, source_target_pairs={{0,2},{1,3},{2,4},{3,5},{4,6},{5,7},{6,8},{7,9},{8,10},{9,11},{10,... | collective-permute-start | bytes 811016 | tf_op jit(solution)/shard_map/ppermute | solution.py:185
  64.8 5.1 %collective-permute-start.9 = (bf16[528,256]{1,0:T(8,128)(2,1)S(1)}, bf16[528,256]{1,0:T(8,128)(2,1)S(1)}, u32[]{:S(2)}, u32[]{:S(2)}) collective-permute-start(bf16[528,256]{1,0:T(8,128)(2,1)S(1)} %collective-permute-done.8.refs_5_), channel_id=1, source_target_pairs={{0,46},{1,47},{2,0},{3,1},{4,2},{5,3},{6,4},{7,5},{8,6},{9,7},{10,... | collective-permute-start | bytes 811016 | tf_op jit(solution)/shard_map/ppermute | solution.py:185
  69.9 2.1 %collective-permute-start.17 = (bf16[528,256]{1,0:T(8,128)(2,1)S(1)}, bf16[528,256]{1,0:T(8,128)(2,1)S(1)}, u32[]{:S(2)}, u32[]{:S(2)}) collective-permute-start(bf16[528,256]{1,0:T(8,128)(2,1)S(1)} %collective-permute-done.13.refs_6_), channel_id=1, source_target_pairs={{16,18},{17,19},{18,20},{19,21},{20,22},{21,23},{22,24},{23,25},{2... | collective-permute-start | bytes 811016 | tf_op jit(solution)/shard_map/ppermute | solution.py:185
  72.0 5.2 %shard_map.66 = (f32[8,256,128]{2,1,0:T(8,128)S(1)}, f32[8,256,128]{2,1,0:T(8,128)S(1)}, f32[8,256,256]{2,1,0:T(8,128)S(1)}) custom-call(s32[4,4]{1,0:T(4,128)S(1)} %copy.31.refs_0_, s32[1]{0:T(128)} %bitcast.17.refs_1_, bf16[2048,256]{1,0:T(8,128)(2,1)S(1)} %bitcast.35, ...), custom_call_target="tpu_custom_call", output_to_operand_aliasing={{0}: (8, {}), {1}: (9, {}), {2}: (10, {})} | custom-call | flops 2147483648 | bytes 10080000 | tf_op jit(solution)/shard_map/pallas_call | solution.py:163
  77.3 5.2 %shard_map.67 = (f32[8,256,128]{2,1,0:T(8,128)S(1)}, f32[8,256,128]{2,1,0:T(8,128)S(1)}, f32[8,256,256]{2,1,0:T(8,128)S(1)}) custom-call(s32[4,4]{1,0:T(4,128)S(1)} %copy.32.refs_0_, s32[1]{0:T(128)} %bitcast.17.refs_1_, bf16[2048,256]{1,0:T(8,128)(2,1)S(1)} %bitcast.36, ...), custom_call_target="tpu_custom_call", output_to_operand_aliasing={{0}: (8, {}), {1}: (9, {}), {2}: (10, {})} | custom-call | flops 2147483648 | bytes 10080000 | tf_op jit(solution)/shard_map/pallas_call | solution.py:163
  82.5 6.6 %shard_map.68 = (bf16[128,2048]{1,0:T(8,128)(2,1)S(1)}, bf16[128,2048]{1,0:T(8,128)(2,1)S(1)}) custom-call(s32[5,4]{1,0:T(8,128)S(1)} %copy.33.refs_0_, s32[1]{0:T(128)} %bitcast.17.refs_1_, bf16[2048,256]{1,0:T(8,128)(2,1)S(1)} %bitcast.37, f32[256,128]{1,0:T(8,128)S(1)} %broadcast_in_dim.56.refs_3_, bf16[528,256]{1,0:T(8,128)(2,1)S(1)} %collective-permute-done.5.refs_4_, ...), custom_call_target="tpu_custom_call" | custom-call | flops 2684354560 | bytes 10350000 | tf_op jit(solution)/shard_map/pallas_call | solution.py:163
  89.1 2.1 %collective-permute-start.19 = (bf16[128,2048]{1,0:T(8,128)(2,1)S(1)}, bf16[128,2048]{1,0:T(8,128)(2,1)S(1)}, u32[]{:S(2)}, u32[]{:S(2)}) collective-permute-start(bf16[128,2048]{1,0:T(8,128)(2,1)S(1)} %get-tuple-element.36), channel_id=1, source_target_pairs={{0,1},{1,0},{2,3},{3,2},{4,5},{5,4},{6,7},{7,6},{8,9},{9,8},{10,11... | collective-permute-start | bytes 1572872 | tf_op jit(solution)/shard_map/ppermute | solution.py:185
  91.2 1.5 %collective-permute-done.19 = bf16[128,2048]{1,0:T(8,128)(2,1)S(1)} collective-permute-done((bf16[128,2048]{1,0:T(8,128)(2,1)S(1)}, bf16[128,2048]{1,0:T(8,128)(2,1)S(1)}, u32[]{:S(2)}, u32[]{:S(2)}) %collective-permute-start.19) | collective-permute-done | bytes 524320 | tf_op jit(solution)/shard_map/ppermute | solution.py:185
  92.7 1.2 %maximum_select_fusion = bf16[128,4096]{1,0:T(8,128)(2,1)} fusion(bf16[128,2048]{1,0:T(8,128)(2,1)S(1)} %collective-permute-done.19, bf16[128,2048]{1,0:T(8,128)(2,1)S(1)} %get-tuple-element.35, pred[]{:T(512)S(6)} %eq.21), kind=kLoop, calls=%fused_computation.2 | loop fusion | flops 4718592 | bytes 2097153 | tf_op jit(solution)/shard_map/jit(_where)/select_n | solution.py:276
  (44 shorter events, 0.3 us)
Async XLA Ops:
  0.0 13.0 %copy-start.1 = (bf16[128,4096]{1,0:T(8,128)(2,1)S(1)}, bf16[128,4096]{1,0:T(8,128)(2,1)}, u32[]{:S(2)}) copy-start(bf16[128,4096]{1,0:T(8,128)(2,1)} %param.6) | copy-start | bytes 3145732
  0.0 34.2 %copy-start = (bf16[128,4096]{1,0:T(8,128)(2,1)S(1)}, bf16[128,4096]{1,0:T(8,128)(2,1)}, u32[]{:S(2)}) copy-start(bf16[128,4096]{1,0:T(8,128)(2,1)} %refs_12_) | copy-start | bytes 3145732
  2.4 1.8 %collective-permute-start = (bf16[272,256]{1,0:T(8,128)(2,1)S(1)}, bf16[272,256]{1,0:T(8,128)(2,1)S(1)}, u32[]{:S(2)}, u32[]{:S(2)}) collective-permute-start(bf16[272,256]{1,0:T(8,128)(2,1)S(1)} %pad_maximum_fusion.1), channel_id=1, source_target_pairs={{0,1},{1,0},{2,3},{3,2},{4,5},{5,4},{6,7},{7,6},{8,9},{9,8},{10,11... | collective-permute-start | bytes 417800 | tf_op jit(solution)/shard_map/ppermute | solution.py:185
  5.1 10.2 %collective-permute-start.10 = (bf16[528,256]{1,0:T(8,128)(2,1)S(1)}, bf16[528,256]{1,0:T(8,128)(2,1)S(1)}, u32[]{:S(2)}, u32[]{:S(2)}) collective-permute-start(bf16[528,256]{1,0:T(8,128)(2,1)S(1)} %slice_dynamic-update-slice_fusion.refs_4_), channel_id=1, source_target_pairs={{0,16},{1,17},{2,18},{3,19},{4,20},{5,21},{6,22},{7,23},{8,24},{9,... | collective-permute-start | bytes 811016 | tf_op jit(solution)/shard_map/ppermute | solution.py:185
  6.4 17.9 %collective-permute-start.2 = (bf16[528,256]{1,0:T(8,128)(2,1)S(1)}, bf16[528,256]{1,0:T(8,128)(2,1)S(1)}, u32[]{:S(2)}, u32[]{:S(2)}) collective-permute-start(bf16[528,256]{1,0:T(8,128)(2,1)S(1)} %slice_dynamic-update-slice_fusion.refs_4_), channel_id=1, source_target_pairs={{0,2},{1,3},{2,4},{3,5},{4,6},{5,7},{6,8},{7,9},{8,10},{9,11},{10,... | collective-permute-start | bytes 811016 | tf_op jit(solution)/shard_map/ppermute | solution.py:185
  9.9 16.3 %collective-permute-start.6 = (bf16[528,256]{1,0:T(8,128)(2,1)S(1)}, bf16[528,256]{1,0:T(8,128)(2,1)S(1)}, u32[]{:S(2)}, u32[]{:S(2)}) collective-permute-start(bf16[528,256]{1,0:T(8,128)(2,1)S(1)} %slice_dynamic-update-slice_fusion.refs_4_), channel_id=1, source_target_pairs={{0,32},{1,33},{2,34},{3,35},{4,36},{5,37},{6,38},{7,39},{8,40},{9,... | collective-permute-start | bytes 811016 | tf_op jit(solution)/shard_map/ppermute | solution.py:185
  14.0 20.2 %collective-permute-start.1 = (bf16[128,2048]{1,0:T(8,128)(2,1)}, bf16[128,2048]{1,0:T(8,128)(2,1)}, u32[]{:S(2)}, u32[]{:S(2)}) collective-permute-start(bf16[128,2048]{1,0:T(8,128)(2,1)} %get-tuple-element.38), channel_id=1, source_target_pairs={{0,1},{1,0},{2,3},{3,2},{4,5},{5,4},{6,7},{7,6},{8,9},{9,8},{10,11... | collective-permute-start | bytes 1572872 | tf_op jit(solution)/shard_map/ppermute | solution.py:185
  15.3 16.1 %collective-permute-start.11 = (bf16[528,256]{1,0:T(8,128)(2,1)S(1)}, bf16[528,256]{1,0:T(8,128)(2,1)S(1)}, u32[]{:S(2)}, u32[]{:S(2)}) collective-permute-start(bf16[528,256]{1,0:T(8,128)(2,1)S(1)} %collective-permute-done.10.refs_6_), channel_id=1, source_target_pairs={{16,18},{17,19},{18,20},{19,21},{20,22},{21,23},{22,24},{23,25},{2... | collective-permute-start | bytes 811016 | tf_op jit(solution)/shard_map/ppermute | solution.py:185
  19.0 18.2 %collective-permute-start.14 = (bf16[528,256]{1,0:T(8,128)(2,1)S(1)}, bf16[528,256]{1,0:T(8,128)(2,1)S(1)}, u32[]{:S(2)}, u32[]{:S(2)}) collective-permute-start(bf16[528,256]{1,0:T(8,128)(2,1)S(1)} %collective-permute-done.10.refs_6_), channel_id=1, source_target_pairs={{16,30},{17,31},{18,16},{19,17},{20,18},{21,19},{22,20},{23,21},{2... | collective-permute-start | bytes 811016 | tf_op jit(solution)/shard_map/ppermute | solution.py:185
  24.3 17.8 %collective-permute-start.3 = (bf16[528,256]{1,0:T(8,128)(2,1)S(1)}, bf16[528,256]{1,0:T(8,128)(2,1)S(1)}, u32[]{:S(2)}, u32[]{:S(2)}) collective-permute-start(bf16[528,256]{1,0:T(8,128)(2,1)S(1)} %collective-permute-done.2.refs_4_), channel_id=1, source_target_pairs={{0,2},{1,3},{2,4},{3,5},{4,6},{5,7},{6,8},{7,9},{8,10},{9,11},{10,... | collective-permute-start | bytes 811016 | tf_op jit(solution)/shard_map/ppermute | solution.py:185
  26.2 17.8 %collective-permute-start.7 = (bf16[528,256]{1,0:T(8,128)(2,1)S(1)}, bf16[528,256]{1,0:T(8,128)(2,1)S(1)}, u32[]{:S(2)}, u32[]{:S(2)}) collective-permute-start(bf16[528,256]{1,0:T(8,128)(2,1)S(1)} %collective-permute-done.6.refs_5_), channel_id=1, source_target_pairs={{0,46},{1,47},{2,0},{3,1},{4,2},{5,3},{6,4},{7,5},{8,6},{9,7},{10,... | collective-permute-start | bytes 811016 | tf_op jit(solution)/shard_map/ppermute | solution.py:185
  31.4 17.8 %collective-permute-start.12 = (bf16[528,256]{1,0:T(8,128)(2,1)S(1)}, bf16[528,256]{1,0:T(8,128)(2,1)S(1)}, u32[]{:S(2)}, u32[]{:S(2)}) collective-permute-start(bf16[528,256]{1,0:T(8,128)(2,1)S(1)} %collective-permute-done.11.refs_6_), channel_id=1, source_target_pairs={{16,18},{17,19},{18,20},{19,21},{20,22},{21,23},{22,24},{23,25},{2... | collective-permute-start | bytes 811016 | tf_op jit(solution)/shard_map/ppermute | solution.py:185
  34.2 48.2 %collective-permute-start.18 = (bf16[128,2048]{1,0:T(8,128)(2,1)S(1)}, bf16[128,2048]{1,0:T(8,128)(2,1)S(1)}, u32[]{:S(2)}, u32[]{:S(2)}) collective-permute-start(bf16[128,2048]{1,0:T(8,128)(2,1)S(1)} %constant_dynamic-slice_fusion), channel_id=1, source_target_pairs={{0,1},{1,0},{2,3},{3,2},{4,5},{5,4},{6,7},{7,6},{8,9},{9,8},{10,11... | collective-permute-start | bytes 1572872 | tf_op jit(solution)/shard_map/ppermute | solution.py:185
  37.2 21.1 %collective-permute-start.15 = (bf16[528,256]{1,0:T(8,128)(2,1)S(1)}, bf16[528,256]{1,0:T(8,128)(2,1)S(1)}, u32[]{:S(2)}, u32[]{:S(2)}) collective-permute-start(bf16[528,256]{1,0:T(8,128)(2,1)S(1)} %collective-permute-done.14.refs_7_), channel_id=1, source_target_pairs={{16,30},{17,31},{18,16},{19,17},{20,18},{21,19},{22,20},{23,21},{2... | collective-permute-start | bytes 811016 | tf_op jit(solution)/shard_map/ppermute | solution.py:185
  42.0 20.8 %collective-permute-start.4 = (bf16[528,256]{1,0:T(8,128)(2,1)S(1)}, bf16[528,256]{1,0:T(8,128)(2,1)S(1)}, u32[]{:S(2)}, u32[]{:S(2)}) collective-permute-start(bf16[528,256]{1,0:T(8,128)(2,1)S(1)} %collective-permute-done.3.refs_4_), channel_id=1, source_target_pairs={{0,2},{1,3},{2,4},{3,5},{4,6},{5,7},{6,8},{7,9},{8,10},{9,11},{10,... | collective-permute-start | bytes 811016 | tf_op jit(solution)/shard_map/ppermute | solution.py:185
  44.0 20.8 %collective-permute-start.8 = (bf16[528,256]{1,0:T(8,128)(2,1)S(1)}, bf16[528,256]{1,0:T(8,128)(2,1)S(1)}, u32[]{:S(2)}, u32[]{:S(2)}) collective-permute-start(bf16[528,256]{1,0:T(8,128)(2,1)S(1)} %collective-permute-done.7.refs_5_), channel_id=1, source_target_pairs={{0,46},{1,47},{2,0},{3,1},{4,2},{5,3},{6,4},{7,5},{8,6},{9,7},{10,... | collective-permute-start | bytes 811016 | tf_op jit(solution)/shard_map/ppermute | solution.py:185
  49.1 20.8 %collective-permute-start.13 = (bf16[528,256]{1,0:T(8,128)(2,1)S(1)}, bf16[528,256]{1,0:T(8,128)(2,1)S(1)}, u32[]{:S(2)}, u32[]{:S(2)}) collective-permute-start(bf16[528,256]{1,0:T(8,128)(2,1)S(1)} %collective-permute-done.12.refs_6_), channel_id=1, source_target_pairs={{16,18},{17,19},{18,20},{19,21},{20,22},{21,23},{22,24},{23,25},{2... | collective-permute-start | bytes 811016 | tf_op jit(solution)/shard_map/ppermute | solution.py:185
  58.3 24.2 %collective-permute-start.16 = (bf16[528,256]{1,0:T(8,128)(2,1)S(1)}, bf16[528,256]{1,0:T(8,128)(2,1)S(1)}, u32[]{:S(2)}, u32[]{:S(2)}) collective-permute-start(bf16[528,256]{1,0:T(8,128)(2,1)S(1)} %collective-permute-done.15.refs_7_), channel_id=1, source_target_pairs={{16,30},{17,31},{18,16},{19,17},{20,18},{21,19},{22,20},{23,21},{2... | collective-permute-start | bytes 811016 | tf_op jit(solution)/shard_map/ppermute | solution.py:185
  62.9 19.6 %collective-permute-start.5 = (bf16[528,256]{1,0:T(8,128)(2,1)S(1)}, bf16[528,256]{1,0:T(8,128)(2,1)S(1)}, u32[]{:S(2)}, u32[]{:S(2)}) collective-permute-start(bf16[528,256]{1,0:T(8,128)(2,1)S(1)} %collective-permute-done.4.refs_4_), channel_id=1, source_target_pairs={{0,2},{1,3},{2,4},{3,5},{4,6},{5,7},{6,8},{7,9},{8,10},{9,11},{10,... | collective-permute-start | bytes 811016 | tf_op jit(solution)/shard_map/ppermute | solution.py:185
  64.8 17.7 %collective-permute-start.9 = (bf16[528,256]{1,0:T(8,128)(2,1)S(1)}, bf16[528,256]{1,0:T(8,128)(2,1)S(1)}, u32[]{:S(2)}, u32[]{:S(2)}) collective-permute-start(bf16[528,256]{1,0:T(8,128)(2,1)S(1)} %collective-permute-done.8.refs_5_), channel_id=1, source_target_pairs={{0,46},{1,47},{2,0},{3,1},{4,2},{5,3},{6,4},{7,5},{8,6},{9,7},{10,... | collective-permute-start | bytes 811016 | tf_op jit(solution)/shard_map/ppermute | solution.py:185
  69.9 12.6 %collective-permute-start.17 = (bf16[528,256]{1,0:T(8,128)(2,1)S(1)}, bf16[528,256]{1,0:T(8,128)(2,1)S(1)}, u32[]{:S(2)}, u32[]{:S(2)}) collective-permute-start(bf16[528,256]{1,0:T(8,128)(2,1)S(1)} %collective-permute-done.13.refs_6_), channel_id=1, source_target_pairs={{16,18},{17,19},{18,20},{19,21},{20,22},{21,23},{22,24},{23,25},{2... | collective-permute-start | bytes 811016 | tf_op jit(solution)/shard_map/ppermute | solution.py:185
  89.1 3.6 %collective-permute-start.19 = (bf16[128,2048]{1,0:T(8,128)(2,1)S(1)}, bf16[128,2048]{1,0:T(8,128)(2,1)S(1)}, u32[]{:S(2)}, u32[]{:S(2)}) collective-permute-start(bf16[128,2048]{1,0:T(8,128)(2,1)S(1)} %get-tuple-element.36), channel_id=1, source_target_pairs={{0,1},{1,0},{2,3},{3,2},{4,5},{5,4},{6,7},{7,6},{8,9},{9,8},{10,11... | collective-permute-start | bytes 1572872 | tf_op jit(solution)/shard_map/ppermute | solution.py:185

commit v9 on v1

--- a/solution.py
+++ b/solution.py
@@ -216,10 +216,10 @@
     mup, mdown = [mid0], [mid0]
     for s in range(4):
         up.append(send(up[-1], NEAR_UP))
-        mup.append(send(mup[-1], MID_UP))
+        mdown.append(send(mdown[-1], MID_DOWN))
         if s < 3:
             down.append(send(down[-1], NEAR_DOWN))
-            mdown.append(send(mdown[-1], MID_DOWN))
+            mup.append(send(mup[-1], MID_UP))
 
     q_other = send(take(query_rows, 1 - core, HALF), SWAP)
     gate_other = send(take(gate_rows, 1 - core, HALF), SWAP)
@@ -250,7 +250,7 @@
             (down[3], down_id(3)),
             (mup[3], mid_id(-3)),
             (mdown[3], mid_id(3)),
-            (mup[4], mid_id(-4)),
+            (mdown[4], mid_id(4)),
         ],
     ]
     ids = jnp.stack([i for group in groups for _, i in group])

time: 92.1 us -> 89.7 us (0.974)
  starting transfers between devices: 59.5 us -> 57.1 us
    ppermute x20, starting transfers between devices: 59.5 us -> 57.1 us  [send(): return lax.ppermute(value, 'cp', pairs)]
where the time goes in v9:
time: 89.7 us; the launch traced here: 89.2 us
  starting transfers between devices  57.1 us (64%)
  Pallas kernels  20.7 us (23%)
  local copies, waits for them, and re-layouts  4.46 us (5%)
  waiting for transfers between devices  3.38 us (4%)
  other arithmetic  2.92 us (3%)
    ppermute x20, starting transfers between devices, send(): return lax.ppermute(value, 'cp', pairs)  57.1 us
    pallas_call x5, Pallas kernels, attend_call(): pl.pallas_call(functools.partial(attend, own_at, last, count), out_shape=...  20.7 us
    ppermute x20, waiting for transfers between devices, send(): return lax.ppermute(value, 'cp', pairs)  3.38 us
    dynamic_slice x2, local copies, waits for them, and re-layouts, take(): return lax.dynamic_slice_in_dim(rows, which * width, width, 1)  3.25 us
  transfers between devices with their start and end apart: 20, of which 3 were waited for; matrix products, arithmetic and copies ran while one was open for 4% of the time, Pallas kernels for 16%

profile of v9, /device:TPU:15, one launch (start us, length us, event | category | flops | bytes accessed | tf_op | source)
XLA Modules:
  0.0 89.2 jit_solution(9447287372194027431)
XLA Ops:
  0.0 2.4 %constant_dynamic-slice_fusion.2 = (bf16[128,2048]{1,0:T(8,128)(2,1)}, bf16[128,2048]{1,0:T(8,128)(2,1)}) fusion(bf16[128,4096]{1,0:T(8,128)(2,1)} %param.6, s32[]{:T(128)S(6)} %select_n.146, s32[]{:T(128)S(6)} %select_n.147), kind=kLoop, calls=%fused_computation.23 | loop fusion | bytes 2097160 | tf_op jit(solution)/shard_map/dynamic_slice | solution.py:188
  2.4 0.7 collective-permute-start.1
  3.3 0.1 collective-permute-start
  3.5 0.1 stack.83
  3.6 0.9 constant_dynamic-slice_fusion
  4.5 0.1 pad_add_fusion
  4.6 0.1 add_select_fusion
  4.6 0.2 collective-permute-done
  4.9 1.3 %collective-permute-start.10 = (bf16[528,256]{1,0:T(8,128)(2,1)S(1)}, bf16[528,256]{1,0:T(8,128)(2,1)S(1)}, u32[]{:S(2)}, u32[]{:S(2)}) collective-permute-start(bf16[528,256]{1,0:T(8,128)(2,1)S(1)} %slice_dynamic-update-slice_fusion.refs_4_), channel_id=1, source_target_pairs={{0,16},{1,17},{2,18},{3,19},{4,20},{5,21},{6,22},{7,23},{8,24},{9,... | collective-permute-start | bytes 811016 | tf_op jit(solution)/shard_map/ppermute | solution.py:185
  6.2 0.1 iota_compare_fusion
  6.3 3.5 %collective-permute-start.2 = (bf16[528,256]{1,0:T(8,128)(2,1)S(1)}, bf16[528,256]{1,0:T(8,128)(2,1)S(1)}, u32[]{:S(2)}, u32[]{:S(2)}) collective-permute-start(bf16[528,256]{1,0:T(8,128)(2,1)S(1)} %slice_dynamic-update-slice_fusion.refs_4_), channel_id=1, source_target_pairs={{0,2},{1,3},{2,4},{3,5},{4,6},{5,7},{6,8},{7,9},{8,10},{9,11},{10,... | collective-permute-start | bytes 811016 | tf_op jit(solution)/shard_map/ppermute | solution.py:185
  9.9 3.1 %collective-permute-start.6 = (bf16[528,256]{1,0:T(8,128)(2,1)S(1)}, bf16[528,256]{1,0:T(8,128)(2,1)S(1)}, u32[]{:S(2)}, u32[]{:S(2)}) collective-permute-start(bf16[528,256]{1,0:T(8,128)(2,1)S(1)} %slice_dynamic-update-slice_fusion.refs_4_), channel_id=1, source_target_pairs={{0,32},{1,33},{2,34},{3,35},{4,36},{5,37},{6,38},{7,39},{8,40},{9,... | collective-permute-start | bytes 811016 | tf_op jit(solution)/shard_map/ppermute | solution.py:185
  12.9 1.6 %collective-permute-done.10.refs_6_ = bf16[528,256]{1,0:T(8,128)(2,1)S(1)} collective-permute-done((bf16[528,256]{1,0:T(8,128)(2,1)S(1)}, bf16[528,256]{1,0:T(8,128)(2,1)S(1)}, u32[]{:S(2)}, u32[]{:S(2)}) %collective-permute-start.10) | collective-permute-done | bytes 270368 | tf_op jit(solution)/shard_map/ppermute | solution.py:185
  14.5 7.5 %collective-permute-start.14 = (bf16[528,256]{1,0:T(8,128)(2,1)S(1)}, bf16[528,256]{1,0:T(8,128)(2,1)S(1)}, u32[]{:S(2)}, u32[]{:S(2)}) collective-permute-start(bf16[528,256]{1,0:T(8,128)(2,1)S(1)} %collective-permute-done.10.refs_6_), channel_id=1, source_target_pairs={{16,30},{17,31},{18,16},{19,17},{20,18},{21,19},{22,20},{23,21},{2... | collective-permute-start | bytes 811016 | tf_op jit(solution)/shard_map/ppermute | solution.py:185
  22.0 1.9 %collective-permute-start.11 = (bf16[528,256]{1,0:T(8,128)(2,1)S(1)}, bf16[528,256]{1,0:T(8,128)(2,1)S(1)}, u32[]{:S(2)}, u32[]{:S(2)}) collective-permute-start(bf16[528,256]{1,0:T(8,128)(2,1)S(1)} %collective-permute-done.10.refs_6_), channel_id=1, source_target_pairs={{16,18},{17,19},{18,20},{19,21},{20,22},{21,23},{22,24},{23,25},{2... | collective-permute-start | bytes 811016 | tf_op jit(solution)/shard_map/ppermute | solution.py:185
  23.9 1.9 %collective-permute-start.3 = (bf16[528,256]{1,0:T(8,128)(2,1)S(1)}, bf16[528,256]{1,0:T(8,128)(2,1)S(1)}, u32[]{:S(2)}, u32[]{:S(2)}) collective-permute-start(bf16[528,256]{1,0:T(8,128)(2,1)S(1)} %collective-permute-done.2.refs_4_), channel_id=1, source_target_pairs={{0,2},{1,3},{2,4},{3,5},{4,6},{5,7},{6,8},{7,9},{8,10},{9,11},{10,... | collective-permute-start | bytes 811016 | tf_op jit(solution)/shard_map/ppermute | solution.py:185
  25.9 5.1 %collective-permute-start.7 = (bf16[528,256]{1,0:T(8,128)(2,1)S(1)}, bf16[528,256]{1,0:T(8,128)(2,1)S(1)}, u32[]{:S(2)}, u32[]{:S(2)}) collective-permute-start(bf16[528,256]{1,0:T(8,128)(2,1)S(1)} %collective-permute-done.6.refs_5_), channel_id=1, source_target_pairs={{0,46},{1,47},{2,0},{3,1},{4,2},{5,3},{6,4},{7,5},{8,6},{9,7},{10,... | collective-permute-start | bytes 811016 | tf_op jit(solution)/shard_map/ppermute | solution.py:185
  31.0 1.9 %collective-permute-start.15 = (bf16[528,256]{1,0:T(8,128)(2,1)S(1)}, bf16[528,256]{1,0:T(8,128)(2,1)S(1)}, u32[]{:S(2)}, u32[]{:S(2)}) collective-permute-start(bf16[528,256]{1,0:T(8,128)(2,1)S(1)} %collective-permute-done.14.refs_7_), channel_id=1, source_target_pairs={{16,30},{17,31},{18,16},{19,17},{20,18},{21,19},{22,20},{23,21},{2... | collective-permute-start | bytes 811016 | tf_op jit(solution)/shard_map/ppermute | solution.py:185
  32.9 0.1 select_reduce_fusion
  33.1 0.1 slice.67.refs_0_
  33.2 0.1 copy.29
  33.3 0.1 copy.30.refs_0_
  33.4 0.1 copy.28
  33.5 0.1 copy.31.refs_0_
  33.6 0.1 copy.27
  33.7 0.1 copy.32.refs_0_
  33.8 0.1 copy.25
  33.9 0.1 copy.33.refs_0_
  34.0 2.9 %collective-permute-start.18 = (bf16[128,2048]{1,0:T(8,128)(2,1)}, bf16[128,2048]{1,0:T(8,128)(2,1)S(1)}, u32[]{:S(2)}, u32[]{:S(2)}) collective-permute-start(bf16[128,2048]{1,0:T(8,128)(2,1)} %constant_dynamic-slice_fusion), channel_id=1, source_target_pairs={{0,1},{1,0},{2,3},{3,2},{4,5},{5,4},{6,7},{7,6},{8,9},{9,8},{10,11... | collective-permute-start | bytes 1572872 | tf_op jit(solution)/shard_map/ppermute | solution.py:185
  36.9 3.6 %collective-permute-start.12 = (bf16[528,256]{1,0:T(8,128)(2,1)S(1)}, bf16[528,256]{1,0:T(8,128)(2,1)S(1)}, u32[]{:S(2)}, u32[]{:S(2)}) collective-permute-start(bf16[528,256]{1,0:T(8,128)(2,1)S(1)} %collective-permute-done.11.refs_6_), channel_id=1, source_target_pairs={{16,18},{17,19},{18,20},{19,21},{20,22},{21,23},{22,24},{23,25},{2... | collective-permute-start | bytes 811016 | tf_op jit(solution)/shard_map/ppermute | solution.py:185
  40.5 1.9 %collective-permute-start.4 = (bf16[528,256]{1,0:T(8,128)(2,1)S(1)}, bf16[528,256]{1,0:T(8,128)(2,1)S(1)}, u32[]{:S(2)}, u32[]{:S(2)}) collective-permute-start(bf16[528,256]{1,0:T(8,128)(2,1)S(1)} %collective-permute-done.3.refs_4_), channel_id=1, source_target_pairs={{0,2},{1,3},{2,4},{3,5},{4,6},{5,7},{6,8},{7,9},{8,10},{9,11},{10,... | collective-permute-start | bytes 811016 | tf_op jit(solution)/shard_map/ppermute | solution.py:185
  42.5 5.1 %collective-permute-start.8 = (bf16[528,256]{1,0:T(8,128)(2,1)S(1)}, bf16[528,256]{1,0:T(8,128)(2,1)S(1)}, u32[]{:S(2)}, u32[]{:S(2)}) collective-permute-start(bf16[528,256]{1,0:T(8,128)(2,1)S(1)} %collective-permute-done.7.refs_5_), channel_id=1, source_target_pairs={{0,46},{1,47},{2,0},{3,1},{4,2},{5,3},{6,4},{7,5},{8,6},{9,7},{10,... | collective-permute-start | bytes 811016 | tf_op jit(solution)/shard_map/ppermute | solution.py:185
  47.6 1.9 %collective-permute-start.16 = (bf16[528,256]{1,0:T(8,128)(2,1)S(1)}, bf16[528,256]{1,0:T(8,128)(2,1)S(1)}, u32[]{:S(2)}, u32[]{:S(2)}) collective-permute-start(bf16[528,256]{1,0:T(8,128)(2,1)S(1)} %collective-permute-done.15.refs_7_), channel_id=1, source_target_pairs={{16,30},{17,31},{18,16},{19,17},{20,18},{21,19},{22,20},{23,21},{2... | collective-permute-start | bytes 811016 | tf_op jit(solution)/shard_map/ppermute | solution.py:185
  49.5 1.3 %pad_maximum_fusion = bf16[256,2048]{1,0:T(8,128)(2,1)S(1)} fusion(bf16[128,2048]{1,0:T(8,128)(2,1)} %collective-permute-done.1, bf16[128,2048]{1,0:T(8,128)(2,1)} %get-tuple-element.33), kind=kLoop, calls=%fused_computation.1 | loop fusion | flops 2097152 | bytes 2097152 | tf_op jit(solution)/shard_map/concatenate | solution.py:226
  50.8 0.1 copy.36
  50.9 0.1 broadcast_in_dim.56.refs_3_
  51.0 1.7 %shard_map.64 = (f32[8,256,128]{2,1,0:T(8,128)S(1)}, f32[8,256,128]{2,1,0:T(8,128)S(1)}, f32[8,256,256]{2,1,0:T(8,128)S(1)}) custom-call(s32[1,4]{1,0:T(1,128)S(1)} %slice.67.refs_0_, s32[1]{0:T(128)} %bitcast.17.refs_1_, bf16[2048,256]{1,0:T(8,128)(2,1)S(1)} %bitcast.33, f32[256,128]{1,0:T(8,128)S(1)} %broadcast_in_dim.56.refs_3_, ...), custom_call_target="tpu_custom_call" | custom-call | flops 536870912 | bytes 9270000 | tf_op jit(solution)/shard_map/pallas_call | solution.py:163
  52.7 3.6 %shard_map.65 = (f32[8,256,128]{2,1,0:T(8,128)S(1)}, f32[8,256,128]{2,1,0:T(8,128)S(1)}, f32[8,256,256]{2,1,0:T(8,128)S(1)}) custom-call(s32[3,4]{1,0:T(4,128)S(1)} %copy.30.refs_0_, s32[1]{0:T(128)} %bitcast.17.refs_1_, bf16[2048,256]{1,0:T(8,128)(2,1)S(1)} %bitcast.34, ...), custom_call_target="tpu_custom_call", output_to_operand_aliasing={{0}: (7, {}), {1}: (8, {}), {2}: (9, {})} | custom-call | flops 1610612736 | bytes 9810000 | tf_op jit(solution)/shard_map/pallas_call | solution.py:163
  56.4 3.4 %collective-permute-start.13 = (bf16[528,256]{1,0:T(8,128)(2,1)S(1)}, bf16[528,256]{1,0:T(8,128)(2,1)S(1)}, u32[]{:S(2)}, u32[]{:S(2)}) collective-permute-start(bf16[528,256]{1,0:T(8,128)(2,1)S(1)} %collective-permute-done.12.refs_6_), channel_id=1, source_target_pairs={{16,18},{17,19},{18,20},{19,21},{20,22},{21,23},{22,24},{23,25},{2... | collective-permute-start | bytes 811016 | tf_op jit(solution)/shard_map/ppermute | solution.py:185
  59.8 1.9 %collective-permute-start.5 = (bf16[528,256]{1,0:T(8,128)(2,1)S(1)}, bf16[528,256]{1,0:T(8,128)(2,1)S(1)}, u32[]{:S(2)}, u32[]{:S(2)}) collective-permute-start(bf16[528,256]{1,0:T(8,128)(2,1)S(1)} %collective-permute-done.4.refs_4_), channel_id=1, source_target_pairs={{0,2},{1,3},{2,4},{3,5},{4,6},{5,7},{6,8},{7,9},{8,10},{9,11},{10,... | collective-permute-start | bytes 811016 | tf_op jit(solution)/shard_map/ppermute | solution.py:185
  61.7 5.1 %collective-permute-start.9 = (bf16[528,256]{1,0:T(8,128)(2,1)S(1)}, bf16[528,256]{1,0:T(8,128)(2,1)S(1)}, u32[]{:S(2)}, u32[]{:S(2)}) collective-permute-start(bf16[528,256]{1,0:T(8,128)(2,1)S(1)} %collective-permute-done.8.refs_5_), channel_id=1, source_target_pairs={{0,46},{1,47},{2,0},{3,1},{4,2},{5,3},{6,4},{7,5},{8,6},{9,7},{10,... | collective-permute-start | bytes 811016 | tf_op jit(solution)/shard_map/ppermute | solution.py:185
  66.8 2.1 %collective-permute-start.17 = (bf16[528,256]{1,0:T(8,128)(2,1)S(1)}, bf16[528,256]{1,0:T(8,128)(2,1)S(1)}, u32[]{:S(2)}, u32[]{:S(2)}) collective-permute-start(bf16[528,256]{1,0:T(8,128)(2,1)S(1)} %collective-permute-done.16.refs_7_), channel_id=1, source_target_pairs={{16,30},{17,31},{18,16},{19,17},{20,18},{21,19},{22,20},{23,21},{2... | collective-permute-start | bytes 811016 | tf_op jit(solution)/shard_map/ppermute | solution.py:185
  68.9 4.6 %shard_map.66 = (f32[8,256,128]{2,1,0:T(8,128)S(1)}, f32[8,256,128]{2,1,0:T(8,128)S(1)}, f32[8,256,256]{2,1,0:T(8,128)S(1)}) custom-call(s32[4,4]{1,0:T(4,128)S(1)} %copy.31.refs_0_, s32[1]{0:T(128)} %bitcast.17.refs_1_, bf16[2048,256]{1,0:T(8,128)(2,1)S(1)} %bitcast.35, ...), custom_call_target="tpu_custom_call", output_to_operand_aliasing={{0}: (8, {}), {1}: (9, {}), {2}: (10, {})} | custom-call | flops 2147483648 | bytes 10080000 | tf_op jit(solution)/shard_map/pallas_call | solution.py:163
  73.5 4.6 %shard_map.67 = (f32[8,256,128]{2,1,0:T(8,128)S(1)}, f32[8,256,128]{2,1,0:T(8,128)S(1)}, f32[8,256,256]{2,1,0:T(8,128)S(1)}) custom-call(s32[4,4]{1,0:T(4,128)S(1)} %copy.32.refs_0_, s32[1]{0:T(128)} %bitcast.17.refs_1_, bf16[2048,256]{1,0:T(8,128)(2,1)S(1)} %bitcast.36, ...), custom_call_target="tpu_custom_call", output_to_operand_aliasing={{0}: (8, {}), {1}: (9, {}), {2}: (10, {})} | custom-call | flops 2147483648 | bytes 10080000 | tf_op jit(solution)/shard_map/pallas_call | solution.py:163
  78.2 6.1 %shard_map.68 = (bf16[128,2048]{1,0:T(8,128)(2,1)S(1)}, bf16[128,2048]{1,0:T(8,128)(2,1)S(1)}) custom-call(s32[5,4]{1,0:T(8,128)S(1)} %copy.33.refs_0_, s32[1]{0:T(128)} %bitcast.17.refs_1_, bf16[2048,256]{1,0:T(8,128)(2,1)S(1)} %bitcast.37, f32[256,128]{1,0:T(8,128)S(1)} %broadcast_in_dim.56.refs_3_, bf16[528,256]{1,0:T(8,128)(2,1)S(1)} %collective-permute-done.5.refs_4_, ...), custom_call_target="tpu_custom_call" | custom-call | flops 2684354560 | bytes 10350000 | tf_op jit(solution)/shard_map/pallas_call | solution.py:163
  84.4 2.1 %collective-permute-start.19 = (bf16[128,2048]{1,0:T(8,128)(2,1)S(1)}, bf16[128,2048]{1,0:T(8,128)(2,1)S(1)}, u32[]{:S(2)}, u32[]{:S(2)}) collective-permute-start(bf16[128,2048]{1,0:T(8,128)(2,1)S(1)} %get-tuple-element.32), channel_id=1, source_target_pairs={{0,1},{1,0},{2,3},{3,2},{4,5},{5,4},{6,7},{7,6},{8,9},{9,8},{10,11... | collective-permute-start | bytes 1572872 | tf_op jit(solution)/shard_map/ppermute | solution.py:185
  86.4 1.5 %collective-permute-done.19 = bf16[128,2048]{1,0:T(8,128)(2,1)S(1)} collective-permute-done((bf16[128,2048]{1,0:T(8,128)(2,1)S(1)}, bf16[128,2048]{1,0:T(8,128)(2,1)S(1)}, u32[]{:S(2)}, u32[]{:S(2)}) %collective-permute-start.19) | collective-permute-done | bytes 524320 | tf_op jit(solution)/shard_map/ppermute | solution.py:185
  88.0 1.2 %maximum_select_fusion = bf16[128,4096]{1,0:T(8,128)(2,1)} fusion(bf16[128,2048]{1,0:T(8,128)(2,1)S(1)} %collective-permute-done.19, bf16[128,2048]{1,0:T(8,128)(2,1)S(1)} %get-tuple-element.31, pred[]{:T(512)S(6)} %eq.21), kind=kLoop, calls=%fused_computation.2 | loop fusion | flops 4718592 | bytes 2097153 | tf_op jit(solution)/shard_map/jit(_where)/select_n | solution.py:275
  (50 shorter events, 0.2 us)
Async XLA Ops:
  0.0 3.1 %copy-start.3 = (s32[1,64]{1,0:T(1,128)S(1)}, s32[1,64]{1,0:T(1,128)}, u32[]{:S(2)}) copy-start(s32[1,64]{1,0:T(1,128)} %param.11) | copy-start | bytes 772
  0.0 3.1 %copy-start.4 = (s32[128]{0:T(128)S(1)}, s32[128]{0:T(128)}, u32[]{:S(2)}) copy-start(s32[128]{0:T(128)} %param.10) | copy-start | bytes 1540
  0.0 3.2 %copy-start.1 = (bf16[128,512]{1,0:T(8,128)(2,1)S(1)}, bf16[128,512]{1,0:T(8,128)(2,1)}, u32[]{:S(2)}) copy-start(bf16[128,512]{1,0:T(8,128)(2,1)} %param.7) | copy-start | bytes 393220
  0.0 3.2 %copy-start.2 = (bf16[128,512]{1,0:T(8,128)(2,1)S(1)}, bf16[128,512]{1,0:T(8,128)(2,1)}, u32[]{:S(2)}) copy-start(bf16[128,512]{1,0:T(8,128)(2,1)} %param.8) | copy-start | bytes 393220
  0.0 3.6 %copy-start = (bf16[128,4096]{1,0:T(8,128)(2,1)S(1)}, bf16[128,4096]{1,0:T(8,128)(2,1)}, u32[]{:S(2)}) copy-start(bf16[128,4096]{1,0:T(8,128)(2,1)} %refs_12_.1) | copy-start | bytes 3145732
  2.4 31.6 %collective-permute-start.1 = (bf16[128,2048]{1,0:T(8,128)(2,1)}, bf16[128,2048]{1,0:T(8,128)(2,1)}, u32[]{:S(2)}, u32[]{:S(2)}) collective-permute-start(bf16[128,2048]{1,0:T(8,128)(2,1)} %get-tuple-element.34), channel_id=1, source_target_pairs={{0,1},{1,0},{2,3},{3,2},{4,5},{5,4},{6,7},{7,6},{8,9},{9,8},{10,11... | collective-permute-start | bytes 1572872 | tf_op jit(solution)/shard_map/ppermute | solution.py:185
  3.3 1.6 %collective-permute-start = (bf16[272,256]{1,0:T(8,128)(2,1)S(1)}, bf16[272,256]{1,0:T(8,128)(2,1)S(1)}, u32[]{:S(2)}, u32[]{:S(2)}) collective-permute-start(bf16[272,256]{1,0:T(8,128)(2,1)S(1)} %pad_maximum_fusion.1), channel_id=1, source_target_pairs={{0,1},{1,0},{2,3},{3,2},{4,5},{5,4},{6,7},{7,6},{8,9},{9,8},{10,11... | collective-permute-start | bytes 417800 | tf_op jit(solution)/shard_map/ppermute | solution.py:185
  4.9 9.6 %collective-permute-start.10 = (bf16[528,256]{1,0:T(8,128)(2,1)S(1)}, bf16[528,256]{1,0:T(8,128)(2,1)S(1)}, u32[]{:S(2)}, u32[]{:S(2)}) collective-permute-start(bf16[528,256]{1,0:T(8,128)(2,1)S(1)} %slice_dynamic-update-slice_fusion.refs_4_), channel_id=1, source_target_pairs={{0,16},{1,17},{2,18},{3,19},{4,20},{5,21},{6,22},{7,23},{8,24},{9,... | collective-permute-start | bytes 811016 | tf_op jit(solution)/shard_map/ppermute | solution.py:185
  6.3 17.6 %collective-permute-start.2 = (bf16[528,256]{1,0:T(8,128)(2,1)S(1)}, bf16[528,256]{1,0:T(8,128)(2,1)S(1)}, u32[]{:S(2)}, u32[]{:S(2)}) collective-permute-start(bf16[528,256]{1,0:T(8,128)(2,1)S(1)} %slice_dynamic-update-slice_fusion.refs_4_), channel_id=1, source_target_pairs={{0,2},{1,3},{2,4},{3,5},{4,6},{5,7},{6,8},{7,9},{8,10},{9,11},{10,... | collective-permute-start | bytes 811016 | tf_op jit(solution)/shard_map/ppermute | solution.py:185
  9.9 16.0 %collective-permute-start.6 = (bf16[528,256]{1,0:T(8,128)(2,1)S(1)}, bf16[528,256]{1,0:T(8,128)(2,1)S(1)}, u32[]{:S(2)}, u32[]{:S(2)}) collective-permute-start(bf16[528,256]{1,0:T(8,128)(2,1)S(1)} %slice_dynamic-update-slice_fusion.refs_4_), channel_id=1, source_target_pairs={{0,32},{1,33},{2,34},{3,35},{4,36},{5,37},{6,38},{7,39},{8,40},{9,... | collective-permute-start | bytes 811016 | tf_op jit(solution)/shard_map/ppermute | solution.py:185
  14.5 16.5 %collective-permute-start.14 = (bf16[528,256]{1,0:T(8,128)(2,1)S(1)}, bf16[528,256]{1,0:T(8,128)(2,1)S(1)}, u32[]{:S(2)}, u32[]{:S(2)}) collective-permute-start(bf16[528,256]{1,0:T(8,128)(2,1)S(1)} %collective-permute-done.10.refs_6_), channel_id=1, source_target_pairs={{16,30},{17,31},{18,16},{19,17},{20,18},{21,19},{22,20},{23,21},{2... | collective-permute-start | bytes 811016 | tf_op jit(solution)/shard_map/ppermute | solution.py:185
  22.0 14.9 %collective-permute-start.11 = (bf16[528,256]{1,0:T(8,128)(2,1)S(1)}, bf16[528,256]{1,0:T(8,128)(2,1)S(1)}, u32[]{:S(2)}, u32[]{:S(2)}) collective-permute-start(bf16[528,256]{1,0:T(8,128)(2,1)S(1)} %collective-permute-done.10.refs_6_), channel_id=1, source_target_pairs={{16,18},{17,19},{18,20},{19,21},{20,22},{21,23},{22,24},{23,25},{2... | collective-permute-start | bytes 811016 | tf_op jit(solution)/shard_map/ppermute | solution.py:185
  23.9 16.6 %collective-permute-start.3 = (bf16[528,256]{1,0:T(8,128)(2,1)S(1)}, bf16[528,256]{1,0:T(8,128)(2,1)S(1)}, u32[]{:S(2)}, u32[]{:S(2)}) collective-permute-start(bf16[528,256]{1,0:T(8,128)(2,1)S(1)} %collective-permute-done.2.refs_4_), channel_id=1, source_target_pairs={{0,2},{1,3},{2,4},{3,5},{4,6},{5,7},{6,8},{7,9},{8,10},{9,11},{10,... | collective-permute-start | bytes 811016 | tf_op jit(solution)/shard_map/ppermute | solution.py:185
  25.9 16.6 %collective-permute-start.7 = (bf16[528,256]{1,0:T(8,128)(2,1)S(1)}, bf16[528,256]{1,0:T(8,128)(2,1)S(1)}, u32[]{:S(2)}, u32[]{:S(2)}) collective-permute-start(bf16[528,256]{1,0:T(8,128)(2,1)S(1)} %collective-permute-done.6.refs_5_), channel_id=1, source_target_pairs={{0,46},{1,47},{2,0},{3,1},{4,2},{5,3},{6,4},{7,5},{8,6},{9,7},{10,... | collective-permute-start | bytes 811016 | tf_op jit(solution)/shard_map/ppermute | solution.py:185
  31.0 16.6 %collective-permute-start.15 = (bf16[528,256]{1,0:T(8,128)(2,1)S(1)}, bf16[528,256]{1,0:T(8,128)(2,1)S(1)}, u32[]{:S(2)}, u32[]{:S(2)}) collective-permute-start(bf16[528,256]{1,0:T(8,128)(2,1)S(1)} %collective-permute-done.14.refs_7_), channel_id=1, source_target_pairs={{16,30},{17,31},{18,16},{19,17},{20,18},{21,19},{22,20},{23,21},{2... | collective-permute-start | bytes 811016 | tf_op jit(solution)/shard_map/ppermute | solution.py:185
  34.0 44.2 %collective-permute-start.18 = (bf16[128,2048]{1,0:T(8,128)(2,1)}, bf16[128,2048]{1,0:T(8,128)(2,1)S(1)}, u32[]{:S(2)}, u32[]{:S(2)}) collective-permute-start(bf16[128,2048]{1,0:T(8,128)(2,1)} %constant_dynamic-slice_fusion), channel_id=1, source_target_pairs={{0,1},{1,0},{2,3},{3,2},{4,5},{5,4},{6,7},{7,6},{8,9},{9,8},{10,11... | collective-permute-start | bytes 1572872 | tf_op jit(solution)/shard_map/ppermute | solution.py:185
  36.9 19.5 %collective-permute-start.12 = (bf16[528,256]{1,0:T(8,128)(2,1)S(1)}, bf16[528,256]{1,0:T(8,128)(2,1)S(1)}, u32[]{:S(2)}, u32[]{:S(2)}) collective-permute-start(bf16[528,256]{1,0:T(8,128)(2,1)S(1)} %collective-permute-done.11.refs_6_), channel_id=1, source_target_pairs={{16,18},{17,19},{18,20},{19,21},{20,22},{21,23},{22,24},{23,25},{2... | collective-permute-start | bytes 811016 | tf_op jit(solution)/shard_map/ppermute | solution.py:185
  40.5 19.2 %collective-permute-start.4 = (bf16[528,256]{1,0:T(8,128)(2,1)S(1)}, bf16[528,256]{1,0:T(8,128)(2,1)S(1)}, u32[]{:S(2)}, u32[]{:S(2)}) collective-permute-start(bf16[528,256]{1,0:T(8,128)(2,1)S(1)} %collective-permute-done.3.refs_4_), channel_id=1, source_target_pairs={{0,2},{1,3},{2,4},{3,5},{4,6},{5,7},{6,8},{7,9},{8,10},{9,11},{10,... | collective-permute-start | bytes 811016 | tf_op jit(solution)/shard_map/ppermute | solution.py:185
  42.5 19.2 %collective-permute-start.8 = (bf16[528,256]{1,0:T(8,128)(2,1)S(1)}, bf16[528,256]{1,0:T(8,128)(2,1)S(1)}, u32[]{:S(2)}, u32[]{:S(2)}) collective-permute-start(bf16[528,256]{1,0:T(8,128)(2,1)S(1)} %collective-permute-done.7.refs_5_), channel_id=1, source_target_pairs={{0,46},{1,47},{2,0},{3,1},{4,2},{5,3},{6,4},{7,5},{8,6},{9,7},{10,... | collective-permute-start | bytes 811016 | tf_op jit(solution)/shard_map/ppermute | solution.py:185
  47.6 19.2 %collective-permute-start.16 = (bf16[528,256]{1,0:T(8,128)(2,1)S(1)}, bf16[528,256]{1,0:T(8,128)(2,1)S(1)}, u32[]{:S(2)}, u32[]{:S(2)}) collective-permute-start(bf16[528,256]{1,0:T(8,128)(2,1)S(1)} %collective-permute-done.15.refs_7_), channel_id=1, source_target_pairs={{16,30},{17,31},{18,16},{19,17},{20,18},{21,19},{22,20},{23,21},{2... | collective-permute-start | bytes 811016 | tf_op jit(solution)/shard_map/ppermute | solution.py:185
  56.4 21.8 %collective-permute-start.13 = (bf16[528,256]{1,0:T(8,128)(2,1)S(1)}, bf16[528,256]{1,0:T(8,128)(2,1)S(1)}, u32[]{:S(2)}, u32[]{:S(2)}) collective-permute-start(bf16[528,256]{1,0:T(8,128)(2,1)S(1)} %collective-permute-done.12.refs_6_), channel_id=1, source_target_pairs={{16,18},{17,19},{18,20},{19,21},{20,22},{21,23},{22,24},{23,25},{2... | collective-permute-start | bytes 811016 | tf_op jit(solution)/shard_map/ppermute | solution.py:185
  59.8 18.4 %collective-permute-start.5 = (bf16[528,256]{1,0:T(8,128)(2,1)S(1)}, bf16[528,256]{1,0:T(8,128)(2,1)S(1)}, u32[]{:S(2)}, u32[]{:S(2)}) collective-permute-start(bf16[528,256]{1,0:T(8,128)(2,1)S(1)} %collective-permute-done.4.refs_4_), channel_id=1, source_target_pairs={{0,2},{1,3},{2,4},{3,5},{4,6},{5,7},{6,8},{7,9},{8,10},{9,11},{10,... | collective-permute-start | bytes 811016 | tf_op jit(solution)/shard_map/ppermute | solution.py:185
  61.7 16.5 %collective-permute-start.9 = (bf16[528,256]{1,0:T(8,128)(2,1)S(1)}, bf16[528,256]{1,0:T(8,128)(2,1)S(1)}, u32[]{:S(2)}, u32[]{:S(2)}) collective-permute-start(bf16[528,256]{1,0:T(8,128)(2,1)S(1)} %collective-permute-done.8.refs_5_), channel_id=1, source_target_pairs={{0,46},{1,47},{2,0},{3,1},{4,2},{5,3},{6,4},{7,5},{8,6},{9,7},{10,... | collective-permute-start | bytes 811016 | tf_op jit(solution)/shard_map/ppermute | solution.py:185
  66.8 11.4 %collective-permute-start.17 = (bf16[528,256]{1,0:T(8,128)(2,1)S(1)}, bf16[528,256]{1,0:T(8,128)(2,1)S(1)}, u32[]{:S(2)}, u32[]{:S(2)}) collective-permute-start(bf16[528,256]{1,0:T(8,128)(2,1)S(1)} %collective-permute-done.16.refs_7_), channel_id=1, source_target_pairs={{16,30},{17,31},{18,16},{19,17},{20,18},{21,19},{22,20},{23,21},{2... | collective-permute-start | bytes 811016 | tf_op jit(solution)/shard_map/ppermute | solution.py:185
  84.4 3.6 %collective-permute-start.19 = (bf16[128,2048]{1,0:T(8,128)(2,1)S(1)}, bf16[128,2048]{1,0:T(8,128)(2,1)S(1)}, u32[]{:S(2)}, u32[]{:S(2)}) collective-permute-start(bf16[128,2048]{1,0:T(8,128)(2,1)S(1)} %get-tuple-element.32), channel_id=1, source_target_pairs={{0,1},{1,0},{2,3},{3,2},{4,5},{5,4},{6,7},{7,6},{8,9},{9,8},{10,11... | collective-permute-start | bytes 1572872 | tf_op jit(solution)/shard_map/ppermute | solution.py:185
